TPU v7x, 256 devices: a whole 4x4x8 slice. The times are simulated.
256 devices in a mesh: dp: 16 (over z, core), expert: 16 (over y, x).
Axes of the slice: x: 4, y: 4, z: 8, core: 2. Of those that a mesh axis runs over, the one named last changes fastest.
Arguments:
- tokens: bfloat16 [65536, 1024], P(('dp', 'expert')), may hold values from -6 to 6
- cotangent: bfloat16 [65536, 1024], P(('dp', 'expert')), may hold values from -6 to 6
- route_logits: float32 [65536, 2], P(('dp', 'expert')), may hold values from -6 to 6
- expert_ids: int32 [65536, 2], P(('dp', 'expert')), may hold values from 0 to 31, as said below
- slot_pos: int32 [65536, 2], P(('dp', 'expert')), may hold values from 0 to 31, as said below
- w_in: bfloat16 [32, 1024, 1536], P('expert'), may hold values from -0.1875 to 0.1875
- w_down: bfloat16 [32, 768, 1024], P('expert'), may hold values from -0.21875 to 0.21875
Outputs:
- input_grad: bfloat16 [65536, 1024], P(('dp', 'expert'))
- grad_in: float32 [32, 1024, 1536], P('expert', 'dp')
- grad_down: float32 [32, 768, 1024], P('expert', 'dp')
Inputs may be any that keep to these rules, and one draw needn't show every extreme that they name: `expert_ids`: each row names 2 different experts. Within each aligned block of 256 rows (the tokens of one device) no expert is named more than 32 times, and one expert, the same in all blocks, is named exactly 32 times in every block. `slot_pos`: within each aligned block of 256 rows, entries whose matching expert_ids entries name the same expert are distinct.
All inputs are finite; a program needn't handle non-finite values.
Results may differ from a plain program's by a relative error of at most 0.02.
Values may be sent and summed in bfloat16 or wider, within the bound.
A program may use at most 128 MiB of HBM per device.

v0:
```python
import jax
import jax.numpy as jnp
from jax import lax
from jax.sharding import PartitionSpec as P

TOP = 2


def recompute(input_slots, w_in, hidden_width):
    gate_up = jnp.einsum("ksd,kdf->ksf", input_slots, w_in, preferred_element_type=jnp.float32)
    gate = gate_up[:, :, :hidden_width]
    upper = gate_up[:, :, hidden_width:]
    sigmoid_gate = jax.nn.sigmoid(gate)
    activated = gate * sigmoid_gate
    hidden = (activated * upper).astype(jnp.bfloat16)
    return (gate, upper, sigmoid_gate, activated, hidden)


def per_device(tokens, cotangent, route_logits, expert_ids, slot_pos, w_in, w_down):
    token_count, width = tokens.shape
    local_experts = w_in.shape[0]
    hidden_width = w_down.shape[1]
    experts_all = local_experts * lax.axis_size("expert")
    capacity = 2 * TOP * token_count // experts_all
    first = jax.nn.sigmoid(route_logits[:, 0] - route_logits[:, 1])
    combine = jnp.stack([first, 1.0 - first], axis=1)
    scaled = (combine[:, :, None] * cotangent[:, None, :].astype(jnp.float32)).astype(jnp.bfloat16)
    destination = (expert_ids * capacity + slot_pos).reshape(-1)
    repeated = jnp.broadcast_to(tokens[:, None, :], (token_count, TOP, width)).reshape(-1, width)
    empty = jnp.zeros((experts_all * capacity, width), jnp.bfloat16)
    send_inputs = empty.at[destination].set(repeated).reshape(experts_all, capacity, width)
    send_scaled = (
        empty.at[destination].set(scaled.reshape(-1, width)).reshape(experts_all, capacity, width)
    )
    input_slots, cotangent_slots = (
        lax.all_to_all(send_inputs, "expert", split_axis=0, concat_axis=1, tiled=True),
        lax.all_to_all(send_scaled, "expert", split_axis=0, concat_axis=1, tiled=True),
    )
    gate, upper, sigmoid_gate, activated, hidden = recompute(input_slots, w_in, hidden_width)
    grad_hidden = jnp.einsum(
        "ksd,kfd->ksf", cotangent_slots, w_down, preferred_element_type=jnp.float32
    )
    term_down = jnp.einsum(
        "ksf,ksd->kfd", hidden, cotangent_slots, preferred_element_type=jnp.float32
    )
    grad_gate = grad_hidden * upper * sigmoid_gate * (1.0 + gate * (1.0 - sigmoid_gate))
    grad_up = grad_hidden * activated
    grad_pair = jnp.concatenate([grad_gate, grad_up], axis=2).astype(jnp.bfloat16)
    term_in = jnp.einsum("ksd,ksf->kdf", input_slots, grad_pair, preferred_element_type=jnp.float32)
    returned = jnp.einsum(
        "ksf,kdf->ksd", grad_pair, w_in, preferred_element_type=jnp.float32
    ).astype(jnp.bfloat16)
    arrived = lax.all_to_all(returned, "expert", split_axis=1, concat_axis=0, tiled=True)
    rows = arrived.reshape(-1, width)[destination].reshape(token_count, TOP, width)
    input_grad = jnp.sum(rows.astype(jnp.float32), axis=1).astype(jnp.bfloat16)
    grad_in, grad_down = (
        lax.psum_scatter(
            term_in.astype(jnp.bfloat16), "dp", scatter_dimension=1, tiled=True
        ).astype(jnp.float32),
        lax.psum_scatter(
            term_down.astype(jnp.bfloat16), "dp", scatter_dimension=1, tiled=True
        ).astype(jnp.float32),
    )
    return (input_grad, grad_in, grad_down)


def solution(mesh):
    in_specs = (
        P(("dp", "expert"), None),
        P(("dp", "expert"), None),
        P(("dp", "expert"), None),
        P(("dp", "expert"), None),
        P(("dp", "expert"), None),
        P("expert", None, None),
        P("expert", None, None),
    )
    out_specs = (P(("dp", "expert"), None), P("expert", "dp", None), P("expert", "dp", None))
    return jax.shard_map(
        per_device, mesh=mesh, in_specs=in_specs, out_specs=out_specs, check_vma=False
    )
```

profile of v0, /device:TPU:4, one launch (start us, length us, event | category | flops | bytes accessed | tf_op | source)
XLA Modules:
  0.0 242.6 jit_solution(9430504251878565319)
XLA Ops:
  7.2 0.9 multiply_add_fusion
  8.3 2.6 %broadcast_in_dim.5 = bf16[256,2,1024]{2,1,0:T(2,128)(2,1)} broadcast(bf16[256,1024]{1,0:T(8,128)(2,1)} %param.7), dimensions={0,2} | broadcast | bytes 1572864 | tf_op jit(solution)/shard_map/broadcast_in_dim | solution.py:29
  10.9 2.2 reshape.87
  13.2 4.8 %scatter_custom_fusion.1 = bf16[1024,1024]{1,0:T(8,128)(2,1)} fusion(s32[512]{0:T(512)S(1)} %bitcast.31, bf16[512,1024]{1,0:T(8,128)(2,1)} %reshape.87, bf16[]{:T(256)} %constant.5.clone.1), kind=kCustom, calls=%fused_computation.16 | custom fusion | bytes 2097664 | tf_op jit(solution)/shard_map/scatter | solution.py:31
  18.0 7.4 %all-to-all-start.1 = ((bf16[32,32,1024]{2,1,0:T(8,128)(2,1)}), bf16[32,32,1024]{2,1,0:T(8,128)(2,1)}, u32[]{:S(2)}, u32[]{:S(2)}) async-start(bf16[32,32,1024]{2,1,0:T(8,128)(2,1)} %bitcast.25), calls=%async_computation.1 | async-start | bytes 4194304 | tf_op jit(solution)/shard_map/all_to_all | solution.py:36
  25.7 2.9 %mul.49 = f32[256,2,1024]{2,1,0:T(2,128)} broadcast(bf16[256,1024]{1,0:T(8,128)(2,1)} %param.8), dimensions={0,2} | broadcast | bytes 2621440 | tf_op jit(solution)/shard_map/mul | solution.py:27
  28.7 3.7 %mul.50 = f32[512,1024]{1,0:T(8,128)} reshape(f32[256,2,1024]{2,1,0:T(2,128)} %mul.49) | data formatting | bytes 4194304 | tf_op jit(solution)/shard_map/mul | solution.py:27
  32.4 5.3 %scatter_custom_fusion = bf16[1024,1024]{1,0:T(8,128)(2,1)} fusion(s32[512]{0:T(512)S(1)} %bitcast.32, f32[512,1024]{1,0:T(8,128)} %mul.50, f32[512]{0:T(512)S(1)} %mul.47, bf16[]{:T(256)} %constant.5.clone.1), kind=kCustom, calls=%fused_computation.14 | custom fusion | flops 1048576 | bytes 4196354 | tf_op jit(solution)/shard_map/scatter | solution.py:33
  37.7 15.5 %all-to-all-done.1 = bf16[32,32,1024]{2,1,0:T(8,128)(2,1)} async-done(((bf16[32,32,1024]{2,1,0:T(8,128)(2,1)}), bf16[32,32,1024]{2,1,0:T(8,128)(2,1)}, u32[]{:S(2)}, u32[]{:S(2)}) %all-to-all-start.1) | async-done | bytes 2097184 | tf_op jit(solution)/shard_map/all_to_all | solution.py:36
  53.2 8.3 %all-to-all-start = ((bf16[32,32,1024]{2,1,0:T(8,128)(2,1)}), bf16[32,32,1024]{2,1,0:T(8,128)(2,1)}, u32[]{:S(2)}, u32[]{:S(2)}) async-start(bf16[32,32,1024]{2,1,0:T(8,128)(2,1)} %bitcast.26), calls=%async_computation | async-start | bytes 4194304 | tf_op jit(solution)/shard_map/all_to_all | solution.py:37
  61.7 3.2 %copy.23 = bf16[2,16,32,1024]{3,2,1,0:T(8,128)(2,1)} copy(bf16[2,16,32,1024]{3,2,0,1:T(8,128)(2,1)} %bitcast.7) | data formatting | bytes 4194304 | tf_op jit(solution)/shard_map/all_to_all | solution.py:36
  64.9 22.0 %all-to-all-done = bf16[32,32,1024]{2,1,0:T(8,128)(2,1)} async-done(((bf16[32,32,1024]{2,1,0:T(8,128)(2,1)}), bf16[32,32,1024]{2,1,0:T(8,128)(2,1)}, u32[]{:S(2)}, u32[]{:S(2)}) %all-to-all-start) | async-done | bytes 2097184 | tf_op jit(solution)/shard_map/all_to_all | solution.py:37
  86.9 1.9 copy.22
  88.8 0.3 copy-done.1
  89.1 6.0 %fusion.12 = f32[2,512,1536]{2,1,0:T(8,128)S(1)} fusion(bf16[2,512,1024]{2,1,0:T(8,128)(2,1)S(1)} %bitcast.27, bf16[2,1024,1536]{2,1,0:T(8,128)(2,1)} %param.12), kind=kOutput, calls=%fused_computation.28 | convolution fusion | flops 3221225472 | bytes 14680064 | tf_op jit(solution)/shard_map/ksd,kdf->ksf/dot_general | solution.py:10
  95.1 2.7 %copy-done.5 = f32[2,512,1536]{2,1,0:T(8,128)} copy-done((f32[2,512,1536]{2,1,0:T(8,128)}, f32[2,512,1536]{2,1,0:T(8,128)S(1)}, u32[]{:S(2)}) %copy-start.5) | copy-done | bytes 6291480
  97.8 3.7 %convolution_convert_fusion.1 = bf16[2,768,1024]{2,1,0:T(8,128)(2,1)} fusion(bf16[2,512,1024]{2,1,0:T(8,128)(2,1)S(1)} %bitcast.29, f32[2,512,1536]{2,1,0:T(8,128)S(1)} %fusion.12), kind=kOutput, calls=%fused_computation.10 | convolution fusion | flops 1616904192 | bytes 11534336 | tf_op jit(solution)/shard_map/ksf,ksd->kfd/dot_general | solution.py:43
  101.5 5.9 %multiply_convert_fusion.2 = (bf16[2,512,768]{2,1,0:T(8,128)(2,1)S(1)}, bf16[2,512,768]{2,1,0:T(8,128)(2,1)S(1)}) fusion(f32[2,512,1536]{2,1,0:T(8,128)} %copy-done.5, bf16[2,512,1024]{2,1,0:T(8,128)(2,1)} %bitcast.30, bf16[2,768,1024]{2,1,0:T(8,128)(2,1)S(1)} %copy-done), kind=kOutput, calls=%fused_computation.7 | convolution fusion | flops 1620836352 | bytes 14680064 | tf_op jit(solution)/shard_map/ksd,kfd->ksf/dot_general | solution.py:40
  107.4 1.2 copy-done.6
  108.7 0.4 copy-done.7
  109.1 5.5 %convolution_convert_fusion = bf16[2,1024,1536]{2,1,0:T(8,128)(2,1)} fusion(bf16[2,512,1024]{2,1,0:T(8,128)(2,1)S(1)} %bitcast.28, bf16[2,512,768]{2,1,0:T(8,128)(2,1)S(1)} %get-tuple-element.6, bf16[2,512,768]{2,1,0:T(8,128)(2,1)S(1)} %get-tuple-element.5), kind=kOutput, calls=%fused_computation.3 | convolution fusion | flops 3230662656 | bytes 11534336 | tf_op jit(solution)/shard_map/ksd,ksf->kdf/dot_general | solution.py:49
  114.6 7.3 %fusion.2 = bf16[2,512,1024]{2,1,0:T(8,128)(2,1)S(1)} fusion(bf16[2,1024,1536]{2,1,0:T(8,128)(2,1)} %param.12, bf16[2,512,768]{2,1,0:T(8,128)(2,1)} %copy-done.7, bf16[2,512,768]{2,1,0:T(8,128)(2,1)} %copy-done.6), kind=kOutput, calls=%fused_computation.13 | convolution fusion | flops 3228565504 | bytes 11534336 | tf_op jit(solution)/shard_map/ksf,kdf->ksd/dot_general | solution.py:50
  121.9 3.5 %copy.24 = bf16[2,512,1024]{2,0,1:T(2,128)(2,1)} copy(bf16[2,512,1024]{2,1,0:T(8,128)(2,1)S(1)} %fusion.2) | data formatting | bytes 4194304 | tf_op jit(solution)/shard_map/convert_element_type | solution.py:52
  125.4 8.3 %all-to-all-start.2 = ((bf16[2,512,1024]{2,0,1:T(2,128)(2,1)}), bf16[2,512,1024]{2,0,1:T(2,128)(2,1)}, u32[]{:S(2)}, u32[]{:S(2)}) async-start(bf16[2,512,1024]{2,0,1:T(2,128)(2,1)} %copy.24), calls=%async_computation.2 | async-start | bytes 4194304 | tf_op jit(solution)/shard_map/all_to_all | solution.py:53
  133.7 25.5 %all-to-all-done.2 = bf16[2,512,1024]{2,0,1:T(2,128)(2,1)} async-done(((bf16[2,512,1024]{2,0,1:T(2,128)(2,1)}), bf16[2,512,1024]{2,0,1:T(2,128)(2,1)}, u32[]{:S(2)}, u32[]{:S(2)}) %all-to-all-start.2) | async-done | bytes 2097184 | tf_op jit(solution)/shard_map/all_to_all | solution.py:53
  159.2 3.6 %copy.25 = bf16[2,16,32,1024]{3,2,0,1:T(8,128)(2,1)} copy(bf16[2,16,32,1024]{3,0,2,1:T(2,128)(2,1)} %bitcast.9) | data formatting | bytes 4194304 | tf_op jit(solution)/shard_map/all_to_all | solution.py:53
  162.9 5.3 %gather_fusion = bf16[512,1024]{1,0:T(8,128)(2,1)} fusion(bf16[1024,1024]{1,0:T(8,128)(2,1)} %bitcast.24, s32[1024]{0:T(1024)S(1)} %pad_clamp_fusion), kind=kCustom, calls=%fused_computation | custom fusion | bytes 2099200 | tf_op jit(solution)/shard_map/gather | solution.py:54
  168.2 2.3 reshape.66
  170.5 4.6 %reduce_sum.12 = bf16[256,1024]{1,0:T(8,128)(2,1)} reduce(bf16[256,2,1024]{2,1,0:T(2,128)(2,1)} %reshape.66, bf16[]{:T(256)} %constant.5.clone.1), dimensions={1}, to_apply=%region_2.0 | reduce | flops 262144 | bytes 1572866 | tf_op jit(solution)/shard_map/reduce_sum | solution.py:55
  175.1 1.7 convert_element_type.36
  176.8 57.0 %reduce-scatter.3.cloned.1.call-done = bf16[2,64,1536]{2,1,0:T(8,128)(2,1)} async-done(((bf16[2,1024,1536]{2,1,0:T(8,128)(2,1)}), bf16[2,64,1536]{2,1,0:T(8,128)(2,1)}) %reduce-scatter.3.cloned.1.call-update) | async-done | bytes 393232 | tf_op jit(solution)/shard_map/reduce_scatter | solution.py:57
  233.8 2.0 convert_element_type.33
  (25 shorter events, 0.9 us)
Async XLA Ops:
  7.2 94.3 %copy-start = (bf16[2,768,1024]{2,1,0:T(8,128)(2,1)S(1)}, bf16[2,768,1024]{2,1,0:T(8,128)(2,1)}, u32[]{:S(2)}) copy-start(bf16[2,768,1024]{2,1,0:T(8,128)(2,1)} %param.13) | copy-start | bytes 9437188
  13.2 12.2 %copy-start.4 = (f32[256,2]{0,1:T(2,128)S(1)}, f32[256,2]{0,1:T(2,128)}, u32[]{:S(2)}) copy-start(f32[256,2]{0,1:T(2,128)} %param.9) | copy-start | bytes 6148
  18.0 35.2 %all-to-all-start.1 = ((bf16[32,32,1024]{2,1,0:T(8,128)(2,1)}), bf16[32,32,1024]{2,1,0:T(8,128)(2,1)}, u32[]{:S(2)}, u32[]{:S(2)}) async-start(bf16[32,32,1024]{2,1,0:T(8,128)(2,1)} %bitcast.25), calls=%async_computation.1 | async-start | bytes 4194304 | tf_op jit(solution)/shard_map/all_to_all | solution.py:36
  53.2 33.7 %all-to-all-start = ((bf16[32,32,1024]{2,1,0:T(8,128)(2,1)}), bf16[32,32,1024]{2,1,0:T(8,128)(2,1)}, u32[]{:S(2)}, u32[]{:S(2)}) async-start(bf16[32,32,1024]{2,1,0:T(8,128)(2,1)} %bitcast.26), calls=%async_computation | async-start | bytes 4194304 | tf_op jit(solution)/shard_map/all_to_all | solution.py:37
  61.4 113.6 %reduce-scatter.5.cloned.1.call-start = ((), (), s32[]{:S(2)}) async-start(), calls=%async_computation.6 | async-start | bytes 3342336 | tf_op jit(solution)/shard_map/reduce_scatter | solution.py:60
  86.9 2.2 copy-start.1
  88.8 6.3 %copy-start.3 = (bf16[2,16,32,1024]{3,2,1,0:T(8,128)(2,1)}, bf16[2,16,32,1024]{3,2,1,0:T(8,128)(2,1)S(1)}, u32[]{:S(2)}) copy-start(bf16[2,16,32,1024]{3,2,1,0:T(8,128)(2,1)S(1)} %copy.22) | copy-start | bytes 6291460
  95.1 2.7 %copy-start.5 = (f32[2,512,1536]{2,1,0:T(8,128)}, f32[2,512,1536]{2,1,0:T(8,128)S(1)}, u32[]{:S(2)}) copy-start(f32[2,512,1536]{2,1,0:T(8,128)S(1)} %fusion.12) | copy-start | bytes 18874372
  101.5 132.3 %reduce-scatter.3.cloned.1.call-start = ((), (), s32[]{:S(2)}) async-start(), calls=%async_computation.5 | async-start | bytes 6684672 | tf_op jit(solution)/shard_map/reduce_scatter | solution.py:57
  101.5 7.6 %copy-start.2 = (bf16[2,16,32,1024]{3,2,1,0:T(8,128)(2,1)S(1)}, bf16[2,16,32,1024]{3,2,1,0:T(8,128)(2,1)}, u32[]{:S(2)}) copy-start(bf16[2,16,32,1024]{3,2,1,0:T(8,128)(2,1)} %copy.23) | copy-start | bytes 6291460
  107.4 1.2 copy-start.6
  107.4 1.6 copy-start.7
  125.4 33.8 %all-to-all-start.2 = ((bf16[2,512,1024]{2,0,1:T(2,128)(2,1)}), bf16[2,512,1024]{2,0,1:T(2,128)(2,1)}, u32[]{:S(2)}, u32[]{:S(2)}) async-start(bf16[2,512,1024]{2,0,1:T(2,128)(2,1)} %copy.24), calls=%async_computation.2 | async-start | bytes 4194304 | tf_op jit(solution)/shard_map/all_to_all | solution.py:53
Sparse Core Ops, SparseCore 0:
  101.6 64.6 reduce-scatter.4
  168.8 64.9 reduce-scatter.2
where the time goes:
time: 243 us
  waiting for transfers between devices  120 us (49%)
  local copies, waits for them, and re-layouts  41.4 us (17%)
  matrix products  28.3 us (12%)
  starting transfers between devices  24.3 us (10%)
  other arithmetic  14.4 us (6%)
  between operations  14.2 us (6%)
    reduce_scatter x1, waiting for transfers between devices, per_device(): lax.psum_scatter(term_in.astype(jnp.bfloat16), 'dp', scatter_dimension=1,...  57 us
    all_to_all x1, waiting for transfers between devices, per_device(): lax.all_to_all(returned, 'expert', split_axis=1, concat_axis=0, tiled=True)  25.5 us
    all_to_all x1, waiting for transfers between devices, per_device(): lax.all_to_all(send_scaled, 'expert', split_axis=0, concat_axis=1, tiled=...  22 us
    all_to_all x1, waiting for transfers between devices, per_device(): lax.all_to_all(send_inputs, 'expert', split_axis=0, concat_axis=1, tiled=...  15.5 us
    all_to_all x1, starting transfers between devices, per_device(): lax.all_to_all(returned, 'expert', split_axis=1, concat_axis=0, tiled=True)  8.3 us
    all_to_all x1, starting transfers between devices, per_device(): lax.all_to_all(send_scaled, 'expert', split_axis=0, concat_axis=1, tiled=...  8.25 us
    all_to_all x1, starting transfers between devices, per_device(): lax.all_to_all(send_inputs, 'expert', split_axis=0, concat_axis=1, tiled=...  7.45 us
    dot_general x1, matrix products, per_device(): jnp.einsum('ksf,kdf->ksd', grad_pair, w_in, preferred_element_type=jnp.fl...  7.32 us
  transfers between devices with their start and end apart: 5, of which 4 were waited for; matrix products, arithmetic and copies ran while one was open for 23% of the time, Pallas kernels for 0%

commit v1 on v0

--- a/solution.py
+++ b/solution.py
@@ -20,22 +20,24 @@
     token_count, width = tokens.shape
     local_experts = w_in.shape[0]
     hidden_width = w_down.shape[1]
-    experts_all = local_experts * lax.axis_size("expert")
+    n_expert = lax.axis_size("expert")
+    n_dp = lax.axis_size("dp")
+    experts_all = local_experts * n_expert
     capacity = 2 * TOP * token_count // experts_all
     first = jax.nn.sigmoid(route_logits[:, 0] - route_logits[:, 1])
     combine = jnp.stack([first, 1.0 - first], axis=1)
     scaled = (combine[:, :, None] * cotangent[:, None, :].astype(jnp.float32)).astype(jnp.bfloat16)
     destination = (expert_ids * capacity + slot_pos).reshape(-1)
+    dest_in = (expert_ids * (2 * capacity) + slot_pos).reshape(-1)
+    dest_all = jnp.concatenate([dest_in, dest_in + capacity])
     repeated = jnp.broadcast_to(tokens[:, None, :], (token_count, TOP, width)).reshape(-1, width)
-    empty = jnp.zeros((experts_all * capacity, width), jnp.bfloat16)
-    send_inputs = empty.at[destination].set(repeated).reshape(experts_all, capacity, width)
-    send_scaled = (
-        empty.at[destination].set(scaled.reshape(-1, width)).reshape(experts_all, capacity, width)
-    )
-    input_slots, cotangent_slots = (
-        lax.all_to_all(send_inputs, "expert", split_axis=0, concat_axis=1, tiled=True),
-        lax.all_to_all(send_scaled, "expert", split_axis=0, concat_axis=1, tiled=True),
-    )
+    rows_all = jnp.concatenate([repeated, scaled.reshape(-1, width)], axis=0)
+    empty = jnp.zeros((experts_all * 2 * capacity, width), jnp.bfloat16)
+    send = empty.at[dest_all].set(rows_all).reshape(experts_all, 2, capacity, width)
+    got = lax.all_to_all(send, "expert", split_axis=0, concat_axis=0, tiled=True)
+    got = got.reshape(n_expert, local_experts, 2, capacity, width)
+    got = jnp.transpose(got, (2, 1, 0, 3, 4)).reshape(2, local_experts, n_expert * capacity, width)
+    input_slots, cotangent_slots = got[0], got[1]
     gate, upper, sigmoid_gate, activated, hidden = recompute(input_slots, w_in, hidden_width)
     grad_hidden = jnp.einsum(
         "ksd,kfd->ksf", cotangent_slots, w_down, preferred_element_type=jnp.float32
@@ -53,14 +55,16 @@
     arrived = lax.all_to_all(returned, "expert", split_axis=1, concat_axis=0, tiled=True)
     rows = arrived.reshape(-1, width)[destination].reshape(token_count, TOP, width)
     input_grad = jnp.sum(rows.astype(jnp.float32), axis=1).astype(jnp.bfloat16)
-    grad_in, grad_down = (
-        lax.psum_scatter(
-            term_in.astype(jnp.bfloat16), "dp", scatter_dimension=1, tiled=True
-        ).astype(jnp.float32),
-        lax.psum_scatter(
-            term_down.astype(jnp.bfloat16), "dp", scatter_dimension=1, tiled=True
-        ).astype(jnp.float32),
-    )
+    in_rows, in_cols = term_in.shape[1], term_in.shape[2]
+    down_rows, down_cols = term_down.shape[1], term_down.shape[2]
+    part_in = term_in.astype(jnp.bfloat16).reshape(local_experts, n_dp, -1)
+    part_down = term_down.astype(jnp.bfloat16).reshape(local_experts, n_dp, -1)
+    parts = jnp.transpose(jnp.concatenate([part_in, part_down], axis=2), (1, 0, 2))
+    parts = parts.reshape(n_dp, -1, width)
+    summed = lax.psum_scatter(parts, "dp", scatter_dimension=0, tiled=True).reshape(1, local_experts, -1)
+    split = part_in.shape[2]
+    grad_in = summed[0, :, :split].reshape(local_experts, in_rows // n_dp, in_cols).astype(jnp.float32)
+    grad_down = summed[0, :, split:].reshape(local_experts, down_rows // n_dp, down_cols).astype(jnp.float32)
     return (input_grad, grad_in, grad_down)
 
 

time: 243 us -> 266 us (1.095)
  waiting for transfers between devices: 120 us -> 44 us
  blocking collectives: 0 us -> 55.7 us
  local copies, waits for them, and re-layouts: 41.4 us -> 78.1 us
  other arithmetic: 14.4 us -> 42.5 us
  starting transfers between devices: 24.3 us -> 6.28 us
  matrix products: 28.3 us -> 23.9 us
    all_to_all x0 -> x1, blocking collectives: none -> 55.7 us  [per_device(): lax.all_to_all(send, 'expert', split_axis=0, concat_axis=0, tiled=True)]
    reshape x0 -> x6, local copies, waits for them, and re-layouts: none -> 47.7 us  [the longest x2 19.1 us: per_device(): part_in = term_in.astype(jnp.bfloat16).reshape(local_experts, n_dp, -1)]
    reduce_scatter x2 -> x1, waiting for transfers between devices: 57 us -> 18.8 us  [per_device(): lax.psum_scatter(parts, 'dp', scatter_dimension=0, tiled=True)]
    all_to_all x2 -> x0, waiting for transfers between devices: 37.5 us -> none  [the longest x1 22 us: per_device(): lax.all_to_all(send_scaled, 'expert', split_axis=0, concat_axis=1, tiled=...]
    transpose x0 -> x1, other arithmetic: none -> 22.2 us  [per_device(): jnp.transpose(jnp.concatenate([part_in, part_down], axis=2), (1, 0, 2))]
    all_to_all x2 -> x0, starting transfers between devices: 15.7 us -> none  [the longest x1 8.25 us: per_device(): lax.all_to_all(send_scaled, 'expert', split_axis=0, concat_axis=1, tiled=...]
    all_to_all x2 -> x0, local copies, waits for them, and re-layouts: 5.16 us -> none  [the longest x1 3.23 us: per_device(): lax.all_to_all(send_inputs, 'expert', split_axis=0, concat_axis=1, tiled=...]
    scatter x1 -> x0, local copies, waits for them, and re-layouts: 4.79 us -> none  [per_device(): empty.at[destination].set(repeated).reshape(experts_all, capacity, width)]
  transfers between devices with their start and end apart: 5 -> 2, of which waited for: 4 -> 2; matrix products, arithmetic and copies ran while one was open for 23% -> 9% of each run, Pallas kernels for 0% -> 0%
where the time goes in v1:
time: 266 us; the launch traced here: 265 us
  local copies, waits for them, and re-layouts  78.1 us (29%)
  blocking collectives  55.7 us (21%)
  waiting for transfers between devices  44 us (17%)
  other arithmetic  42.5 us (16%)
  matrix products  23.9 us (9%)
  between operations  14.2 us (5%)
  starting transfers between devices  6.28 us (2%)
    all_to_all x1, blocking collectives, per_device(): lax.all_to_all(send, 'expert', split_axis=0, concat_axis=0, tiled=True)  55.7 us
    all_to_all x1, waiting for transfers between devices, per_device(): lax.all_to_all(returned, 'expert', split_axis=1, concat_axis=0, tiled=True)  25.2 us
    transpose x1, other arithmetic, per_device(): jnp.transpose(jnp.concatenate([part_in, part_down], axis=2), (1, 0, 2))  22.2 us
    reshape x2, local copies, waits for them, and re-layouts, per_device(): part_in = term_in.astype(jnp.bfloat16).reshape(local_experts, n_dp, -1)  19.1 us
    reduce_scatter x1, waiting for transfers between devices, per_device(): lax.psum_scatter(parts, 'dp', scatter_dimension=0, tiled=True)  18.8 us
    reshape x1, local copies, waits for them, and re-layouts, per_device(): parts = parts.reshape(n_dp, -1, width)  16.1 us
    reshape x2, local copies, waits for them, and re-layouts, per_device(): part_down = term_down.astype(jnp.bfloat16).reshape(local_experts, n_dp, -1)  10.1 us
    scatter x1, other arithmetic, per_device(): empty.at[dest_all].set(rows_all).reshape(experts_all, 2, capacity, width)  9.05 us
  transfers between devices with their start and end apart: 2, of which 2 were waited for; matrix products, arithmetic and copies ran while one was open for 9% of the time, Pallas kernels for 0%

profile of v1, /device:TPU:4, one launch (start us, length us, event | category | flops | bytes accessed | tf_op | source)
XLA Modules:
  0.0 264.8 jit_solution(7775496048006080013)
XLA Ops:
  9.8 2.6 broadcast_in_dim.5
  12.3 2.2 reshape.164
  14.6 2.9 %mul.53 = f32[256,2,1024]{2,1,0:T(2,128)} broadcast(bf16[256,1024]{1,0:T(8,128)(2,1)} %param.8), dimensions={0,2} | broadcast | bytes 2621440 | tf_op jit(solution)/shard_map/mul | solution.py:29
  17.5 3.7 %mul.54 = f32[512,1024]{1,0:T(8,128)} reshape(f32[256,2,1024]{2,1,0:T(2,128)} %mul.53) | data formatting | bytes 4194304 | tf_op jit(solution)/shard_map/mul | solution.py:29
  21.2 2.8 %multiply_convert_fusion.3 = bf16[512,1024]{1,0:T(8,128)(2,1)} fusion(f32[512,1024]{1,0:T(8,128)} %mul.54, f32[512]{0:T(512)S(1)} %mul.51), kind=kLoop, calls=%fused_computation.15 | loop fusion | flops 1048576 | bytes 3147776 | tf_op jit(solution)/shard_map/convert_element_type | solution.py:29
  23.9 9.1 %scatter_custom_fusion = bf16[2048,1024]{1,0:T(8,128)(2,1)} fusion(s32[1024]{0:T(1024)S(1)} %bitcast.45, bf16[512,1024]{1,0:T(8,128)(2,1)} %multiply_convert_fusion.3, bf16[]{:T(256)} %constant.6, bf16[512,1024]{1,0:T(8,128)(2,1)} %reshape.164, bf16[]{:T(256)} %constant.7.clone.1), kind=kCustom, calls=%fused_computation.11 | custom fusion | flops 4194304 | bytes 6291460 | tf_op jit(solution)/shard_map/scatter | solution.py:36
  33.0 55.7 %all_to_all.20 = bf16[32,2,32,1024]{3,2,1,0:T(8,128)(2,1)S(1)} all-to-all(bf16[32,2,32,1024]{3,2,1,0:T(8,128)(2,1)} %bitcast.33), channel_id=1, replica_groups=mesh['dp'=16,'expert'=16] {'expert'}, dimensions={0} | all-to-all | bytes 8388608 | tf_op jit(solution)/shard_map/all_to_all | solution.py:37
  89.9 1.4 slice-done
  91.3 1.2 slice-done.1
  92.5 3.4 %fusion.13 = f32[2,512,1536]{2,1,0:T(8,128)S(1)} fusion(bf16[2,512,1024]{2,1,0:T(8,128)(2,1)S(1)} %bitcast.37, bf16[2,1024,1536]{2,1,0:T(8,128)(2,1)S(1)} %bitcast.47), kind=kOutput, calls=%fused_computation.38 | convolution fusion | flops 3221225472 | bytes 14680064 | tf_op jit(solution)/shard_map/ksd,kdf->ksf/dot_general | solution.py:10
  95.9 3.6 %convolution_convert_fusion.1 = bf16[2,768,1024]{2,1,0:T(8,128)(2,1)} fusion(bf16[2,512,1024]{2,1,0:T(8,128)(2,1)S(1)} %bitcast.39, f32[2,512,1536]{2,1,0:T(8,128)S(1)} %fusion.13), kind=kOutput, calls=%fused_computation.10 | convolution fusion | flops 1616904192 | bytes 11534336 | tf_op jit(solution)/shard_map/ksf,ksd->kfd/dot_general | solution.py:45
  99.6 4.2 %multiply_convert_fusion.2 = (bf16[2,512,768]{2,1,0:T(8,128)(2,1)}, bf16[2,512,768]{2,1,0:T(8,128)(2,1)}) fusion(f32[2,512,1536]{2,1,0:T(8,128)S(1)} %fusion.13, bf16[2,512,1024]{2,1,0:T(8,128)(2,1)S(1)} %bitcast.40, bf16[2,768,1024]{2,1,0:T(8,128)(2,1)S(1)} %copy-done), kind=kOutput, calls=%fused_computation.7 | convolution fusion | flops 1620836352 | bytes 14680064 | tf_op jit(solution)/shard_map/ksd,kfd->ksf/dot_general | solution.py:42
  103.8 4.8 %reshape.171 = bf16[2,16,49152]{2,1,0:T(8,128)(2,1)} reshape(bf16[2,768,1024]{2,1,0:T(8,128)(2,1)} %convolution_convert_fusion.1) | data formatting | bytes 6291456 | tf_op jit(solution)/shard_map/reshape | solution.py:61
  108.6 5.3 %copy.35 = bf16[2,16,49152]{2,0,1:T(2,128)(2,1)S(1)} copy(bf16[2,16,49152]{2,1,0:T(8,128)(2,1)} %reshape.171) | data formatting | bytes 6291456 | tf_op jit(solution)/shard_map/reshape | solution.py:61
  113.9 5.4 %convolution_convert_fusion = bf16[2,1024,1536]{2,1,0:T(8,128)(2,1)} fusion(bf16[2,512,1024]{2,1,0:T(8,128)(2,1)S(1)} %bitcast.38, bf16[2,512,768]{2,1,0:T(8,128)(2,1)S(1)} %copy-done.6, bf16[2,512,768]{2,1,0:T(8,128)(2,1)S(1)} %copy-done.5), kind=kOutput, calls=%fused_computation.3 | convolution fusion | flops 3230662656 | bytes 11534336 | tf_op jit(solution)/shard_map/ksd,ksf->kdf/dot_general | solution.py:51
  119.4 7.3 %reshape.170 = bf16[2,16,98304]{2,1,0:T(8,128)(2,1)} reshape(bf16[2,1024,1536]{2,1,0:T(8,128)(2,1)} %convolution_convert_fusion) | data formatting | bytes 12582912 | tf_op jit(solution)/shard_map/reshape | solution.py:60
  126.6 11.9 %copy.34 = bf16[2,16,98304]{2,0,1:T(2,128)(2,1)S(1)} copy(bf16[2,16,98304]{2,1,0:T(8,128)(2,1)} %reshape.170) | data formatting | bytes 12582912 | tf_op jit(solution)/shard_map/reshape | solution.py:60
  138.5 22.2 %maximum_bitcast_fusion = bf16[16,2,147456]{2,1,0:T(2,128)(2,1)} fusion(bf16[2,16,49152]{2,0,1:T(2,128)(2,1)S(1)} %copy.35, bf16[2,16,98304]{2,0,1:T(2,128)(2,1)S(1)} %copy.34), kind=kLoop, calls=%fused_computation.2 | loop fusion | flops 18874368 | bytes 18874368 | tf_op jit(solution)/shard_map/transpose | solution.py:62
  160.6 16.1 %reshape.172 = bf16[16,288,1024]{2,1,0:T(8,128)(2,1)} reshape(bf16[16,2,147456]{2,1,0:T(2,128)(2,1)} %maximum_bitcast_fusion) | data formatting | bytes 18874368 | tf_op jit(solution)/shard_map/reshape | solution.py:63
  176.8 7.2 %fusion.7 = bf16[2,512,1024]{2,1,0:T(8,128)(2,1)S(1)} fusion(bf16[2,1024,1536]{2,1,0:T(8,128)(2,1)} %param.12, bf16[2,512,768]{2,1,0:T(8,128)(2,1)} %get-tuple-element.8, bf16[2,512,768]{2,1,0:T(8,128)(2,1)} %get-tuple-element.7), kind=kOutput, calls=%fused_computation.18 | convolution fusion | flops 3228565504 | bytes 11534336 | tf_op jit(solution)/shard_map/ksf,kdf->ksd/dot_general | solution.py:52
  184.0 3.5 %copy.29 = bf16[2,512,1024]{2,0,1:T(2,128)(2,1)} copy(bf16[2,512,1024]{2,1,0:T(8,128)(2,1)S(1)} %fusion.7) | data formatting | bytes 4194304 | tf_op jit(solution)/shard_map/convert_element_type | solution.py:54
  187.5 6.2 %all-to-all-start.1 = ((bf16[2,512,1024]{2,0,1:T(2,128)(2,1)}), bf16[2,512,1024]{2,0,1:T(2,128)(2,1)S(1)}, u32[]{:S(2)}, u32[]{:S(2)}) async-start(bf16[2,512,1024]{2,0,1:T(2,128)(2,1)} %copy.29), calls=%async_computation.1 | async-start | bytes 4194304 | tf_op jit(solution)/shard_map/all_to_all | solution.py:55
  194.0 25.2 %all-to-all-done.1 = bf16[2,512,1024]{2,0,1:T(2,128)(2,1)S(1)} async-done(((bf16[2,512,1024]{2,0,1:T(2,128)(2,1)}), bf16[2,512,1024]{2,0,1:T(2,128)(2,1)S(1)}, u32[]{:S(2)}, u32[]{:S(2)}) %all-to-all-start.1) | async-done | bytes 2097184 | tf_op jit(solution)/shard_map/all_to_all | solution.py:55
  219.2 1.3 copy-done.2
  220.6 2.3 copy.30
  222.8 2.8 %gather_fusion = bf16[512,1024]{1,0:T(8,128)(2,1)} fusion(bf16[1024,1024]{1,0:T(8,128)(2,1)S(1)} %bitcast.32, s32[1024]{0:T(1024)S(1)} %pad_clamp_fusion), kind=kCustom, calls=%fused_computation | custom fusion | bytes 2099200 | tf_op jit(solution)/shard_map/gather | solution.py:56
  225.6 2.4 reshape.169
  228.0 4.6 %reduce_sum.12 = bf16[256,1024]{1,0:T(8,128)(2,1)} reduce(bf16[256,2,1024]{2,1,0:T(2,128)(2,1)} %reshape.169, bf16[]{:T(256)} %constant.7.clone.1), dimensions={1}, to_apply=%region_1.0 | reduce | flops 262144 | bytes 1572866 | tf_op jit(solution)/shard_map/reduce_sum | solution.py:57
  232.6 18.8 %reduce-scatter.2.cloned.1.call-done = bf16[1,288,1024]{2,1,0:T(8,128)(2,1)} async-done(((bf16[16,288,1024]{2,1,0:T(8,128)(2,1)}), bf16[1,288,1024]{2,1,0:T(8,128)(2,1)}) %reduce-scatter.2.cloned.1.call-update) | async-done | bytes 589840 | tf_op jit(solution)/shard_map/reduce_scatter | solution.py:64
  251.4 2.3 reshape.173
  253.7 1.1 slice_convert_fusion.1
  254.8 1.3 slice_convert_fusion
  (39 shorter events, 6.0 us)
Async XLA Ops:
  7.2 92.4 %copy-start = (bf16[2,768,1024]{2,1,0:T(8,128)(2,1)S(1)}, bf16[2,768,1024]{2,1,0:T(8,128)(2,1)}, u32[]{:S(2)}) copy-start(bf16[2,768,1024]{2,1,0:T(8,128)(2,1)} %param.13) | copy-start | bytes 9437188
  7.2 244.2 %reduce-scatter.2.cloned.1.call-start = ((), (), s32[]{:S(2)}) async-start(), calls=%async_computation.3 | async-start | bytes 10027008 | tf_op jit(solution)/shard_map/reduce_scatter | solution.py:64
  88.7 2.6 slice-start
  89.5 3.0 %slice-start.1 = ((s8[6291456]{0:T(1024)(128)(4,1)}), s8[2097152]{0:T(1024)(128)(4,1)S(1)}, s32[]{:S(2)}) async-start(s8[6291456]{0:T(1024)(128)(4,1)} %bitcast.46), calls=%async_computation.5 | async-start | bytes 4194304
  89.7 6.2 %copy-start.3 = (bf16[1,2,16,32,1024]{4,3,2,1,0:T(8,128)(2,1)}, bf16[1,2,16,32,1024]{4,3,2,1,0:T(8,128)(2,1)S(1)}, u32[]{:S(2)}) copy-start(bf16[1,2,16,32,1024]{4,3,2,1,0:T(8,128)(2,1)S(1)} %copy.28) | copy-start | bytes 6291460
  108.6 5.3 %copy-start.4 = (bf16[1,2,16,32,1024]{4,3,2,1,0:T(8,128)(2,1)S(1)}, bf16[1,2,16,32,1024]{4,3,2,1,0:T(8,128)(2,1)}, u32[]{:S(2)}) copy-start(bf16[1,2,16,32,1024]{4,3,2,1,0:T(8,128)(2,1)} %copy-done.3) | copy-start | bytes 6291460
  108.6 5.3 %copy-start.5 = (bf16[2,512,768]{2,1,0:T(8,128)(2,1)S(1)}, bf16[2,512,768]{2,1,0:T(8,128)(2,1)}, u32[]{:S(2)}) copy-start(bf16[2,512,768]{2,1,0:T(8,128)(2,1)} %get-tuple-element.7) | copy-start | bytes 4718596
  108.6 5.3 %copy-start.6 = (bf16[2,512,768]{2,1,0:T(8,128)(2,1)S(1)}, bf16[2,512,768]{2,1,0:T(8,128)(2,1)}, u32[]{:S(2)}) copy-start(bf16[2,512,768]{2,1,0:T(8,128)(2,1)} %get-tuple-element.8) | copy-start | bytes 4718596
  187.5 31.8 %all-to-all-start.1 = ((bf16[2,512,1024]{2,0,1:T(2,128)(2,1)}), bf16[2,512,1024]{2,0,1:T(2,128)(2,1)S(1)}, u32[]{:S(2)}, u32[]{:S(2)}) async-start(bf16[2,512,1024]{2,0,1:T(2,128)(2,1)} %copy.29), calls=%async_computation.1 | async-start | bytes 4194304 | tf_op jit(solution)/shard_map/all_to_all | solution.py:55
  219.2 1.3 copy-start.2
  225.6 32.3 %copy-start.1 = (bf16[2,768,1024]{2,1,0:T(8,128)(2,1)S(1)}, bf16[2,768,1024]{2,1,0:T(8,128)(2,1)}, u32[]{:S(2)}) copy-start(bf16[2,768,1024]{2,1,0:T(8,128)(2,1)} %param.13) | copy-start | bytes 9437188
Sparse Core Ops, SparseCore 0:
  176.9 74.4 reduce-scatter.1

commit v2 on v1

--- a/solution.py
+++ b/solution.py
@@ -28,12 +28,14 @@
     combine = jnp.stack([first, 1.0 - first], axis=1)
     scaled = (combine[:, :, None] * cotangent[:, None, :].astype(jnp.float32)).astype(jnp.bfloat16)
     destination = (expert_ids * capacity + slot_pos).reshape(-1)
-    dest_in = (expert_ids * (2 * capacity) + slot_pos).reshape(-1)
-    dest_all = jnp.concatenate([dest_in, dest_in + capacity])
-    repeated = jnp.broadcast_to(tokens[:, None, :], (token_count, TOP, width)).reshape(-1, width)
-    rows_all = jnp.concatenate([repeated, scaled.reshape(-1, width)], axis=0)
-    empty = jnp.zeros((experts_all * 2 * capacity, width), jnp.bfloat16)
-    send = empty.at[dest_all].set(rows_all).reshape(experts_all, 2, capacity, width)
+    target = expert_ids * (2 * capacity) + slot_pos
+    sources = jnp.concatenate([tokens, scaled.reshape(-1, width)], axis=0)
+    first_row = jnp.concatenate([target[:, 0], target.reshape(-1) + capacity])
+    second_row = jnp.concatenate([target[:, 1], jnp.full((TOP * token_count,), -1, jnp.int32)])
+    buffer_row = lax.broadcasted_iota(jnp.int32, (experts_all * 2 * capacity, sources.shape[0]), 0)
+    picks = ((buffer_row == first_row[None, :]) | (buffer_row == second_row[None, :])).astype(jnp.bfloat16)
+    send = jnp.dot(picks, sources, preferred_element_type=jnp.float32).astype(jnp.bfloat16)
+    send = send.reshape(experts_all, 2, capacity, width)
     got = lax.all_to_all(send, "expert", split_axis=0, concat_axis=0, tiled=True)
     got = got.reshape(n_expert, local_experts, 2, capacity, width)
     got = jnp.transpose(got, (2, 1, 0, 3, 4)).reshape(2, local_experts, n_expert * capacity, width)
@@ -57,14 +59,13 @@
     input_grad = jnp.sum(rows.astype(jnp.float32), axis=1).astype(jnp.bfloat16)
     in_rows, in_cols = term_in.shape[1], term_in.shape[2]
     down_rows, down_cols = term_down.shape[1], term_down.shape[2]
-    part_in = term_in.astype(jnp.bfloat16).reshape(local_experts, n_dp, -1)
-    part_down = term_down.astype(jnp.bfloat16).reshape(local_experts, n_dp, -1)
-    parts = jnp.transpose(jnp.concatenate([part_in, part_down], axis=2), (1, 0, 2))
-    parts = parts.reshape(n_dp, -1, width)
-    summed = lax.psum_scatter(parts, "dp", scatter_dimension=0, tiled=True).reshape(1, local_experts, -1)
-    split = part_in.shape[2]
-    grad_in = summed[0, :, :split].reshape(local_experts, in_rows // n_dp, in_cols).astype(jnp.float32)
-    grad_down = summed[0, :, split:].reshape(local_experts, down_rows // n_dp, down_cols).astype(jnp.float32)
+    part_in = term_in.astype(jnp.bfloat16).reshape(local_experts, n_dp, in_rows // n_dp, in_cols)
+    down_flat = (down_rows // n_dp) * down_cols // in_cols
+    part_down = term_down.astype(jnp.bfloat16).reshape(local_experts, n_dp, down_flat, in_cols)
+    parts = jnp.concatenate([part_in, part_down], axis=2).reshape(local_experts, -1, in_cols)
+    summed = lax.psum_scatter(parts, "dp", scatter_dimension=1, tiled=True)
+    grad_in = summed[:, : in_rows // n_dp].astype(jnp.float32)
+    grad_down = summed[:, in_rows // n_dp :].reshape(local_experts, down_rows // n_dp, down_cols).astype(jnp.float32)
     return (input_grad, grad_in, grad_down)
 
 

time: 266 us -> 193 us (0.73)
  local copies, waits for them, and re-layouts: 78.1 us -> 30 us
  other arithmetic: 42.5 us -> 15.1 us
  matrix products: 23.9 us -> 28 us
    reshape x7 -> x2, local copies, waits for them, and re-layouts: 49.9 us -> 5.29 us  [the longest x1 4.5 us: per_device(): term_down.astype(jnp.bfloat16)]
    transpose x1 -> x0, other arithmetic: 22.2 us -> none  [per_device(): jnp.transpose(jnp.concatenate([part_in, part_down], axis=2), (1, 0, 2))]
    scatter x1 -> x0, other arithmetic: 9.05 us -> none  [per_device(): empty.at[dest_all].set(rows_all).reshape(experts_all, 2, capacity, width)]
    concatenate x0 -> x2, other arithmetic: none -> 4.1 us  [the longest x1 4.09 us: per_device(): jnp.concatenate([part_in, part_down], axis=2)]
    dot_general x0 -> x1, matrix products: none -> 3.66 us  [per_device(): jnp.dot(picks, sources, preferred_element_type=jnp.float32)]
    unnamed x21 -> x12, local copies, waits for them, and re-layouts: 5.81 us -> 2.51 us
    gather x1, local copies, waits for them, and re-layouts: 2.79 us -> 5.53 us  [per_device(): arrived.reshape(-1, width)[destination].reshape(token_count, TOP, width)]
  transfers between devices with their start and end apart: 2 -> 2, of which waited for: 2 -> 2; matrix products, arithmetic and copies ran while one was open for 9% -> 13% of each run, Pallas kernels for 0% -> 0%
where the time goes in v2:
time: 193 us; the launch traced here: 192 us
  blocking collectives  55.5 us (29%)
  waiting for transfers between devices  43.1 us (22%)
  local copies, waits for them, and re-layouts  30 us (16%)
  matrix products  28 us (15%)
  other arithmetic  15.1 us (8%)
  between operations  14.2 us (7%)
  starting transfers between devices  6.26 us (3%)
    all_to_all x1, blocking collectives, per_device(): lax.all_to_all(send, 'expert', split_axis=0, concat_axis=0, tiled=True)  55.5 us
    all_to_all x1, waiting for transfers between devices, per_device(): lax.all_to_all(returned, 'expert', split_axis=1, concat_axis=0, tiled=True)  25.2 us
    reduce_scatter x1, waiting for transfers between devices, per_device(): summed = lax.psum_scatter(parts, 'dp', scatter_dimension=1, tiled=True)  17.9 us
    dot_general x1, matrix products, per_device(): jnp.einsum('ksf,kdf->ksd', grad_pair, w_in, preferred_element_type=jnp.fl...  7.18 us
    mul x3, local copies, waits for them, and re-layouts, per_device(): combine[:, :, None] * cotangent[:, None, :].astype(jnp.float32)  6.75 us
    all_to_all x1, starting transfers between devices, per_device(): lax.all_to_all(returned, 'expert', split_axis=1, concat_axis=0, tiled=True)  6.23 us
    dot_general x1, matrix products, per_device(): jnp.einsum('ksd,ksf->kdf', input_slots, grad_pair, preferred_element_type...  5.98 us
    gather x1, local copies, waits for them, and re-layouts, per_device(): arrived.reshape(-1, width)[destination].reshape(token_count, TOP, width)  5.53 us
  transfers between devices with their start and end apart: 2, of which 2 were waited for; matrix products, arithmetic and copies ran while one was open for 13% of the time, Pallas kernels for 0%

profile of v2, /device:TPU:4, one launch (start us, length us, event | category | flops | bytes accessed | tf_op | source)
XLA Modules:
  0.0 192.0 jit_solution(10411846773504207823)
XLA Ops:
  7.2 0.9 broadcast_subtract_fusion
  8.1 0.8 broadcast_add_fusion
  9.0 0.1 add.46
  9.3 0.1 mul.51
  9.4 2.9 %mul.53 = f32[256,2,1024]{2,1,0:T(2,128)} broadcast(bf16[256,1024]{1,0:T(8,128)(2,1)} %param.8), dimensions={0,2} | broadcast | bytes 2621440 | tf_op jit(solution)/shard_map/mul | solution.py:29
  12.4 3.7 %mul.54 = f32[512,1024]{1,0:T(8,128)} reshape(f32[256,2,1024]{2,1,0:T(2,128)} %mul.53) | data formatting | bytes 4194304 | tf_op jit(solution)/shard_map/mul | solution.py:29
  16.1 1.8 multiply_convert_fusion.3
  17.9 3.7 %fusion.3 = bf16[2048,1024]{1,0:T(8,128)(2,1)S(1)} fusion(s32[768]{0:T(1024)S(1)} %concatenate.17, s32[768]{0:T(1024)S(1)} %pad_add_fusion, bf16[512,1024]{1,0:T(8,128)(2,1)S(1)} %multiply_convert_fusion.3, bf16[256,1024]{1,0:T(8,128)(2,1)S(1)} %copy-done.3), kind=kOutput, calls=%fused_computation.8 | convolution fusion | flops 3231186944 | bytes 5773312 | tf_op jit(solution)/shard_map/dot_general | solution.py:37
  21.6 55.5 %all_to_all.20 = bf16[32,2,32,1024]{3,2,1,0:T(8,128)(2,1)S(1)} all-to-all(bf16[32,2,32,1024]{3,2,1,0:T(8,128)(2,1)S(1)} %bitcast.29), channel_id=1, replica_groups=mesh['dp'=16,'expert'=16] {'expert'}, dimensions={0} | all-to-all | bytes 8388608 | tf_op jit(solution)/shard_map/all_to_all | solution.py:39
  77.0 0.8 copy.32
  77.9 0.6 fusion.19
  78.5 0.2 slice-done
  78.6 2.3 %slice-done.1 = s8[4194304]{0:T(1024)(128)(4,1)S(1)} async-done(((s8[6291456]{0:T(1024)(128)(4,1)}), s8[4194304]{0:T(1024)(128)(4,1)S(1)}, s32[]{:S(2)}) %slice-start.1) | async-done | bytes 4194328
  81.0 3.4 %fusion.21 = f32[2,512,1536]{2,1,0:T(8,128)S(1)} fusion(bf16[2,512,1024]{2,1,0:T(8,128)(2,1)S(1)} %bitcast.30, bf16[2,1024,1536]{2,1,0:T(8,128)(2,1)S(1)} %bitcast.38), kind=kOutput, calls=%fused_computation.41 | convolution fusion | flops 3221225472 | bytes 14680064 | tf_op jit(solution)/shard_map/ksd,kdf->ksf/dot_general | solution.py:10
  84.4 3.7 %convolution_convert_fusion.1 = bf16[2,768,1024]{2,1,0:T(8,128)(2,1)} fusion(bf16[2,512,1024]{2,1,0:T(8,128)(2,1)S(1)} %bitcast.32, f32[2,512,1536]{2,1,0:T(8,128)S(1)} %fusion.21), kind=kOutput, calls=%fused_computation.17 | convolution fusion | flops 1616904192 | bytes 11534336 | tf_op jit(solution)/shard_map/ksf,ksd->kfd/dot_general | solution.py:47
  88.1 4.1 %multiply_convert_fusion.2 = (bf16[2,512,768]{2,1,0:T(8,128)(2,1)}, bf16[2,512,768]{2,1,0:T(8,128)(2,1)}) fusion(f32[2,512,1536]{2,1,0:T(8,128)S(1)} %fusion.21, bf16[2,512,1024]{2,1,0:T(8,128)(2,1)S(1)} %bitcast.33, bf16[2,768,1024]{2,1,0:T(8,128)(2,1)S(1)} %copy-done), kind=kOutput, calls=%fused_computation.12 | convolution fusion | flops 1620836352 | bytes 14680064 | tf_op jit(solution)/shard_map/ksd,kfd->ksf/dot_general | solution.py:44
  92.1 4.5 %reshape.85 = bf16[2,16,32,1536]{3,2,1,0:T(8,128)(2,1)S(1)} reshape(bf16[2,768,1024]{2,1,0:T(8,128)(2,1)} %convolution_convert_fusion.1) | data formatting | bytes 6291456 | tf_op jit(solution)/shard_map/reshape | solution.py:64
  96.6 6.0 %convolution_convert_fusion = bf16[2,1024,1536]{2,1,0:T(8,128)(2,1)S(1)} fusion(bf16[2,512,1024]{2,1,0:T(8,128)(2,1)} %bitcast.31, bf16[2,512,768]{2,1,0:T(8,128)(2,1)} %get-tuple-element.8, bf16[2,512,768]{2,1,0:T(8,128)(2,1)} %get-tuple-element.7), kind=kOutput, calls=%fused_computation.6 | convolution fusion | flops 3230662656 | bytes 11534336 | tf_op jit(solution)/shard_map/ksd,ksf->kdf/dot_general | solution.py:53
  102.6 4.1 %pad_maximum_fusion = bf16[2,16,96,1536]{3,2,1,0:T(8,128)(2,1)} fusion(bf16[2,16,32,1536]{3,2,1,0:T(8,128)(2,1)S(1)} %reshape.85, bf16[2,16,64,1536]{3,2,1,0:T(8,128)(2,1)S(1)} %bitcast.28), kind=kLoop, calls=%fused_computation.1 | loop fusion | flops 18874368 | bytes 18874368 | tf_op jit(solution)/shard_map/concatenate | solution.py:65
  106.7 7.2 %fusion.10 = bf16[2,512,1024]{2,1,0:T(8,128)(2,1)S(1)} fusion(bf16[2,1024,1536]{2,1,0:T(8,128)(2,1)} %param.12, bf16[2,512,768]{2,1,0:T(8,128)(2,1)} %get-tuple-element.8, bf16[2,512,768]{2,1,0:T(8,128)(2,1)} %get-tuple-element.7), kind=kOutput, calls=%fused_computation.20 | convolution fusion | flops 3228565504 | bytes 11534336 | tf_op jit(solution)/shard_map/ksf,kdf->ksd/dot_general | solution.py:54
  113.9 3.5 %copy.24 = bf16[2,512,1024]{2,0,1:T(2,128)(2,1)} copy(bf16[2,512,1024]{2,1,0:T(8,128)(2,1)S(1)} %fusion.10) | data formatting | bytes 4194304 | tf_op jit(solution)/shard_map/convert_element_type | solution.py:56
  117.4 6.2 %all-to-all-start.1 = ((bf16[2,512,1024]{2,0,1:T(2,128)(2,1)}), bf16[2,512,1024]{2,0,1:T(2,128)(2,1)S(1)}, u32[]{:S(2)}, u32[]{:S(2)}) async-start(bf16[2,512,1024]{2,0,1:T(2,128)(2,1)} %copy.24), calls=%async_computation.1 | async-start | bytes 4194304 | tf_op jit(solution)/shard_map/all_to_all | solution.py:57
  123.8 0.1 reshape.82
  123.9 25.2 %all-to-all-done.1 = bf16[2,512,1024]{2,0,1:T(2,128)(2,1)S(1)} async-done(((bf16[2,512,1024]{2,0,1:T(2,128)(2,1)}), bf16[2,512,1024]{2,0,1:T(2,128)(2,1)S(1)}, u32[]{:S(2)}, u32[]{:S(2)}) %all-to-all-start.1) | async-done | bytes 2097184 | tf_op jit(solution)/shard_map/all_to_all | solution.py:57
  149.2 2.0 %copy.25 = bf16[2,16,32,1024]{3,2,0,1:T(8,128)(2,1)} copy(bf16[2,16,32,1024]{3,0,2,1:T(2,128)(2,1)S(1)} %bitcast.27) | data formatting | bytes 4194304 | tf_op jit(solution)/shard_map/all_to_all | solution.py:57
  151.2 5.5 %gather_fusion = bf16[512,1024]{1,0:T(8,128)(2,1)} fusion(bf16[1024,1024]{1,0:T(8,128)(2,1)} %bitcast.23, s32[1024]{0:T(1024)S(1)} %pad_clamp_fusion), kind=kCustom, calls=%fused_computation | custom fusion | bytes 2099200 | tf_op jit(solution)/shard_map/gather | solution.py:58
  156.7 2.3 %reshape.83 = bf16[256,2,1024]{2,1,0:T(2,128)(2,1)} reshape(bf16[512,1024]{1,0:T(8,128)(2,1)} %gather_fusion) | data formatting | bytes 2097152 | tf_op jit(solution)/shard_map/reshape | solution.py:58
  159.0 4.6 %reduce_sum.12 = bf16[256,1024]{1,0:T(8,128)(2,1)} reduce(bf16[256,2,1024]{2,1,0:T(2,128)(2,1)} %reshape.83, bf16[]{:T(256)} %constant.5.clone.1), dimensions={1}, to_apply=%region_0.0 | reduce | flops 262144 | bytes 1572866 | tf_op jit(solution)/shard_map/reduce_sum | solution.py:59
  163.5 17.9 %reduce-scatter.2.cloned.1.call-done = bf16[2,96,1536]{2,1,0:T(8,128)(2,1)} async-done(((bf16[2,1536,1536]{2,1,0:T(8,128)(2,1)}), bf16[2,96,1536]{2,1,0:T(8,128)(2,1)}) %reduce-scatter.2.cloned.1.call-update) | async-done | bytes 589840 | tf_op jit(solution)/shard_map/reduce_scatter | solution.py:66
  181.4 1.0 slice_convert_fusion.1
  182.4 0.9 reshape.87
  183.2 2.0 %slice_convert_fusion = f32[2,64,1536]{2,1,0:T(8,128)} fusion(bf16[2,96,1536]{2,1,0:T(8,128)(2,1)} %reduce-scatter.2.cloned.1.call-done), kind=kLoop, calls=%fused_computation.24 | loop fusion | flops 196608 | bytes 1179648 | tf_op jit(solution)/shard_map/convert_element_type | solution.py:67
  (22 shorter events, 0.5 us)
Async XLA Ops:
  7.2 80.9 %copy-start = (bf16[2,768,1024]{2,1,0:T(8,128)(2,1)S(1)}, bf16[2,768,1024]{2,1,0:T(8,128)(2,1)}, u32[]{:S(2)}) copy-start(bf16[2,768,1024]{2,1,0:T(8,128)(2,1)} %param.13) | copy-start | bytes 9437188
  7.2 174.2 %reduce-scatter.2.cloned.1.call-start = ((), (), s32[]{:S(2)}) async-start(), calls=%async_computation.3 | async-start | bytes 10027008 | tf_op jit(solution)/shard_map/reduce_scatter | solution.py:66
  16.1 1.8 copy-start.3
  77.0 1.6 slice-start
  77.9 3.1 %slice-start.1 = ((s8[6291456]{0:T(1024)(128)(4,1)}), s8[4194304]{0:T(1024)(128)(4,1)S(1)}, s32[]{:S(2)}) async-start(s8[6291456]{0:T(1024)(128)(4,1)} %bitcast.37), calls=%async_computation.5 | async-start | bytes 8388608
  78.5 5.9 %copy-start.2 = (bf16[1,2,16,32,1024]{4,3,2,1,0:T(8,128)(2,1)}, bf16[1,2,16,32,1024]{4,3,2,1,0:T(8,128)(2,1)S(1)}, u32[]{:S(2)}) copy-start(bf16[1,2,16,32,1024]{4,3,2,1,0:T(8,128)(2,1)S(1)} %get-tuple-element.9) | copy-start | bytes 6291460
  117.4 31.8 %all-to-all-start.1 = ((bf16[2,512,1024]{2,0,1:T(2,128)(2,1)}), bf16[2,512,1024]{2,0,1:T(2,128)(2,1)S(1)}, u32[]{:S(2)}, u32[]{:S(2)}) async-start(bf16[2,512,1024]{2,0,1:T(2,128)(2,1)} %copy.24), calls=%async_computation.1 | async-start | bytes 4194304 | tf_op jit(solution)/shard_map/all_to_all | solution.py:57
  151.2 34.0 %copy-start.1 = (bf16[2,768,1024]{2,1,0:T(8,128)(2,1)S(1)}, bf16[2,768,1024]{2,1,0:T(8,128)(2,1)}, u32[]{:S(2)}) copy-start(bf16[2,768,1024]{2,1,0:T(8,128)(2,1)} %param.13) | copy-start | bytes 9437188
Sparse Core Ops, SparseCore 0:
  106.9 74.5 reduce-scatter.1

commit v3 on v2

--- a/solution.py
+++ b/solution.py
@@ -21,7 +21,8 @@
     local_experts = w_in.shape[0]
     hidden_width = w_down.shape[1]
     n_expert = lax.axis_size("expert")
-    n_dp = lax.axis_size("dp")
+    n_z, n_core = lax.axis_size("dz"), lax.axis_size("dc")
+    n_dp = n_z * n_core
     experts_all = local_experts * n_expert
     capacity = 2 * TOP * token_count // experts_all
     first = jax.nn.sigmoid(route_logits[:, 0] - route_logits[:, 1])
@@ -62,24 +63,33 @@
     part_in = term_in.astype(jnp.bfloat16).reshape(local_experts, n_dp, in_rows // n_dp, in_cols)
     down_flat = (down_rows // n_dp) * down_cols // in_cols
     part_down = term_down.astype(jnp.bfloat16).reshape(local_experts, n_dp, down_flat, in_cols)
-    parts = jnp.concatenate([part_in, part_down], axis=2).reshape(local_experts, -1, in_cols)
-    summed = lax.psum_scatter(parts, "dp", scatter_dimension=1, tiled=True)
+    parts = jnp.concatenate([part_in, part_down], axis=2)
+    parts = parts.reshape(local_experts, n_z, n_core, -1, in_cols)
+    parts = jnp.transpose(parts, (0, 2, 1, 3, 4)).reshape(local_experts, -1, in_cols)
+    summed = lax.psum_scatter(parts, "dc", scatter_dimension=1, tiled=True)
+    summed = lax.psum_scatter(summed, "dz", scatter_dimension=1, tiled=True)
     grad_in = summed[:, : in_rows // n_dp].astype(jnp.float32)
     grad_down = summed[:, in_rows // n_dp :].reshape(local_experts, down_rows // n_dp, down_cols).astype(jnp.float32)
     return (input_grad, grad_in, grad_down)
 
 
 def solution(mesh):
+    n_dp = mesh.shape["dp"]
+    n_z = n_dp // 2
+    split_mesh = jax.sharding.Mesh(
+        mesh.devices.reshape(n_z, n_dp // n_z, mesh.shape["expert"]), ("dz", "dc", "expert")
+    )
+    dp = ("dz", "dc")
     in_specs = (
-        P(("dp", "expert"), None),
-        P(("dp", "expert"), None),
-        P(("dp", "expert"), None),
-        P(("dp", "expert"), None),
-        P(("dp", "expert"), None),
+        P((*dp, "expert"), None),
+        P((*dp, "expert"), None),
+        P((*dp, "expert"), None),
+        P((*dp, "expert"), None),
+        P((*dp, "expert"), None),
         P("expert", None, None),
         P("expert", None, None),
     )
-    out_specs = (P(("dp", "expert"), None), P("expert", "dp", None), P("expert", "dp", None))
+    out_specs = (P((*dp, "expert"), None), P("expert", dp, None), P("expert", dp, None))
     return jax.shard_map(
-        per_device, mesh=mesh, in_specs=in_specs, out_specs=out_specs, check_vma=False
+        per_device, mesh=split_mesh, in_specs=in_specs, out_specs=out_specs, check_vma=False
     )

time: 193 us -> 217 us (1.12)
  waiting for transfers between devices: 43.1 us -> 56 us
  local copies, waits for them, and re-layouts: 30 us -> 38.2 us
    reduce_scatter x1 -> x2, waiting for transfers between devices: 17.9 us -> 27.8 us  [the longest x1 24.4 us: per_device(): summed = lax.psum_scatter(parts, 'dc', scatter_dimension=1, tiled=True)]
    transpose x0 -> x1, local copies, waits for them, and re-layouts: none -> 8.32 us  [per_device(): jnp.transpose(parts, (0, 2, 1, 3, 4)).reshape(local_experts, -1, in_cols)]
    concatenate x0 -> x1, local copies, waits for them, and re-layouts: none -> 4.5 us  [per_device(): parts = jnp.concatenate([part_in, part_down], axis=2)]
    reshape x1 -> x0, local copies, waits for them, and re-layouts: 4.5 us -> none  [per_device(): term_down.astype(jnp.bfloat16)]
    transpose x0 -> x1, other arithmetic: none -> 4.12 us  [per_device(): jnp.transpose(parts, (0, 2, 1, 3, 4)).reshape(local_experts, -1, in_cols)]
    concatenate x1 -> x0, other arithmetic: 4.09 us -> none  [per_device(): jnp.concatenate([part_in, part_down], axis=2)]
    all_to_all x1, waiting for transfers between devices: 25.2 us -> 28.2 us  [per_device(): lax.all_to_all(returned, 'expert', split_axis=1, concat_axis=0, tiled=True)]
  transfers between devices with their start and end apart: 2 -> 3, of which waited for: 2 -> 3; matrix products, arithmetic and copies ran while one was open for 13% -> 12% of each run, Pallas kernels for 0% -> 0%
where the time goes in v3:
time: 217 us; the launch traced here: 215 us
  waiting for transfers between devices  56 us (26%)
  blocking collectives  55.5 us (26%)
  local copies, waits for them, and re-layouts  38.2 us (18%)
  matrix products  28 us (13%)
  other arithmetic  15.1 us (7%)
  between operations  14.2 us (7%)
  starting transfers between devices  7.53 us (3%)
    all_to_all x1, blocking collectives, per_device(): lax.all_to_all(send, 'expert', split_axis=0, concat_axis=0, tiled=True)  55.5 us
    all_to_all x1, waiting for transfers between devices, per_device(): lax.all_to_all(returned, 'expert', split_axis=1, concat_axis=0, tiled=True)  28.2 us
    reduce_scatter x1, waiting for transfers between devices, per_device(): summed = lax.psum_scatter(parts, 'dc', scatter_dimension=1, tiled=True)  24.4 us
    transpose x1, local copies, waits for them, and re-layouts, per_device(): jnp.transpose(parts, (0, 2, 1, 3, 4)).reshape(local_experts, -1, in_cols)  8.32 us
    all_to_all x1, starting transfers between devices, per_device(): lax.all_to_all(returned, 'expert', split_axis=1, concat_axis=0, tiled=True)  7.23 us
    dot_general x1, matrix products, per_device(): jnp.einsum('ksf,kdf->ksd', grad_pair, w_in, preferred_element_type=jnp.fl...  7.19 us
    mul x3, local copies, waits for them, and re-layouts, per_device(): combine[:, :, None] * cotangent[:, None, :].astype(jnp.float32)  6.75 us
    dot_general x1, matrix products, per_device(): jnp.einsum('ksd,ksf->kdf', input_slots, grad_pair, preferred_element_type...  5.97 us
  transfers between devices with their start and end apart: 3, of which 3 were waited for; matrix products, arithmetic and copies ran while one was open for 12% of the time, Pallas kernels for 0%

profile of v3, /device:TPU:4, one launch (start us, length us, event | category | flops | bytes accessed | tf_op | source)
XLA Modules:
  0.0 214.5 jit_solution(16231243210420335591)
XLA Ops:
  7.2 0.9 broadcast_subtract_fusion
  8.1 0.8 broadcast_add_fusion
  9.4 2.9 %mul.53 = f32[256,2,1024]{2,1,0:T(2,128)} broadcast(bf16[256,1024]{1,0:T(8,128)(2,1)} %param.8), dimensions={0,2} | broadcast | bytes 2621440 | tf_op jit(solution)/shard_map/mul | solution.py:30
  12.4 3.7 %mul.54 = f32[512,1024]{1,0:T(8,128)} reshape(f32[256,2,1024]{2,1,0:T(2,128)} %mul.53) | data formatting | bytes 4194304 | tf_op jit(solution)/shard_map/mul | solution.py:30
  16.1 1.8 multiply_convert_fusion.3
  17.9 3.7 %fusion.3 = bf16[2048,1024]{1,0:T(8,128)(2,1)S(1)} fusion(s32[768]{0:T(1024)S(1)} %concatenate.22, s32[768]{0:T(1024)S(1)} %pad_add_fusion, bf16[512,1024]{1,0:T(8,128)(2,1)S(1)} %multiply_convert_fusion.3, bf16[256,1024]{1,0:T(8,128)(2,1)S(1)} %copy-done.3), kind=kOutput, calls=%fused_computation.8 | convolution fusion | flops 3231186944 | bytes 5773312 | tf_op jit(solution)/shard_map/dot_general | solution.py:38
  21.6 55.5 %all_to_all.20 = bf16[32,2,32,1024]{3,2,1,0:T(8,128)(2,1)S(1)} all-to-all(bf16[32,2,32,1024]{3,2,1,0:T(8,128)(2,1)S(1)} %bitcast.31), channel_id=1, replica_groups=mesh['dz'=8,'dc'=2,'expert'=16] {'expert'}, dimensions={0} | all-to-all | bytes 8388608 | tf_op jit(solution)/shard_map/all_to_all | solution.py:40
  77.0 0.8 copy.35
  77.9 0.6 fusion.19
  78.5 0.2 slice-done
  78.6 2.3 %slice-done.1 = s8[4194304]{0:T(1024)(128)(4,1)S(1)} async-done(((s8[6291456]{0:T(1024)(128)(4,1)}), s8[4194304]{0:T(1024)(128)(4,1)S(1)}, s32[]{:S(2)}) %slice-start.1) | async-done | bytes 4194328
  81.0 3.4 %fusion.21 = f32[2,512,1536]{2,1,0:T(8,128)S(1)} fusion(bf16[2,512,1024]{2,1,0:T(8,128)(2,1)S(1)} %bitcast.32, bf16[2,1024,1536]{2,1,0:T(8,128)(2,1)S(1)} %bitcast.40), kind=kOutput, calls=%fused_computation.41 | convolution fusion | flops 3221225472 | bytes 14680064 | tf_op jit(solution)/shard_map/ksd,kdf->ksf/dot_general | solution.py:10
  84.4 3.7 %convolution_convert_fusion.1 = bf16[2,768,1024]{2,1,0:T(8,128)(2,1)} fusion(bf16[2,512,1024]{2,1,0:T(8,128)(2,1)S(1)} %bitcast.34, f32[2,512,1536]{2,1,0:T(8,128)S(1)} %fusion.21), kind=kOutput, calls=%fused_computation.17 | convolution fusion | flops 1616904192 | bytes 11534336 | tf_op jit(solution)/shard_map/ksf,ksd->kfd/dot_general | solution.py:48
  88.1 4.1 %multiply_convert_fusion.2 = (bf16[2,512,768]{2,1,0:T(8,128)(2,1)}, bf16[2,512,768]{2,1,0:T(8,128)(2,1)}) fusion(f32[2,512,1536]{2,1,0:T(8,128)S(1)} %fusion.21, bf16[2,512,1024]{2,1,0:T(8,128)(2,1)S(1)} %bitcast.35, bf16[2,768,1024]{2,1,0:T(8,128)(2,1)S(1)} %copy-done), kind=kOutput, calls=%fused_computation.12 | convolution fusion | flops 1620836352 | bytes 14680064 | tf_op jit(solution)/shard_map/ksd,kfd->ksf/dot_general | solution.py:45
  92.2 4.5 %concatenate.26 = bf16[2,8,2,32,1536]{4,3,2,1,0:T(8,128)(2,1)S(1)} reshape(bf16[2,768,1024]{2,1,0:T(8,128)(2,1)} %convolution_convert_fusion.1) | data formatting | bytes 6291456 | tf_op jit(solution)/shard_map/concatenate | solution.py:66
  96.7 6.0 %convolution_convert_fusion = bf16[2,1024,1536]{2,1,0:T(8,128)(2,1)S(1)} fusion(bf16[2,512,1024]{2,1,0:T(8,128)(2,1)} %bitcast.33, bf16[2,512,768]{2,1,0:T(8,128)(2,1)} %get-tuple-element.8, bf16[2,512,768]{2,1,0:T(8,128)(2,1)} %get-tuple-element.7), kind=kOutput, calls=%fused_computation.6 | convolution fusion | flops 3230662656 | bytes 11534336 | tf_op jit(solution)/shard_map/ksd,ksf->kdf/dot_general | solution.py:54
  102.7 4.1 %maximum_bitcast_fusion = bf16[2,2,8,96,1536]{4,3,1,2,0:T(8,128)(2,1)} fusion(bf16[2,8,2,32,1536]{4,3,2,1,0:T(8,128)(2,1)S(1)} %concatenate.26, bf16[2,8,2,64,1536]{4,3,2,1,0:T(8,128)(2,1)S(1)} %bitcast.30), kind=kLoop, calls=%fused_computation.1 | loop fusion | flops 18874368 | bytes 18874368 | tf_op jit(solution)/shard_map/transpose | solution.py:68
  106.8 8.3 %copy.31 = bf16[2,2,8,96,1536]{4,3,2,1,0:T(8,128)(2,1)} copy(bf16[2,2,8,96,1536]{4,3,1,2,0:T(8,128)(2,1)} %maximum_bitcast_fusion) | data formatting | bytes 18874368 | tf_op jit(solution)/shard_map/transpose | solution.py:68
  115.1 0.3 reduce-scatter.5.cloned.1.call-start
  115.4 24.4 %reduce-scatter.3.cloned.1.call-done = bf16[2,768,1536]{2,1,0:T(8,128)(2,1)} async-done(((bf16[2,1536,1536]{2,1,0:T(8,128)(2,1)}), bf16[2,768,1536]{2,1,0:T(8,128)(2,1)}) %reduce-scatter.3.cloned.1.call-update) | async-done | bytes 4718608 | tf_op jit(solution)/shard_map/reduce_scatter | solution.py:69
  139.8 7.2 %fusion.10 = bf16[2,512,1024]{2,1,0:T(8,128)(2,1)S(1)} fusion(bf16[2,1024,1536]{2,1,0:T(8,128)(2,1)} %param.12, bf16[2,512,768]{2,1,0:T(8,128)(2,1)} %get-tuple-element.8, bf16[2,512,768]{2,1,0:T(8,128)(2,1)} %get-tuple-element.7), kind=kOutput, calls=%fused_computation.20 | convolution fusion | flops 3228565504 | bytes 11534336 | tf_op jit(solution)/shard_map/ksf,kdf->ksd/dot_general | solution.py:55
  147.0 3.5 %copy.26 = bf16[2,512,1024]{2,0,1:T(2,128)(2,1)} copy(bf16[2,512,1024]{2,1,0:T(8,128)(2,1)S(1)} %fusion.10) | data formatting | bytes 4194304 | tf_op jit(solution)/shard_map/convert_element_type | solution.py:57
  150.5 7.2 %all-to-all-start.1 = ((bf16[2,512,1024]{2,0,1:T(2,128)(2,1)}), bf16[2,512,1024]{2,0,1:T(2,128)(2,1)S(1)}, u32[]{:S(2)}, u32[]{:S(2)}) async-start(bf16[2,512,1024]{2,0,1:T(2,128)(2,1)} %copy.26), calls=%async_computation.1 | async-start | bytes 4194304 | tf_op jit(solution)/shard_map/all_to_all | solution.py:58
  158.1 28.2 %all-to-all-done.1 = bf16[2,512,1024]{2,0,1:T(2,128)(2,1)S(1)} async-done(((bf16[2,512,1024]{2,0,1:T(2,128)(2,1)}), bf16[2,512,1024]{2,0,1:T(2,128)(2,1)S(1)}, u32[]{:S(2)}, u32[]{:S(2)}) %all-to-all-start.1) | async-done | bytes 2097184 | tf_op jit(solution)/shard_map/all_to_all | solution.py:58
  186.2 2.0 copy.27
  188.2 5.5 %gather_fusion = bf16[512,1024]{1,0:T(8,128)(2,1)} fusion(bf16[1024,1024]{1,0:T(8,128)(2,1)} %bitcast.25, s32[1024]{0:T(1024)S(1)} %pad_clamp_fusion), kind=kCustom, calls=%fused_computation | custom fusion | bytes 2099200 | tf_op jit(solution)/shard_map/gather | solution.py:59
  193.7 2.3 %reshape.84 = bf16[256,2,1024]{2,1,0:T(2,128)(2,1)} reshape(bf16[512,1024]{1,0:T(8,128)(2,1)} %gather_fusion) | data formatting | bytes 2097152 | tf_op jit(solution)/shard_map/reshape | solution.py:59
  196.0 4.6 %reduce_sum.12 = bf16[256,1024]{1,0:T(8,128)(2,1)} reduce(bf16[256,2,1024]{2,1,0:T(2,128)(2,1)} %reshape.84, bf16[]{:T(256)} %constant.5.clone.1), dimensions={1}, to_apply=%region_0.0 | reduce | flops 262144 | bytes 1572866 | tf_op jit(solution)/shard_map/reduce_sum | solution.py:60
  200.6 3.4 %reduce-scatter.5.cloned.1.call-done = bf16[2,96,1536]{2,1,0:T(8,128)(2,1)} async-done(((bf16[2,768,1536]{2,1,0:T(8,128)(2,1)}), bf16[2,96,1536]{2,1,0:T(8,128)(2,1)}) %reduce-scatter.5.cloned.1.call-update) | async-done | bytes 589840 | tf_op jit(solution)/shard_map/reduce_scatter | solution.py:70
  203.9 1.0 slice_convert_fusion.1
  204.9 0.9 reshape.86
  205.7 2.0 slice_convert_fusion
  (26 shorter events, 1.0 us)
Async XLA Ops:
  7.2 80.9 %copy-start = (bf16[2,768,1024]{2,1,0:T(8,128)(2,1)S(1)}, bf16[2,768,1024]{2,1,0:T(8,128)(2,1)}, u32[]{:S(2)}) copy-start(bf16[2,768,1024]{2,1,0:T(8,128)(2,1)} %param.13) | copy-start | bytes 9437188
  7.2 132.6 %reduce-scatter.3.cloned.1.call-start = ((), (), s32[]{:S(2)}) async-start(), calls=%async_computation.4 | async-start | bytes 14155776 | tf_op jit(solution)/shard_map/reduce_scatter | solution.py:69
  16.1 1.8 copy-start.3
  77.0 1.6 slice-start
  77.9 3.1 %slice-start.1 = ((s8[6291456]{0:T(1024)(128)(4,1)}), s8[4194304]{0:T(1024)(128)(4,1)S(1)}, s32[]{:S(2)}) async-start(s8[6291456]{0:T(1024)(128)(4,1)} %bitcast.39), calls=%async_computation.7 | async-start | bytes 8388608
  78.5 5.9 %copy-start.2 = (bf16[1,2,16,32,1024]{4,3,2,1,0:T(8,128)(2,1)}, bf16[1,2,16,32,1024]{4,3,2,1,0:T(8,128)(2,1)S(1)}, u32[]{:S(2)}) copy-start(bf16[1,2,16,32,1024]{4,3,2,1,0:T(8,128)(2,1)S(1)} %get-tuple-element.9) | copy-start | bytes 6291460
  115.1 88.8 %reduce-scatter.5.cloned.1.call-start = ((), (), s32[]{:S(2)}) async-start(), calls=%async_computation.5 | async-start | bytes 5308416 | tf_op jit(solution)/shard_map/reduce_scatter | solution.py:70
  150.5 35.7 %all-to-all-start.1 = ((bf16[2,512,1024]{2,0,1:T(2,128)(2,1)}), bf16[2,512,1024]{2,0,1:T(2,128)(2,1)S(1)}, u32[]{:S(2)}, u32[]{:S(2)}) async-start(bf16[2,512,1024]{2,0,1:T(2,128)(2,1)} %copy.26), calls=%async_computation.1 | async-start | bytes 4194304 | tf_op jit(solution)/shard_map/all_to_all | solution.py:58
  188.2 19.5 %copy-start.1 = (bf16[2,768,1024]{2,1,0:T(8,128)(2,1)S(1)}, bf16[2,768,1024]{2,1,0:T(8,128)(2,1)}, u32[]{:S(2)}) copy-start(bf16[2,768,1024]{2,1,0:T(8,128)(2,1)} %param.13) | copy-start | bytes 9437188
Sparse Core Ops, SparseCore 0:
  115.2 24.5 reduce-scatter.2
  142.4 61.5 reduce-scatter.4

commit v4 on v2

--- a/solution.py
+++ b/solution.py
@@ -25,17 +25,21 @@
     experts_all = local_experts * n_expert
     capacity = 2 * TOP * token_count // experts_all
     first = jax.nn.sigmoid(route_logits[:, 0] - route_logits[:, 1])
-    combine = jnp.stack([first, 1.0 - first], axis=1)
-    scaled = (combine[:, :, None] * cotangent[:, None, :].astype(jnp.float32)).astype(jnp.bfloat16)
+    combine = (first, 1.0 - first)
+    cotangent_wide = cotangent.astype(jnp.float32)
     destination = (expert_ids * capacity + slot_pos).reshape(-1)
     target = expert_ids * (2 * capacity) + slot_pos
-    sources = jnp.concatenate([tokens, scaled.reshape(-1, width)], axis=0)
-    first_row = jnp.concatenate([target[:, 0], target.reshape(-1) + capacity])
-    second_row = jnp.concatenate([target[:, 1], jnp.full((TOP * token_count,), -1, jnp.int32)])
-    buffer_row = lax.broadcasted_iota(jnp.int32, (experts_all * 2 * capacity, sources.shape[0]), 0)
-    picks = ((buffer_row == first_row[None, :]) | (buffer_row == second_row[None, :])).astype(jnp.bfloat16)
-    send = jnp.dot(picks, sources, preferred_element_type=jnp.float32).astype(jnp.bfloat16)
-    send = send.reshape(experts_all, 2, capacity, width)
+    buffer_row = lax.broadcasted_iota(jnp.int32, (experts_all * 2 * capacity, token_count), 0)
+    picks = []
+    for k in range(TOP):
+        picks.append((buffer_row == target[None, :, k]).astype(jnp.bfloat16))
+    token_picks = picks[0] + picks[1]
+    send = jnp.dot(token_picks, tokens, preferred_element_type=jnp.float32)
+    for k in range(TOP):
+        scaled = (combine[k][:, None] * cotangent_wide).astype(jnp.bfloat16)
+        shifted = (buffer_row == target[None, :, k] + capacity).astype(jnp.bfloat16)
+        send = send + jnp.dot(shifted, scaled, preferred_element_type=jnp.float32)
+    send = send.astype(jnp.bfloat16).reshape(experts_all, 2, capacity, width)
     got = lax.all_to_all(send, "expert", split_axis=0, concat_axis=0, tiled=True)
     got = got.reshape(n_expert, local_experts, 2, capacity, width)
     got = jnp.transpose(got, (2, 1, 0, 3, 4)).reshape(2, local_experts, n_expert * capacity, width)

time: 193 us -> 185 us (0.959)
  local copies, waits for them, and re-layouts: 30 us -> 22.8 us
  matrix products: 28 us -> 30.6 us
  other arithmetic: 15.1 us -> 12.5 us
    mul x3 -> x0, local copies, waits for them, and re-layouts: 6.75 us -> none  [per_device(): combine[:, :, None] * cotangent[:, None, :].astype(jnp.float32)]
    dot_general x1 -> x3, matrix products: 3.66 us -> 6.31 us  [the longest x2 3.95 us: per_device(): send = send + jnp.dot(shifted, scaled, preferred_element_type=jnp.float32)]
  transfers between devices with their start and end apart: 2 -> 2, of which waited for: 2 -> 2; matrix products, arithmetic and copies ran while one was open for 13% -> 14% of each run, Pallas kernels for 0% -> 0%
where the time goes in v4:
time: 185 us
  blocking collectives  55.5 us (30%)
  waiting for transfers between devices  43.1 us (23%)
  matrix products  30.6 us (17%)
  local copies, waits for them, and re-layouts  22.8 us (12%)
  between operations  14.2 us (8%)
  other arithmetic  12.5 us (7%)
  starting transfers between devices  6.26 us (3%)
    all_to_all x1, blocking collectives, per_device(): lax.all_to_all(send, 'expert', split_axis=0, concat_axis=0, tiled=True)  55.5 us
    all_to_all x1, waiting for transfers between devices, per_device(): lax.all_to_all(returned, 'expert', split_axis=1, concat_axis=0, tiled=True)  25.2 us
    reduce_scatter x1, waiting for transfers between devices, per_device(): summed = lax.psum_scatter(parts, 'dp', scatter_dimension=1, tiled=True)  17.8 us
    dot_general x1, matrix products, per_device(): jnp.einsum('ksf,kdf->ksd', grad_pair, w_in, preferred_element_type=jnp.fl...  7.19 us
    all_to_all x1, starting transfers between devices, per_device(): lax.all_to_all(returned, 'expert', split_axis=1, concat_axis=0, tiled=True)  6.22 us
    dot_general x1, matrix products, per_device(): jnp.einsum('ksd,ksf->kdf', input_slots, grad_pair, preferred_element_type...  5.98 us
    gather x1, local copies, waits for them, and re-layouts, per_device(): arrived.reshape(-1, width)[destination].reshape(token_count, TOP, width)  5.53 us
    reduce_sum x1, other arithmetic, per_device(): input_grad = jnp.sum(rows.astype(jnp.float32), axis=1).astype(jnp.bfloat16)  4.59 us
  transfers between devices with their start and end apart: 2, of which 2 were waited for; matrix products, arithmetic and copies ran while one was open for 14% of the time, Pallas kernels for 0%

profile of v4, /device:TPU:4, one launch (start us, length us, event | category | flops | bytes accessed | tf_op | source)
XLA Modules:
  0.0 184.9 jit_solution(12968782361954455943)
XLA Ops:
  7.2 0.0 copy-start
  7.2 0.0 reduce-scatter.2.cloned.1.call-start
  7.2 0.9 multiply_add_fusion
  8.1 2.4 %fusion.9 = f32[2048,1024]{1,0:T(8,128)S(1)} fusion(bf16[256,1024]{1,0:T(8,128)(2,1)} %param.7, s32[256]{0:T(256)S(1)} %bitcast.40, s32[256]{0:T(256)S(1)} %bitcast.38), kind=kOutput, calls=%fused_computation.26 | convolution fusion | flops 1077936128 | bytes 8914944 | tf_op jit(solution)/shard_map/dot_general | solution.py:37
  10.5 1.3 fusion.3
  11.9 2.6 %add_convert_fusion = bf16[2048,1024]{1,0:T(8,128)(2,1)S(1)} fusion(f32[2048,1024]{1,0:T(8,128)S(1)} %fusion.9, f32[2048,1024]{1,0:T(8,128)S(1)} %fusion.3, s32[256]{0:T(256)S(1)} %broadcast_add_fusion, bf16[256,1024]{1,0:T(8,128)(2,1)} %param.8, f32[256]{0:T(256)S(1)} %bitcast.42), kind=kOutput, calls=%fused_computation.2 | convolution fusion | flops 1081344000 | bytes 21497856 | tf_op jit(solution)/shard_map/dot_general | solution.py:41
  14.5 55.5 %all_to_all.20 = bf16[32,2,32,1024]{3,2,1,0:T(8,128)(2,1)S(1)} all-to-all(bf16[32,2,32,1024]{3,2,1,0:T(8,128)(2,1)S(1)} %bitcast.30), channel_id=1, replica_groups=mesh['dp'=16,'expert'=16] {'expert'}, dimensions={0} | all-to-all | bytes 8388608 | tf_op jit(solution)/shard_map/all_to_all | solution.py:43
  70.0 0.8 copy.28
  70.8 0.6 fusion.24
  71.4 0.2 slice-done
  71.6 2.3 %slice-done.1 = s8[4194304]{0:T(1024)(128)(4,1)S(1)} async-done(((s8[6291456]{0:T(1024)(128)(4,1)}), s8[4194304]{0:T(1024)(128)(4,1)S(1)}, s32[]{:S(2)}) %slice-start.1) | async-done | bytes 4194328
  73.9 3.4 %fusion.26 = f32[2,512,1536]{2,1,0:T(8,128)S(1)} fusion(bf16[2,512,1024]{2,1,0:T(8,128)(2,1)S(1)} %bitcast.33, bf16[2,1024,1536]{2,1,0:T(8,128)(2,1)S(1)} %bitcast.45), kind=kOutput, calls=%fused_computation.48 | convolution fusion | flops 3221225472 | bytes 14680064 | tf_op jit(solution)/shard_map/ksd,kdf->ksf/dot_general | solution.py:10
  77.3 3.7 %convolution_convert_fusion.1 = bf16[2,768,1024]{2,1,0:T(8,128)(2,1)} fusion(bf16[2,512,1024]{2,1,0:T(8,128)(2,1)S(1)} %bitcast.35, f32[2,512,1536]{2,1,0:T(8,128)S(1)} %fusion.26), kind=kOutput, calls=%fused_computation.11 | convolution fusion | flops 1616904192 | bytes 11534336 | tf_op jit(solution)/shard_map/ksf,ksd->kfd/dot_general | solution.py:51
  81.0 4.0 %multiply_convert_fusion.2 = (bf16[2,512,768]{2,1,0:T(8,128)(2,1)}, bf16[2,512,768]{2,1,0:T(8,128)(2,1)}) fusion(f32[2,512,1536]{2,1,0:T(8,128)S(1)} %fusion.26, bf16[2,512,1024]{2,1,0:T(8,128)(2,1)S(1)} %bitcast.36, bf16[2,768,1024]{2,1,0:T(8,128)(2,1)S(1)} %copy-done), kind=kOutput, calls=%fused_computation.8 | convolution fusion | flops 1620836352 | bytes 14680064 | tf_op jit(solution)/shard_map/ksd,kfd->ksf/dot_general | solution.py:48
  85.0 4.5 %reshape.89 = bf16[2,16,32,1536]{3,2,1,0:T(8,128)(2,1)S(1)} reshape(bf16[2,768,1024]{2,1,0:T(8,128)(2,1)} %convolution_convert_fusion.1) | data formatting | bytes 6291456 | tf_op jit(solution)/shard_map/reshape | solution.py:68
  89.5 6.0 %convolution_convert_fusion = bf16[2,1024,1536]{2,1,0:T(8,128)(2,1)S(1)} fusion(bf16[2,512,1024]{2,1,0:T(8,128)(2,1)} %bitcast.34, bf16[2,512,768]{2,1,0:T(8,128)(2,1)} %get-tuple-element.6, bf16[2,512,768]{2,1,0:T(8,128)(2,1)} %get-tuple-element.5), kind=kOutput, calls=%fused_computation.3 | convolution fusion | flops 3230662656 | bytes 11534336 | tf_op jit(solution)/shard_map/ksd,ksf->kdf/dot_general | solution.py:57
  95.5 4.1 %pad_maximum_fusion = bf16[2,16,96,1536]{3,2,1,0:T(8,128)(2,1)} fusion(bf16[2,16,32,1536]{3,2,1,0:T(8,128)(2,1)S(1)} %reshape.89, bf16[2,16,64,1536]{3,2,1,0:T(8,128)(2,1)S(1)} %bitcast.32), kind=kLoop, calls=%fused_computation.1 | loop fusion | flops 18874368 | bytes 18874368 | tf_op jit(solution)/shard_map/concatenate | solution.py:69
  99.6 0.0 reduce-scatter.2.cloned.1.call-update
  99.7 7.2 %fusion.5 = bf16[2,512,1024]{2,1,0:T(8,128)(2,1)S(1)} fusion(bf16[2,1024,1536]{2,1,0:T(8,128)(2,1)} %param.12, bf16[2,512,768]{2,1,0:T(8,128)(2,1)} %get-tuple-element.6, bf16[2,512,768]{2,1,0:T(8,128)(2,1)} %get-tuple-element.5), kind=kOutput, calls=%fused_computation.20 | convolution fusion | flops 3228565504 | bytes 11534336 | tf_op jit(solution)/shard_map/ksf,kdf->ksd/dot_general | solution.py:58
  106.9 3.5 %copy.20 = bf16[2,512,1024]{2,0,1:T(2,128)(2,1)} copy(bf16[2,512,1024]{2,1,0:T(8,128)(2,1)S(1)} %fusion.5) | data formatting | bytes 4194304 | tf_op jit(solution)/shard_map/convert_element_type | solution.py:60
  110.3 6.2 %all-to-all-start.1 = ((bf16[2,512,1024]{2,0,1:T(2,128)(2,1)}), bf16[2,512,1024]{2,0,1:T(2,128)(2,1)S(1)}, u32[]{:S(2)}, u32[]{:S(2)}) async-start(bf16[2,512,1024]{2,0,1:T(2,128)(2,1)} %copy.20), calls=%async_computation.1 | async-start | bytes 4194304 | tf_op jit(solution)/shard_map/all_to_all | solution.py:61
  116.5 0.1 copy.22
  116.7 0.1 reshape.86
  116.9 25.2 %all-to-all-done.1 = bf16[2,512,1024]{2,0,1:T(2,128)(2,1)S(1)} async-done(((bf16[2,512,1024]{2,0,1:T(2,128)(2,1)}), bf16[2,512,1024]{2,0,1:T(2,128)(2,1)S(1)}, u32[]{:S(2)}, u32[]{:S(2)}) %all-to-all-start.1) | async-done | bytes 2097184 | tf_op jit(solution)/shard_map/all_to_all | solution.py:61
  142.1 2.0 %copy.21 = bf16[2,16,32,1024]{3,2,0,1:T(8,128)(2,1)} copy(bf16[2,16,32,1024]{3,0,2,1:T(2,128)(2,1)S(1)} %bitcast.31) | data formatting | bytes 4194304 | tf_op jit(solution)/shard_map/all_to_all | solution.py:61
  144.1 5.5 %gather_fusion = bf16[512,1024]{1,0:T(8,128)(2,1)} fusion(bf16[1024,1024]{1,0:T(8,128)(2,1)} %bitcast.26, s32[1024]{0:T(1024)S(1)} %pad_clamp_fusion), kind=kCustom, calls=%fused_computation | custom fusion | bytes 2099200 | tf_op jit(solution)/shard_map/gather | solution.py:62
  149.6 2.3 %reshape.87 = bf16[256,2,1024]{2,1,0:T(2,128)(2,1)} reshape(bf16[512,1024]{1,0:T(8,128)(2,1)} %gather_fusion) | data formatting | bytes 2097152 | tf_op jit(solution)/shard_map/reshape | solution.py:62
  151.9 4.6 %reduce_sum.12 = bf16[256,1024]{1,0:T(8,128)(2,1)} reduce(bf16[256,2,1024]{2,1,0:T(2,128)(2,1)} %reshape.87, bf16[]{:T(256)} %constant.4.clone.1), dimensions={1}, to_apply=%region_0.0 | reduce | flops 262144 | bytes 1572866 | tf_op jit(solution)/shard_map/reduce_sum | solution.py:63
  156.5 17.8 %reduce-scatter.2.cloned.1.call-done = bf16[2,96,1536]{2,1,0:T(8,128)(2,1)} async-done(((bf16[2,1536,1536]{2,1,0:T(8,128)(2,1)}), bf16[2,96,1536]{2,1,0:T(8,128)(2,1)}) %reduce-scatter.2.cloned.1.call-update) | async-done | bytes 589840 | tf_op jit(solution)/shard_map/reduce_scatter | solution.py:70
  174.3 1.0 slice_convert_fusion.1
  175.3 0.9 reshape.91
  176.1 2.0 %slice_convert_fusion = f32[2,64,1536]{2,1,0:T(8,128)} fusion(bf16[2,96,1536]{2,1,0:T(8,128)(2,1)} %reduce-scatter.2.cloned.1.call-done), kind=kLoop, calls=%fused_computation.33 | loop fusion | flops 196608 | bytes 1179648 | tf_op jit(solution)/shard_map/convert_element_type | solution.py:71
  (18 shorter events, 0.1 us)
Async XLA Ops:
  7.2 73.8 %copy-start = (bf16[2,768,1024]{2,1,0:T(8,128)(2,1)S(1)}, bf16[2,768,1024]{2,1,0:T(8,128)(2,1)}, u32[]{:S(2)}) copy-start(bf16[2,768,1024]{2,1,0:T(8,128)(2,1)} %param.13) | copy-start | bytes 9437188
  7.2 167.1 %reduce-scatter.2.cloned.1.call-start = ((), (), s32[]{:S(2)}) async-start(), calls=%async_computation.3 | async-start | bytes 10027008 | tf_op jit(solution)/shard_map/reduce_scatter | solution.py:70
  8.1 2.4 %copy-start.4 = (f32[256,2]{0,1:T(2,128)S(1)}, f32[256,2]{0,1:T(2,128)}, u32[]{:S(2)}) copy-start(f32[256,2]{0,1:T(2,128)} %param.9) | copy-start | bytes 6148
  8.1 2.4 %copy-start.3 = (bf16[256,1024]{1,0:T(8,128)(2,1)S(1)}, bf16[256,1024]{1,0:T(8,128)(2,1)}, u32[]{:S(2)}) copy-start(bf16[256,1024]{1,0:T(8,128)(2,1)} %param.8) | copy-start | bytes 1572868
  70.0 1.6 slice-start
  70.8 3.1 %slice-start.1 = ((s8[6291456]{0:T(1024)(128)(4,1)}), s8[4194304]{0:T(1024)(128)(4,1)S(1)}, s32[]{:S(2)}) async-start(s8[6291456]{0:T(1024)(128)(4,1)} %bitcast.44), calls=%async_computation.5 | async-start | bytes 8388608
  71.4 5.9 %copy-start.2 = (bf16[1,2,16,32,1024]{4,3,2,1,0:T(8,128)(2,1)}, bf16[1,2,16,32,1024]{4,3,2,1,0:T(8,128)(2,1)S(1)}, u32[]{:S(2)}) copy-start(bf16[1,2,16,32,1024]{4,3,2,1,0:T(8,128)(2,1)S(1)} %get-tuple-element.7) | copy-start | bytes 6291460
  110.3 31.8 %all-to-all-start.1 = ((bf16[2,512,1024]{2,0,1:T(2,128)(2,1)}), bf16[2,512,1024]{2,0,1:T(2,128)(2,1)S(1)}, u32[]{:S(2)}, u32[]{:S(2)}) async-start(bf16[2,512,1024]{2,0,1:T(2,128)(2,1)} %copy.20), calls=%async_computation.1 | async-start | bytes 4194304 | tf_op jit(solution)/shard_map/all_to_all | solution.py:61
  144.1 34.0 %copy-start.1 = (bf16[2,768,1024]{2,1,0:T(8,128)(2,1)S(1)}, bf16[2,768,1024]{2,1,0:T(8,128)(2,1)}, u32[]{:S(2)}) copy-start(bf16[2,768,1024]{2,1,0:T(8,128)(2,1)} %param.13) | copy-start | bytes 9437188
Sparse Core Ops, SparseCore 0:
  99.8 74.4 reduce-scatter.1

commit v5 on v4

--- a/solution.py
+++ b/solution.py
@@ -63,13 +63,21 @@
     input_grad = jnp.sum(rows.astype(jnp.float32), axis=1).astype(jnp.bfloat16)
     in_rows, in_cols = term_in.shape[1], term_in.shape[2]
     down_rows, down_cols = term_down.shape[1], term_down.shape[2]
+    rows_q = down_rows // n_dp
+    main = rows_q * down_cols // in_cols
+    spare = in_cols - down_cols
     part_in = term_in.astype(jnp.bfloat16).reshape(local_experts, n_dp, in_rows // n_dp, in_cols)
-    down_flat = (down_rows // n_dp) * down_cols // in_cols
-    part_down = term_down.astype(jnp.bfloat16).reshape(local_experts, n_dp, down_flat, in_cols)
-    parts = jnp.concatenate([part_in, part_down], axis=2).reshape(local_experts, -1, in_cols)
+    part_down = term_down.astype(jnp.bfloat16).reshape(local_experts, n_dp, rows_q, down_cols)
+    pieces = [part_down[:, :, main:, c : c + spare] for c in range(0, down_cols, spare)]
+    packed = jnp.concatenate([part_down[:, :, :main], jnp.concatenate(pieces, axis=2)], axis=3)
+    parts = jnp.concatenate([part_in, packed], axis=2).reshape(local_experts, -1, in_cols)
     summed = lax.psum_scatter(parts, "dp", scatter_dimension=1, tiled=True)
     grad_in = summed[:, : in_rows // n_dp].astype(jnp.float32)
-    grad_down = summed[:, in_rows // n_dp :].reshape(local_experts, down_rows // n_dp, down_cols).astype(jnp.float32)
+    got_down = summed[:, in_rows // n_dp :]
+    rest = rows_q - main
+    tail = [got_down[:, i * rest : (i + 1) * rest, down_cols:] for i in range(down_cols // spare)]
+    grad_down = jnp.concatenate([got_down[:, :, :down_cols], jnp.concatenate(tail, axis=2)], axis=1)
+    grad_down = grad_down.astype(jnp.float32)
     return (input_grad, grad_in, grad_down)
 
 

time: 185 us -> 183 us (0.989)
    reshape x1 -> x0, local copies, waits for them, and re-layouts: 4.5 us -> none  [per_device(): term_down.astype(jnp.bfloat16)]
    dot_general x1, matrix products: 5.98 us -> 3.77 us  [per_device(): jnp.einsum('ksd,ksf->kdf', input_slots, grad_pair, preferred_element_type...]
    slice x0 -> x4, local copies, waits for them, and re-layouts: none -> 2.06 us  [the longest x1 0.91 us: per_device(): got_down[:, :, :down_cols]]
    dot_general x1, matrix products: 3.43 us -> 5.34 us  [recompute(): jnp.einsum('ksd,kdf->ksf', input_slots, w_in, preferred_element_type=jnp....]
    unnamed x14 -> x18, local copies, waits for them, and re-layouts: 2.52 us -> 4.08 us
where the time goes in v5:
time: 183 us
  blocking collectives  55.5 us (30%)
  waiting for transfers between devices  42.8 us (23%)
  matrix products  30.4 us (17%)
  local copies, waits for them, and re-layouts  21.1 us (12%)
  between operations  14.3 us (8%)
  other arithmetic  12.2 us (7%)
  starting transfers between devices  6.49 us (4%)
    all_to_all x1, blocking collectives, per_device(): lax.all_to_all(send, 'expert', split_axis=0, concat_axis=0, tiled=True)  55.5 us
    all_to_all x1, waiting for transfers between devices, per_device(): lax.all_to_all(returned, 'expert', split_axis=1, concat_axis=0, tiled=True)  25.2 us
    reduce_scatter x1, waiting for transfers between devices, per_device(): summed = lax.psum_scatter(parts, 'dp', scatter_dimension=1, tiled=True)  17.6 us
    dot_general x1, matrix products, per_device(): jnp.einsum('ksf,kdf->ksd', grad_pair, w_in, preferred_element_type=jnp.fl...  7.19 us
    all_to_all x1, starting transfers between devices, per_device(): lax.all_to_all(returned, 'expert', split_axis=1, concat_axis=0, tiled=True)  6.45 us
    gather x1, local copies, waits for them, and re-layouts, per_device(): arrived.reshape(-1, width)[destination].reshape(token_count, TOP, width)  5.52 us
    dot_general x1, matrix products, recompute(): jnp.einsum('ksd,kdf->ksf', input_slots, w_in, preferred_element_type=jnp....  5.34 us
    dot_general x1, matrix products, per_device(): jnp.einsum('ksf,ksd->kfd', hidden, cotangent_slots, preferred_element_typ...  4.85 us
  transfers between devices with their start and end apart: 2, of which 2 were waited for; matrix products, arithmetic and copies ran while one was open for 14% of the time, Pallas kernels for 0%

profile of v5, /device:TPU:4, one launch (start us, length us, event | category | flops | bytes accessed | tf_op | source)
XLA Modules:
  0.0 182.8 jit_solution(8444955441323931821)
XLA Ops:
  7.2 0.9 multiply_add_fusion
  8.1 2.4 %fusion.9 = f32[2048,1024]{1,0:T(8,128)S(1)} fusion(bf16[256,1024]{1,0:T(8,128)(2,1)} %param.7, s32[256]{0:T(256)S(1)} %bitcast.43, s32[256]{0:T(256)S(1)} %bitcast.41), kind=kOutput, calls=%fused_computation.26 | convolution fusion | flops 1077936128 | bytes 8914944 | tf_op jit(solution)/shard_map/dot_general | solution.py:37
  10.5 1.3 fusion.3
  11.9 2.6 %add_convert_fusion = bf16[2048,1024]{1,0:T(8,128)(2,1)S(1)} fusion(f32[2048,1024]{1,0:T(8,128)S(1)} %fusion.9, f32[2048,1024]{1,0:T(8,128)S(1)} %fusion.3, s32[256]{0:T(256)S(1)} %broadcast_add_fusion, bf16[256,1024]{1,0:T(8,128)(2,1)} %param.8, f32[256]{0:T(256)S(1)} %bitcast.45), kind=kOutput, calls=%fused_computation.2 | convolution fusion | flops 1081344000 | bytes 21497856 | tf_op jit(solution)/shard_map/dot_general | solution.py:41
  14.5 55.5 %all_to_all.20 = bf16[32,2,32,1024]{3,2,1,0:T(8,128)(2,1)S(1)} all-to-all(bf16[32,2,32,1024]{3,2,1,0:T(8,128)(2,1)S(1)} %bitcast.31), channel_id=1, replica_groups=mesh['dp'=16,'expert'=16] {'expert'}, dimensions={0} | all-to-all | bytes 8388608 | tf_op jit(solution)/shard_map/all_to_all | solution.py:43
  70.0 0.8 copy.28
  70.8 0.6 fusion.24
  71.4 0.8 slice-done
  72.2 0.9 slice-done.1
  73.0 5.3 %fusion.28 = f32[2,512,1536]{2,1,0:T(8,128)} fusion(bf16[2,512,1024]{2,1,0:T(8,128)(2,1)S(1)} %bitcast.36, bf16[2,1024,1536]{2,1,0:T(8,128)(2,1)S(1)} %bitcast.48), kind=kOutput, calls=%fused_computation.50 | convolution fusion | flops 3221225472 | bytes 14680064 | tf_op jit(solution)/shard_map/ksd,kdf->ksf/dot_general | solution.py:10
  78.4 4.8 %convolution_convert_fusion.1 = bf16[2,768,1024]{2,1,0:T(8,128)(2,1)S(1)} fusion(bf16[2,512,1024]{2,1,0:T(8,128)(2,1)S(1)} %bitcast.38, f32[2,512,1536]{2,1,0:T(8,128)} %fusion.28), kind=kOutput, calls=%fused_computation.11 | convolution fusion | flops 1616904192 | bytes 11534336 | tf_op jit(solution)/shard_map/ksf,ksd->kfd/dot_general | solution.py:51
  83.3 0.1 fusion.25
  83.4 0.2 slice.76
  83.6 2.4 %copy-done.4 = f32[2,512,1536]{2,1,0:T(8,128)S(1)} copy-done((f32[2,512,1536]{2,1,0:T(8,128)S(1)}, f32[2,512,1536]{2,1,0:T(8,128)}, u32[]{:S(2)}) %copy-start.4) | copy-done | bytes 6291480
  86.0 3.0 %multiply_convert_fusion.2 = (bf16[2,512,768]{2,1,0:T(8,128)(2,1)S(1)}, bf16[2,512,768]{2,1,0:T(8,128)(2,1)S(1)}) fusion(f32[2,512,1536]{2,1,0:T(8,128)S(1)} %copy-done.4, bf16[2,512,1024]{2,1,0:T(8,128)(2,1)S(1)} %bitcast.39, bf16[2,768,1024]{2,1,0:T(8,128)(2,1)S(1)} %copy-done), kind=kOutput, calls=%fused_computation.8 | convolution fusion | flops 1620836352 | bytes 14680064 | tf_op jit(solution)/shard_map/ksd,kfd->ksf/dot_general | solution.py:48
  89.0 3.8 %convolution_convert_fusion = bf16[2,1024,1536]{2,1,0:T(8,128)(2,1)S(1)} fusion(bf16[2,512,1024]{2,1,0:T(8,128)(2,1)S(1)} %bitcast.37, bf16[2,512,768]{2,1,0:T(8,128)(2,1)S(1)} %get-tuple-element.6, bf16[2,512,768]{2,1,0:T(8,128)(2,1)S(1)} %get-tuple-element.5), kind=kOutput, calls=%fused_computation.3 | convolution fusion | flops 3230662656 | bytes 11534336 | tf_op jit(solution)/shard_map/ksd,ksf->kdf/dot_general | solution.py:57
  92.8 4.0 %maximum_maximum_fusion = bf16[2,16,96,1536]{3,2,1,0:T(8,128)(2,1)} fusion(bf16[2,16,16,512]{3,2,1,0:T(8,128)(2,1)S(1)} %get-tuple-element.10, bf16[2,16,16,512]{3,2,1,0:T(8,128)(2,1)S(1)} %get-tuple-element.9, bf16[2,16,32,1024]{3,2,1,0:T(8,128)(2,1)S(1)} %slice.76, bf16[2,16,64,1536]{3,2,1,0:T(8,128)(2,1)S(1)} %bitcast.33), kind=kLoop, calls=%fused_computation.1 | loop fusion | flops 37748736 | bytes 18874368 | tf_op jit(solution)/shard_map/concatenate | solution.py:73
  96.9 7.2 %fusion.5 = bf16[2,512,1024]{2,1,0:T(8,128)(2,1)S(1)} fusion(bf16[2,1024,1536]{2,1,0:T(8,128)(2,1)} %param.12, bf16[2,512,768]{2,1,0:T(8,128)(2,1)} %copy-done.6, bf16[2,512,768]{2,1,0:T(8,128)(2,1)} %copy-done.5), kind=kOutput, calls=%fused_computation.20 | convolution fusion | flops 3228565504 | bytes 11534336 | tf_op jit(solution)/shard_map/ksf,kdf->ksd/dot_general | solution.py:58
  104.0 3.5 %copy.20 = bf16[2,512,1024]{2,0,1:T(2,128)(2,1)} copy(bf16[2,512,1024]{2,1,0:T(8,128)(2,1)S(1)} %fusion.5) | data formatting | bytes 4194304 | tf_op jit(solution)/shard_map/convert_element_type | solution.py:60
  107.5 6.4 %all-to-all-start.1 = ((bf16[2,512,1024]{2,0,1:T(2,128)(2,1)}), bf16[2,512,1024]{2,0,1:T(2,128)(2,1)S(1)}, u32[]{:S(2)}, u32[]{:S(2)}) async-start(bf16[2,512,1024]{2,0,1:T(2,128)(2,1)} %copy.20), calls=%async_computation.1 | async-start | bytes 4194304 | tf_op jit(solution)/shard_map/all_to_all | solution.py:61
  114.0 0.1 copy.22
  114.1 0.1 reshape.83
  114.3 25.2 %all-to-all-done.1 = bf16[2,512,1024]{2,0,1:T(2,128)(2,1)S(1)} async-done(((bf16[2,512,1024]{2,0,1:T(2,128)(2,1)}), bf16[2,512,1024]{2,0,1:T(2,128)(2,1)S(1)}, u32[]{:S(2)}, u32[]{:S(2)}) %all-to-all-start.1) | async-done | bytes 2097184 | tf_op jit(solution)/shard_map/all_to_all | solution.py:61
  139.5 2.0 %copy.21 = bf16[2,16,32,1024]{3,2,0,1:T(8,128)(2,1)} copy(bf16[2,16,32,1024]{3,0,2,1:T(2,128)(2,1)S(1)} %bitcast.32) | data formatting | bytes 4194304 | tf_op jit(solution)/shard_map/all_to_all | solution.py:61
  141.5 5.5 %gather_fusion = bf16[512,1024]{1,0:T(8,128)(2,1)} fusion(bf16[1024,1024]{1,0:T(8,128)(2,1)} %bitcast.27, s32[1024]{0:T(1024)S(1)} %pad_clamp_fusion), kind=kCustom, calls=%fused_computation | custom fusion | bytes 2099200 | tf_op jit(solution)/shard_map/gather | solution.py:62
  147.1 2.3 %reshape.84 = bf16[256,2,1024]{2,1,0:T(2,128)(2,1)} reshape(bf16[512,1024]{1,0:T(8,128)(2,1)} %gather_fusion) | data formatting | bytes 2097152 | tf_op jit(solution)/shard_map/reshape | solution.py:62
  149.3 4.6 %reduce_sum.12 = bf16[256,1024]{1,0:T(8,128)(2,1)} reduce(bf16[256,2,1024]{2,1,0:T(2,128)(2,1)} %reshape.84, bf16[]{:T(256)} %constant.4.clone.1), dimensions={1}, to_apply=%region_0.0 | reduce | flops 262144 | bytes 1572866 | tf_op jit(solution)/shard_map/reduce_sum | solution.py:63
  153.9 17.6 %reduce-scatter.2.cloned.1.call-done = bf16[2,96,1536]{2,1,0:T(8,128)(2,1)} async-done(((bf16[2,1536,1536]{2,1,0:T(8,128)(2,1)}), bf16[2,96,1536]{2,1,0:T(8,128)(2,1)}) %reduce-scatter.2.cloned.1.call-update) | async-done | bytes 589840 | tf_op jit(solution)/shard_map/reduce_scatter | solution.py:74
  171.5 0.8 fusion.26
  172.3 0.9 slice.80
  173.2 0.8 maximum_convert_fusion
  174.0 2.0 %slice_convert_fusion = f32[2,64,1536]{2,1,0:T(8,128)} fusion(bf16[2,96,1536]{2,1,0:T(8,128)(2,1)} %reduce-scatter.2.cloned.1.call-done), kind=kLoop, calls=%fused_computation.33 | loop fusion | flops 196608 | bytes 1179648 | tf_op jit(solution)/shard_map/convert_element_type | solution.py:75
  (24 shorter events, 0.1 us)
Async XLA Ops:
  7.2 76.5 %copy-start = (bf16[2,768,1024]{2,1,0:T(8,128)(2,1)S(1)}, bf16[2,768,1024]{2,1,0:T(8,128)(2,1)}, u32[]{:S(2)}) copy-start(bf16[2,768,1024]{2,1,0:T(8,128)(2,1)} %param.13) | copy-start | bytes 9437188
  7.2 164.3 %reduce-scatter.2.cloned.1.call-start = ((), (), s32[]{:S(2)}) async-start(), calls=%async_computation.3 | async-start | bytes 10027008 | tf_op jit(solution)/shard_map/reduce_scatter | solution.py:74
  8.1 2.4 %copy-start.3 = (f32[256,2]{0,1:T(2,128)S(1)}, f32[256,2]{0,1:T(2,128)}, u32[]{:S(2)}) copy-start(f32[256,2]{0,1:T(2,128)} %param.9) | copy-start | bytes 6148
  8.1 2.4 %copy-start.2 = (bf16[256,1024]{1,0:T(8,128)(2,1)S(1)}, bf16[256,1024]{1,0:T(8,128)(2,1)}, u32[]{:S(2)}) copy-start(bf16[256,1024]{1,0:T(8,128)(2,1)} %param.8) | copy-start | bytes 1572868
  70.0 2.2 %slice-start = ((s8[6291456]{0:T(1024)(128)(4,1)}), s8[4194304]{0:T(1024)(128)(4,1)S(1)}, s32[]{:S(2)}) async-start(s8[6291456]{0:T(1024)(128)(4,1)} %bitcast.47), calls=%async_computation.4 | async-start | bytes 8388608
  70.8 2.3 %slice-start.1 = ((s8[6291456]{0:T(1024)(128)(4,1)}), s8[2097152]{0:T(1024)(128)(4,1)S(1)}, s32[]{:S(2)}) async-start(s8[6291456]{0:T(1024)(128)(4,1)} %bitcast.47), calls=%async_computation.5 | async-start | bytes 4194304
  83.2 2.8 %copy-start.4 = (f32[2,512,1536]{2,1,0:T(8,128)S(1)}, f32[2,512,1536]{2,1,0:T(8,128)}, u32[]{:S(2)}) copy-start(f32[2,512,1536]{2,1,0:T(8,128)} %fusion.28) | copy-start | bytes 18874372
  89.0 3.8 %copy-start.5 = (bf16[2,512,768]{2,1,0:T(8,128)(2,1)}, bf16[2,512,768]{2,1,0:T(8,128)(2,1)S(1)}, u32[]{:S(2)}) copy-start(bf16[2,512,768]{2,1,0:T(8,128)(2,1)S(1)} %get-tuple-element.5) | copy-start | bytes 4718596
  89.0 3.8 %copy-start.6 = (bf16[2,512,768]{2,1,0:T(8,128)(2,1)}, bf16[2,512,768]{2,1,0:T(8,128)(2,1)S(1)}, u32[]{:S(2)}) copy-start(bf16[2,512,768]{2,1,0:T(8,128)(2,1)S(1)} %get-tuple-element.6) | copy-start | bytes 4718596
  107.5 32.0 %all-to-all-start.1 = ((bf16[2,512,1024]{2,0,1:T(2,128)(2,1)}), bf16[2,512,1024]{2,0,1:T(2,128)(2,1)S(1)}, u32[]{:S(2)}, u32[]{:S(2)}) async-start(bf16[2,512,1024]{2,0,1:T(2,128)(2,1)} %copy.20), calls=%async_computation.1 | async-start | bytes 4194304 | tf_op jit(solution)/shard_map/all_to_all | solution.py:61
  141.5 34.4 %copy-start.1 = (bf16[2,768,1024]{2,1,0:T(8,128)(2,1)S(1)}, bf16[2,768,1024]{2,1,0:T(8,128)(2,1)}, u32[]{:S(2)}) copy-start(bf16[2,768,1024]{2,1,0:T(8,128)(2,1)} %param.13) | copy-start | bytes 9437188
Sparse Core Ops, SparseCore 0:
  97.0 74.4 reduce-scatter.1

commit v6 on v5

--- a/solution.py
+++ b/solution.py
@@ -29,16 +29,18 @@
     cotangent_wide = cotangent.astype(jnp.float32)
     destination = (expert_ids * capacity + slot_pos).reshape(-1)
     target = expert_ids * (2 * capacity) + slot_pos
-    buffer_row = lax.broadcasted_iota(jnp.int32, (experts_all * 2 * capacity, token_count), 0)
-    picks = []
+    sources = [tokens]
+    first_row, second_row = [target[:, 0]], [target[:, 1]]
     for k in range(TOP):
-        picks.append((buffer_row == target[None, :, k]).astype(jnp.bfloat16))
-    token_picks = picks[0] + picks[1]
-    send = jnp.dot(token_picks, tokens, preferred_element_type=jnp.float32)
-    for k in range(TOP):
-        scaled = (combine[k][:, None] * cotangent_wide).astype(jnp.bfloat16)
-        shifted = (buffer_row == target[None, :, k] + capacity).astype(jnp.bfloat16)
-        send = send + jnp.dot(shifted, scaled, preferred_element_type=jnp.float32)
+        sources.append((combine[k][:, None] * cotangent_wide).astype(jnp.bfloat16))
+        first_row.append(target[:, k] + capacity)
+        second_row.append(jnp.full((token_count,), -1, jnp.int32))
+    sources = jnp.concatenate(sources, axis=0)
+    first_row = jnp.concatenate(first_row)
+    second_row = jnp.concatenate(second_row)
+    buffer_row = lax.broadcasted_iota(jnp.int32, (experts_all * 2 * capacity, sources.shape[0]), 0)
+    picks = ((buffer_row == first_row[None, :]) | (buffer_row == second_row[None, :])).astype(jnp.bfloat16)
+    send = jnp.dot(picks, sources, preferred_element_type=jnp.float32)
     send = send.astype(jnp.bfloat16).reshape(experts_all, 2, capacity, width)
     got = lax.all_to_all(send, "expert", split_axis=0, concat_axis=0, tiled=True)
     got = got.reshape(n_expert, local_experts, 2, capacity, width)

time: 183 us -> 184 us (level)
  other arithmetic: 12.2 us -> 14.3 us
    dot_general x3 -> x1, matrix products: 6.31 us -> 4.68 us  [per_device(): send = jnp.dot(picks, sources, preferred_element_type=jnp.float32)]
    unnamed x18 -> x14, local copies, waits for them, and re-layouts: 4.08 us -> 4.06 us
where the time goes in v6:
time: 184 us; the launch traced here: 183 us
  blocking collectives  55.5 us (30%)
  waiting for transfers between devices  42.8 us (23%)
  matrix products  28.8 us (16%)
  local copies, waits for them, and re-layouts  21.1 us (11%)
  other arithmetic  14.3 us (8%)
  between operations  14.2 us (8%)
  starting transfers between devices  6.49 us (4%)
    all_to_all x1, blocking collectives, per_device(): lax.all_to_all(send, 'expert', split_axis=0, concat_axis=0, tiled=True)  55.5 us
    all_to_all x1, waiting for transfers between devices, per_device(): lax.all_to_all(returned, 'expert', split_axis=1, concat_axis=0, tiled=True)  25.2 us
    reduce_scatter x1, waiting for transfers between devices, per_device(): summed = lax.psum_scatter(parts, 'dp', scatter_dimension=1, tiled=True)  17.6 us
    dot_general x1, matrix products, per_device(): jnp.einsum('ksf,kdf->ksd', grad_pair, w_in, preferred_element_type=jnp.fl...  7.19 us
    all_to_all x1, starting transfers between devices, per_device(): lax.all_to_all(returned, 'expert', split_axis=1, concat_axis=0, tiled=True)  6.45 us
    gather x1, local copies, waits for them, and re-layouts, per_device(): arrived.reshape(-1, width)[destination].reshape(token_count, TOP, width)  5.52 us
    dot_general x1, matrix products, recompute(): jnp.einsum('ksd,kdf->ksf', input_slots, w_in, preferred_element_type=jnp....  5.34 us
    dot_general x1, matrix products, per_device(): jnp.einsum('ksf,ksd->kfd', hidden, cotangent_slots, preferred_element_typ...  4.85 us
  transfers between devices with their start and end apart: 2, of which 2 were waited for; matrix products, arithmetic and copies ran while one was open for 14% of the time, Pallas kernels for 0%

profile of v6, /device:TPU:4, one launch (start us, length us, event | category | flops | bytes accessed | tf_op | source)
XLA Modules:
  0.0 183.1 jit_solution(9438202184739525028)
XLA Ops:
  7.2 0.9 broadcast_subtract_fusion
  8.1 0.8 multiply_add_fusion
  8.9 1.3 fusion.16
  10.2 4.7 %fusion.3 = bf16[2048,1024]{1,0:T(8,128)(2,1)S(1)} fusion(s32[768]{0:T(1024)S(1)} %concatenate.30, s32[768]{0:T(1024)S(1)} %pad_add_fusion, bf16[256,1024]{1,0:T(8,128)(2,1)S(1)} %get-tuple-element.14, bf16[256,1024]{1,0:T(8,128)(2,1)S(1)} %get-tuple-element.13, bf16[256,1024]{1,0:T(8,128)(2,1)} %param.7), kind=kOutput, calls=%fused_computation.8 | convolution fusion | flops 3232759808 | bytes 5773312 | tf_op jit(solution)/shard_map/dot_general | solution.py:43
  14.9 55.5 %all_to_all.20 = bf16[32,2,32,1024]{3,2,1,0:T(8,128)(2,1)S(1)} all-to-all(bf16[32,2,32,1024]{3,2,1,0:T(8,128)(2,1)S(1)} %bitcast.32), channel_id=1, replica_groups=mesh['dp'=16,'expert'=16] {'expert'}, dimensions={0} | all-to-all | bytes 8388608 | tf_op jit(solution)/shard_map/all_to_all | solution.py:45
  70.3 0.8 copy.28
  71.2 0.6 fusion.23
  71.8 0.8 slice-done
  72.5 0.9 slice-done.1
  73.4 5.3 %fusion.27 = f32[2,512,1536]{2,1,0:T(8,128)} fusion(bf16[2,512,1024]{2,1,0:T(8,128)(2,1)S(1)} %bitcast.35, bf16[2,1024,1536]{2,1,0:T(8,128)(2,1)S(1)} %bitcast.47), kind=kOutput, calls=%fused_computation.48 | convolution fusion | flops 3221225472 | bytes 14680064 | tf_op jit(solution)/shard_map/ksd,kdf->ksf/dot_general | solution.py:10
  78.7 4.8 %convolution_convert_fusion.1 = bf16[2,768,1024]{2,1,0:T(8,128)(2,1)S(1)} fusion(bf16[2,512,1024]{2,1,0:T(8,128)(2,1)S(1)} %bitcast.37, f32[2,512,1536]{2,1,0:T(8,128)} %fusion.27), kind=kOutput, calls=%fused_computation.17 | convolution fusion | flops 1616904192 | bytes 11534336 | tf_op jit(solution)/shard_map/ksf,ksd->kfd/dot_general | solution.py:53
  83.6 0.1 fusion.24
  83.7 0.2 slice.76
  84.0 2.4 %copy-done.2 = f32[2,512,1536]{2,1,0:T(8,128)S(1)} copy-done((f32[2,512,1536]{2,1,0:T(8,128)S(1)}, f32[2,512,1536]{2,1,0:T(8,128)}, u32[]{:S(2)}) %copy-start.2) | copy-done | bytes 6291480
  86.4 3.0 %multiply_convert_fusion.2 = (bf16[2,512,768]{2,1,0:T(8,128)(2,1)S(1)}, bf16[2,512,768]{2,1,0:T(8,128)(2,1)S(1)}) fusion(f32[2,512,1536]{2,1,0:T(8,128)S(1)} %copy-done.2, bf16[2,512,1024]{2,1,0:T(8,128)(2,1)S(1)} %bitcast.38, bf16[2,768,1024]{2,1,0:T(8,128)(2,1)S(1)} %copy-done), kind=kOutput, calls=%fused_computation.12 | convolution fusion | flops 1620836352 | bytes 14680064 | tf_op jit(solution)/shard_map/ksd,kfd->ksf/dot_general | solution.py:50
  89.4 3.8 %convolution_convert_fusion = bf16[2,1024,1536]{2,1,0:T(8,128)(2,1)S(1)} fusion(bf16[2,512,1024]{2,1,0:T(8,128)(2,1)S(1)} %bitcast.36, bf16[2,512,768]{2,1,0:T(8,128)(2,1)S(1)} %get-tuple-element.6, bf16[2,512,768]{2,1,0:T(8,128)(2,1)S(1)} %get-tuple-element.5), kind=kOutput, calls=%fused_computation.6 | convolution fusion | flops 3230662656 | bytes 11534336 | tf_op jit(solution)/shard_map/ksd,ksf->kdf/dot_general | solution.py:59
  93.2 4.0 %maximum_maximum_fusion = bf16[2,16,96,1536]{3,2,1,0:T(8,128)(2,1)} fusion(bf16[2,16,16,512]{3,2,1,0:T(8,128)(2,1)S(1)} %get-tuple-element.10, bf16[2,16,16,512]{3,2,1,0:T(8,128)(2,1)S(1)} %get-tuple-element.9, bf16[2,16,32,1024]{3,2,1,0:T(8,128)(2,1)S(1)} %slice.76, bf16[2,16,64,1536]{3,2,1,0:T(8,128)(2,1)S(1)} %bitcast.31), kind=kLoop, calls=%fused_computation.1 | loop fusion | flops 37748736 | bytes 18874368 | tf_op jit(solution)/shard_map/concatenate | solution.py:75
  97.2 7.2 %fusion.10 = bf16[2,512,1024]{2,1,0:T(8,128)(2,1)S(1)} fusion(bf16[2,1024,1536]{2,1,0:T(8,128)(2,1)} %param.12, bf16[2,512,768]{2,1,0:T(8,128)(2,1)} %copy-done.4, bf16[2,512,768]{2,1,0:T(8,128)(2,1)} %copy-done.3), kind=kOutput, calls=%fused_computation.19 | convolution fusion | flops 3228565504 | bytes 11534336 | tf_op jit(solution)/shard_map/ksf,kdf->ksd/dot_general | solution.py:60
  104.4 3.5 %copy.20 = bf16[2,512,1024]{2,0,1:T(2,128)(2,1)} copy(bf16[2,512,1024]{2,1,0:T(8,128)(2,1)S(1)} %fusion.10) | data formatting | bytes 4194304 | tf_op jit(solution)/shard_map/convert_element_type | solution.py:62
  107.9 6.4 %all-to-all-start.1 = ((bf16[2,512,1024]{2,0,1:T(2,128)(2,1)}), bf16[2,512,1024]{2,0,1:T(2,128)(2,1)S(1)}, u32[]{:S(2)}, u32[]{:S(2)}) async-start(bf16[2,512,1024]{2,0,1:T(2,128)(2,1)} %copy.20), calls=%async_computation.1 | async-start | bytes 4194304 | tf_op jit(solution)/shard_map/all_to_all | solution.py:63
  114.3 0.1 copy.22
  114.5 0.1 reshape.69
  114.7 25.2 %all-to-all-done.1 = bf16[2,512,1024]{2,0,1:T(2,128)(2,1)S(1)} async-done(((bf16[2,512,1024]{2,0,1:T(2,128)(2,1)}), bf16[2,512,1024]{2,0,1:T(2,128)(2,1)S(1)}, u32[]{:S(2)}, u32[]{:S(2)}) %all-to-all-start.1) | async-done | bytes 2097184 | tf_op jit(solution)/shard_map/all_to_all | solution.py:63
  139.9 2.0 %copy.21 = bf16[2,16,32,1024]{3,2,0,1:T(8,128)(2,1)} copy(bf16[2,16,32,1024]{3,0,2,1:T(2,128)(2,1)S(1)} %bitcast.30) | data formatting | bytes 4194304 | tf_op jit(solution)/shard_map/all_to_all | solution.py:63
  141.9 5.5 %gather_fusion = bf16[512,1024]{1,0:T(8,128)(2,1)} fusion(bf16[1024,1024]{1,0:T(8,128)(2,1)} %bitcast.26, s32[1024]{0:T(1024)S(1)} %pad_clamp_fusion), kind=kCustom, calls=%fused_computation | custom fusion | bytes 2099200 | tf_op jit(solution)/shard_map/gather | solution.py:64
  147.4 2.3 %reshape.70 = bf16[256,2,1024]{2,1,0:T(2,128)(2,1)} reshape(bf16[512,1024]{1,0:T(8,128)(2,1)} %gather_fusion) | data formatting | bytes 2097152 | tf_op jit(solution)/shard_map/reshape | solution.py:64
  149.7 4.6 %reduce_sum.12 = bf16[256,1024]{1,0:T(8,128)(2,1)} reduce(bf16[256,2,1024]{2,1,0:T(2,128)(2,1)} %reshape.70, bf16[]{:T(256)} %constant.5.clone.1), dimensions={1}, to_apply=%region_0.0 | reduce | flops 262144 | bytes 1572866 | tf_op jit(solution)/shard_map/reduce_sum | solution.py:65
  154.3 17.6 %reduce-scatter.2.cloned.1.call-done = bf16[2,96,1536]{2,1,0:T(8,128)(2,1)} async-done(((bf16[2,1536,1536]{2,1,0:T(8,128)(2,1)}), bf16[2,96,1536]{2,1,0:T(8,128)(2,1)}) %reduce-scatter.2.cloned.1.call-update) | async-done | bytes 589840 | tf_op jit(solution)/shard_map/reduce_scatter | solution.py:76
  171.9 0.8 fusion.25
  172.6 0.9 slice.80
  173.6 0.8 maximum_convert_fusion
  174.3 2.0 %slice_convert_fusion = f32[2,64,1536]{2,1,0:T(8,128)} fusion(bf16[2,96,1536]{2,1,0:T(8,128)(2,1)} %reduce-scatter.2.cloned.1.call-done), kind=kLoop, calls=%fused_computation.29 | loop fusion | flops 196608 | bytes 1179648 | tf_op jit(solution)/shard_map/convert_element_type | solution.py:77
  (20 shorter events, 0.1 us)
Async XLA Ops:
  7.2 76.8 %copy-start = (bf16[2,768,1024]{2,1,0:T(8,128)(2,1)S(1)}, bf16[2,768,1024]{2,1,0:T(8,128)(2,1)}, u32[]{:S(2)}) copy-start(bf16[2,768,1024]{2,1,0:T(8,128)(2,1)} %param.13) | copy-start | bytes 9437188
  7.2 164.7 %reduce-scatter.2.cloned.1.call-start = ((), (), s32[]{:S(2)}) async-start(), calls=%async_computation.3 | async-start | bytes 10027008 | tf_op jit(solution)/shard_map/reduce_scatter | solution.py:76
  70.3 2.2 %slice-start = ((s8[6291456]{0:T(1024)(128)(4,1)}), s8[4194304]{0:T(1024)(128)(4,1)S(1)}, s32[]{:S(2)}) async-start(s8[6291456]{0:T(1024)(128)(4,1)} %bitcast.46), calls=%async_computation.4 | async-start | bytes 8388608
  71.1 2.3 %slice-start.1 = ((s8[6291456]{0:T(1024)(128)(4,1)}), s8[2097152]{0:T(1024)(128)(4,1)S(1)}, s32[]{:S(2)}) async-start(s8[6291456]{0:T(1024)(128)(4,1)} %bitcast.46), calls=%async_computation.5 | async-start | bytes 4194304
  83.6 2.8 %copy-start.2 = (f32[2,512,1536]{2,1,0:T(8,128)S(1)}, f32[2,512,1536]{2,1,0:T(8,128)}, u32[]{:S(2)}) copy-start(f32[2,512,1536]{2,1,0:T(8,128)} %fusion.27) | copy-start | bytes 18874372
  89.4 3.8 %copy-start.3 = (bf16[2,512,768]{2,1,0:T(8,128)(2,1)}, bf16[2,512,768]{2,1,0:T(8,128)(2,1)S(1)}, u32[]{:S(2)}) copy-start(bf16[2,512,768]{2,1,0:T(8,128)(2,1)S(1)} %get-tuple-element.5) | copy-start | bytes 4718596
  89.4 3.8 %copy-start.4 = (bf16[2,512,768]{2,1,0:T(8,128)(2,1)}, bf16[2,512,768]{2,1,0:T(8,128)(2,1)S(1)}, u32[]{:S(2)}) copy-start(bf16[2,512,768]{2,1,0:T(8,128)(2,1)S(1)} %get-tuple-element.6) | copy-start | bytes 4718596
  107.9 32.0 %all-to-all-start.1 = ((bf16[2,512,1024]{2,0,1:T(2,128)(2,1)}), bf16[2,512,1024]{2,0,1:T(2,128)(2,1)S(1)}, u32[]{:S(2)}, u32[]{:S(2)}) async-start(bf16[2,512,1024]{2,0,1:T(2,128)(2,1)} %copy.20), calls=%async_computation.1 | async-start | bytes 4194304 | tf_op jit(solution)/shard_map/all_to_all | solution.py:63
  141.9 34.4 %copy-start.1 = (bf16[2,768,1024]{2,1,0:T(8,128)(2,1)S(1)}, bf16[2,768,1024]{2,1,0:T(8,128)(2,1)}, u32[]{:S(2)}) copy-start(bf16[2,768,1024]{2,1,0:T(8,128)(2,1)} %param.13) | copy-start | bytes 9437188
Sparse Core Ops, SparseCore 0:
  97.3 74.4 reduce-scatter.1

commit v7 on v5

--- a/solution.py
+++ b/solution.py
@@ -7,9 +7,12 @@
 
 
 def recompute(input_slots, w_in, hidden_width):
-    gate_up = jnp.einsum("ksd,kdf->ksf", input_slots, w_in, preferred_element_type=jnp.float32)
-    gate = gate_up[:, :, :hidden_width]
-    upper = gate_up[:, :, hidden_width:]
+    gate = jnp.einsum(
+        "ksd,kdf->ksf", input_slots, w_in[:, :, :hidden_width], preferred_element_type=jnp.float32
+    )
+    upper = jnp.einsum(
+        "ksd,kdf->ksf", input_slots, w_in[:, :, hidden_width:], preferred_element_type=jnp.float32
+    )
     sigmoid_gate = jax.nn.sigmoid(gate)
     activated = gate * sigmoid_gate
     hidden = (activated * upper).astype(jnp.bfloat16)

time: 183 us -> 175 us (0.956)
  matrix products: 30.4 us -> 26 us
  local copies, waits for them, and re-layouts: 21.1 us -> 17.4 us
    unnamed x18 -> x16, local copies, waits for them, and re-layouts: 4.08 us -> 0.48 us
    dot_general x1, matrix products: 4.85 us -> 2.03 us  [per_device(): jnp.einsum('ksf,ksd->kfd', hidden, cotangent_slots, preferred_element_typ...]
    dot_general x1 -> x2, matrix products: 5.34 us -> 4.8 us  [the longest x1 3.01 us: recompute(): jnp.einsum('ksd,kdf->ksf', input_slots, w_in[:, :, :hidden_width], prefer...]
where the time goes in v7:
time: 175 us
  blocking collectives  55.5 us (32%)
  waiting for transfers between devices  43.1 us (25%)
  matrix products  26 us (15%)
  local copies, waits for them, and re-layouts  17.4 us (10%)
  between operations  14.3 us (8%)
  other arithmetic  12.3 us (7%)
  starting transfers between devices  6.27 us (4%)
    all_to_all x1, blocking collectives, per_device(): lax.all_to_all(send, 'expert', split_axis=0, concat_axis=0, tiled=True)  55.5 us
    all_to_all x1, waiting for transfers between devices, per_device(): lax.all_to_all(returned, 'expert', split_axis=1, concat_axis=0, tiled=True)  25.2 us
    reduce_scatter x1, waiting for transfers between devices, per_device(): summed = lax.psum_scatter(parts, 'dp', scatter_dimension=1, tiled=True)  17.9 us
    dot_general x1, matrix products, per_device(): jnp.einsum('ksf,kdf->ksd', grad_pair, w_in, preferred_element_type=jnp.fl...  7.19 us
    all_to_all x1, starting transfers between devices, per_device(): lax.all_to_all(returned, 'expert', split_axis=1, concat_axis=0, tiled=True)  6.23 us
    gather x1, local copies, waits for them, and re-layouts, per_device(): arrived.reshape(-1, width)[destination].reshape(token_count, TOP, width)  5.53 us
    reduce_sum x1, other arithmetic, per_device(): input_grad = jnp.sum(rows.astype(jnp.float32), axis=1).astype(jnp.bfloat16)  4.59 us
    concatenate x1, other arithmetic, per_device(): jnp.concatenate([part_in, packed], axis=2)  4.05 us
  transfers between devices with their start and end apart: 2, of which 2 were waited for; matrix products, arithmetic and copies ran while one was open for 14% of the time, Pallas kernels for 0%

profile of v7, /device:TPU:4, one launch (start us, length us, event | category | flops | bytes accessed | tf_op | source)
XLA Modules:
  0.0 174.8 jit_solution(13041412101257724786)
XLA Ops:
  7.2 0.0 reduce-scatter.2.cloned.1.call-start
  7.2 0.9 multiply_add_fusion
  8.1 2.4 %fusion.13 = f32[2048,1024]{1,0:T(8,128)S(1)} fusion(bf16[256,1024]{1,0:T(8,128)(2,1)} %param.7, s32[256]{0:T(256)S(1)} %bitcast.44, s32[256]{0:T(256)S(1)} %bitcast.42), kind=kOutput, calls=%fused_computation.30 | convolution fusion | flops 1077936128 | bytes 8914944 | tf_op jit(solution)/shard_map/dot_general | solution.py:40
  10.5 1.3 fusion.7
  11.9 2.6 %add_convert_fusion = bf16[2048,1024]{1,0:T(8,128)(2,1)S(1)} fusion(f32[2048,1024]{1,0:T(8,128)S(1)} %fusion.13, f32[2048,1024]{1,0:T(8,128)S(1)} %fusion.7, s32[256]{0:T(256)S(1)} %broadcast_add_fusion, bf16[256,1024]{1,0:T(8,128)(2,1)} %param.8, f32[256]{0:T(256)S(1)} %bitcast.46), kind=kOutput, calls=%fused_computation.2 | convolution fusion | flops 1081344000 | bytes 21497856 | tf_op jit(solution)/shard_map/dot_general | solution.py:44
  14.5 55.5 %all_to_all.20 = bf16[32,2,32,1024]{3,2,1,0:T(8,128)(2,1)S(1)} all-to-all(bf16[32,2,32,1024]{3,2,1,0:T(8,128)(2,1)S(1)} %bitcast.31), channel_id=1, replica_groups=mesh['dp'=16,'expert'=16] {'expert'}, dimensions={0} | all-to-all | bytes 8388608 | tf_op jit(solution)/shard_map/all_to_all | solution.py:46
  70.0 0.8 copy.28
  70.8 0.6 fusion.28
  71.4 1.9 %fusion.32 = f32[2,512,768]{2,1,0:T(8,128)S(1)} fusion(bf16[2,512,1024]{2,1,0:T(8,128)(2,1)S(1)} %bitcast.39, bf16[2,768,1024]{2,1,0:T(8,128)(2,1)S(1)} %copy-done), kind=kOutput, calls=%fused_computation.54 | convolution fusion | flops 1610612736 | bytes 8388608 | tf_op jit(solution)/shard_map/ksd,kfd->ksf/dot_general | solution.py:51
  73.3 0.4 slice-done.1
  73.8 1.8 %fusion.3 = f32[2,512,768]{2,1,0:T(8,128)S(1)} fusion(bf16[2,512,1024]{2,1,0:T(8,128)(2,1)S(1)} %bitcast.36, bf16[2,1024,1536]{2,1,0:T(8,128)(2,1)S(1)} %bitcast.49), kind=kOutput, calls=%fused_computation.13 | convolution fusion | flops 1610612736 | bytes 8388608 | tf_op jit(solution)/shard_map/ksd,kdf->ksf/dot_general | solution.py:13
  75.6 3.0 %multiply_convert_fusion.2 = (bf16[2,512,768]{2,1,0:T(8,128)(2,1)S(1)}, bf16[2,512,768]{2,1,0:T(8,128)(2,1)S(1)}, f32[2,512,768]{2,1,0:T(8,128)S(1)}) fusion(f32[2,512,768]{2,1,0:T(8,128)S(1)} %fusion.32, f32[2,512,768]{2,1,0:T(8,128)S(1)} %fusion.3, bf16[2,512,1024]{2,1,0:T(8,128)(2,1)S(1)} %bitcast.37, bf16[2,1024,1536]{2,1,0:T(8,128)(2,1)S(1)} %bitcast.49), kind=kOutput, calls=%fused_computation.8 | convolution fusion | flops 1620836352 | bytes 17825792 | tf_op jit(solution)/shard_map/ksd,kdf->ksf/dot_general | solution.py:10
  78.6 2.0 %convolution_convert_fusion.1 = bf16[2,768,1024]{2,1,0:T(8,128)(2,1)S(1)} fusion(bf16[2,512,1024]{2,1,0:T(8,128)(2,1)S(1)} %bitcast.40, f32[2,512,768]{2,1,0:T(8,128)S(1)} %fusion.3, f32[2,512,768]{2,1,0:T(8,128)S(1)} %get-tuple-element.17), kind=kOutput, calls=%fused_computation.15 | convolution fusion | flops 1616904192 | bytes 11534336 | tf_op jit(solution)/shard_map/ksf,ksd->kfd/dot_general | solution.py:54
  80.6 0.1 fusion.29
  80.8 0.2 slice.74
  81.0 3.8 %convolution_convert_fusion = bf16[2,1024,1536]{2,1,0:T(8,128)(2,1)S(1)} fusion(bf16[2,512,1024]{2,1,0:T(8,128)(2,1)S(1)} %bitcast.38, bf16[2,512,768]{2,1,0:T(8,128)(2,1)S(1)} %get-tuple-element.6, bf16[2,512,768]{2,1,0:T(8,128)(2,1)S(1)} %get-tuple-element.5), kind=kOutput, calls=%fused_computation.3 | convolution fusion | flops 3230662656 | bytes 11534336 | tf_op jit(solution)/shard_map/ksd,ksf->kdf/dot_general | solution.py:60
  84.8 4.1 %maximum_maximum_fusion = bf16[2,16,96,1536]{3,2,1,0:T(8,128)(2,1)} fusion(bf16[2,16,16,512]{3,2,1,0:T(8,128)(2,1)S(1)} %get-tuple-element.10, bf16[2,16,16,512]{3,2,1,0:T(8,128)(2,1)S(1)} %get-tuple-element.9, bf16[2,16,32,1024]{3,2,1,0:T(8,128)(2,1)S(1)} %slice.74, bf16[2,16,64,1536]{3,2,1,0:T(8,128)(2,1)S(1)} %bitcast.33), kind=kLoop, calls=%fused_computation.1 | loop fusion | flops 37748736 | bytes 18874368 | tf_op jit(solution)/shard_map/concatenate | solution.py:76
  88.8 7.2 %fusion.9 = bf16[2,512,1024]{2,1,0:T(8,128)(2,1)S(1)} fusion(bf16[2,1024,1536]{2,1,0:T(8,128)(2,1)} %param.12, bf16[2,512,768]{2,1,0:T(8,128)(2,1)} %copy-done.5, bf16[2,512,768]{2,1,0:T(8,128)(2,1)} %copy-done.4), kind=kOutput, calls=%fused_computation.24 | convolution fusion | flops 3228565504 | bytes 11534336 | tf_op jit(solution)/shard_map/ksf,kdf->ksd/dot_general | solution.py:61
  96.0 3.5 %copy.20 = bf16[2,512,1024]{2,0,1:T(2,128)(2,1)} copy(bf16[2,512,1024]{2,1,0:T(8,128)(2,1)S(1)} %fusion.9) | data formatting | bytes 4194304 | tf_op jit(solution)/shard_map/convert_element_type | solution.py:63
  99.5 6.2 %all-to-all-start.1 = ((bf16[2,512,1024]{2,0,1:T(2,128)(2,1)}), bf16[2,512,1024]{2,0,1:T(2,128)(2,1)S(1)}, u32[]{:S(2)}, u32[]{:S(2)}) async-start(bf16[2,512,1024]{2,0,1:T(2,128)(2,1)} %copy.20), calls=%async_computation.1 | async-start | bytes 4194304 | tf_op jit(solution)/shard_map/all_to_all | solution.py:64
  105.7 0.1 copy.22
  105.9 0.1 reshape.83
  106.0 25.2 %all-to-all-done.1 = bf16[2,512,1024]{2,0,1:T(2,128)(2,1)S(1)} async-done(((bf16[2,512,1024]{2,0,1:T(2,128)(2,1)}), bf16[2,512,1024]{2,0,1:T(2,128)(2,1)S(1)}, u32[]{:S(2)}, u32[]{:S(2)}) %all-to-all-start.1) | async-done | bytes 2097184 | tf_op jit(solution)/shard_map/all_to_all | solution.py:64
  131.3 2.0 %copy.21 = bf16[2,16,32,1024]{3,2,0,1:T(8,128)(2,1)} copy(bf16[2,16,32,1024]{3,0,2,1:T(2,128)(2,1)S(1)} %bitcast.32) | data formatting | bytes 4194304 | tf_op jit(solution)/shard_map/all_to_all | solution.py:64
  133.3 5.5 %gather_fusion = bf16[512,1024]{1,0:T(8,128)(2,1)} fusion(bf16[1024,1024]{1,0:T(8,128)(2,1)} %bitcast.27, s32[1024]{0:T(1024)S(1)} %pad_clamp_fusion), kind=kCustom, calls=%fused_computation | custom fusion | bytes 2099200 | tf_op jit(solution)/shard_map/gather | solution.py:65
  138.8 2.3 %reshape.84 = bf16[256,2,1024]{2,1,0:T(2,128)(2,1)} reshape(bf16[512,1024]{1,0:T(8,128)(2,1)} %gather_fusion) | data formatting | bytes 2097152 | tf_op jit(solution)/shard_map/reshape | solution.py:65
  141.1 4.6 %reduce_sum.12 = bf16[256,1024]{1,0:T(8,128)(2,1)} reduce(bf16[256,2,1024]{2,1,0:T(2,128)(2,1)} %reshape.84, bf16[]{:T(256)} %constant.4.clone.1), dimensions={1}, to_apply=%region_0.0 | reduce | flops 262144 | bytes 1572866 | tf_op jit(solution)/shard_map/reduce_sum | solution.py:66
  145.7 17.9 %reduce-scatter.2.cloned.1.call-done = bf16[2,96,1536]{2,1,0:T(8,128)(2,1)} async-done(((bf16[2,1536,1536]{2,1,0:T(8,128)(2,1)}), bf16[2,96,1536]{2,1,0:T(8,128)(2,1)}) %reduce-scatter.2.cloned.1.call-update) | async-done | bytes 589840 | tf_op jit(solution)/shard_map/reduce_scatter | solution.py:77
  163.5 0.8 fusion.30
  164.3 0.9 slice.78
  165.2 0.8 maximum_convert_fusion
  166.0 2.0 %slice_convert_fusion = f32[2,64,1536]{2,1,0:T(8,128)} fusion(bf16[2,96,1536]{2,1,0:T(8,128)(2,1)} %reduce-scatter.2.cloned.1.call-done), kind=kLoop, calls=%fused_computation.37 | loop fusion | flops 196608 | bytes 1179648 | tf_op jit(solution)/shard_map/convert_element_type | solution.py:78
  (23 shorter events, 0.1 us)
Async XLA Ops:
  7.2 64.2 %copy-start = (bf16[2,768,1024]{2,1,0:T(8,128)(2,1)S(1)}, bf16[2,768,1024]{2,1,0:T(8,128)(2,1)}, u32[]{:S(2)}) copy-start(bf16[2,768,1024]{2,1,0:T(8,128)(2,1)} %param.13) | copy-start | bytes 9437188
  7.2 156.4 %reduce-scatter.2.cloned.1.call-start = ((), (), s32[]{:S(2)}) async-start(), calls=%async_computation.3 | async-start | bytes 10027008 | tf_op jit(solution)/shard_map/reduce_scatter | solution.py:77
  8.1 2.4 %copy-start.3 = (f32[256,2]{0,1:T(2,128)S(1)}, f32[256,2]{0,1:T(2,128)}, u32[]{:S(2)}) copy-start(f32[256,2]{0,1:T(2,128)} %param.9) | copy-start | bytes 6148
  8.1 2.4 %copy-start.2 = (bf16[256,1024]{1,0:T(8,128)(2,1)S(1)}, bf16[256,1024]{1,0:T(8,128)(2,1)}, u32[]{:S(2)}) copy-start(bf16[256,1024]{1,0:T(8,128)(2,1)} %param.8) | copy-start | bytes 1572868
  70.8 2.5 %slice-start = ((s8[6291456]{0:T(1024)(128)(4,1)}), s8[2097152]{0:T(1024)(128)(4,1)S(1)}, s32[]{:S(2)}) async-start(s8[6291456]{0:T(1024)(128)(4,1)} %bitcast.48), calls=%async_computation.4 | async-start | bytes 4194304
  71.4 2.4 %slice-start.1 = ((s8[6291456]{0:T(1024)(128)(4,1)}), s8[4194304]{0:T(1024)(128)(4,1)S(1)}, s32[]{:S(2)}) async-start(s8[6291456]{0:T(1024)(128)(4,1)} %bitcast.48), calls=%async_computation.5 | async-start | bytes 8388608
  78.6 2.4 %copy-start.4 = (bf16[2,512,768]{2,1,0:T(8,128)(2,1)}, bf16[2,512,768]{2,1,0:T(8,128)(2,1)S(1)}, u32[]{:S(2)}) copy-start(bf16[2,512,768]{2,1,0:T(8,128)(2,1)S(1)} %get-tuple-element.5) | copy-start | bytes 4718596
  78.6 2.4 %copy-start.5 = (bf16[2,512,768]{2,1,0:T(8,128)(2,1)}, bf16[2,512,768]{2,1,0:T(8,128)(2,1)S(1)}, u32[]{:S(2)}) copy-start(bf16[2,512,768]{2,1,0:T(8,128)(2,1)S(1)} %get-tuple-element.6) | copy-start | bytes 4718596
  99.5 31.8 %all-to-all-start.1 = ((bf16[2,512,1024]{2,0,1:T(2,128)(2,1)}), bf16[2,512,1024]{2,0,1:T(2,128)(2,1)S(1)}, u32[]{:S(2)}, u32[]{:S(2)}) async-start(bf16[2,512,1024]{2,0,1:T(2,128)(2,1)} %copy.20), calls=%async_computation.1 | async-start | bytes 4194304 | tf_op jit(solution)/shard_map/all_to_all | solution.py:64
  133.3 34.7 %copy-start.1 = (bf16[2,768,1024]{2,1,0:T(8,128)(2,1)S(1)}, bf16[2,768,1024]{2,1,0:T(8,128)(2,1)}, u32[]{:S(2)}) copy-start(bf16[2,768,1024]{2,1,0:T(8,128)(2,1)} %param.13) | copy-start | bytes 9437188
Sparse Core Ops, SparseCore 0:
  88.9 74.5 reduce-scatter.1

commit v8 on v7

--- a/solution.py
+++ b/solution.py
@@ -31,21 +31,19 @@
     combine = (first, 1.0 - first)
     cotangent_wide = cotangent.astype(jnp.float32)
     destination = (expert_ids * capacity + slot_pos).reshape(-1)
-    target = expert_ids * (2 * capacity) + slot_pos
-    buffer_row = lax.broadcasted_iota(jnp.int32, (experts_all * 2 * capacity, token_count), 0)
-    picks = []
-    for k in range(TOP):
-        picks.append((buffer_row == target[None, :, k]).astype(jnp.bfloat16))
-    token_picks = picks[0] + picks[1]
-    send = jnp.dot(token_picks, tokens, preferred_element_type=jnp.float32)
+    target = expert_ids * capacity + slot_pos
+    buffer_row = lax.broadcasted_iota(jnp.int32, (experts_all * capacity, token_count), 0)
+    picks = [(buffer_row == target[None, :, k]).astype(jnp.bfloat16) for k in range(TOP)]
+    send_tokens = jnp.dot(picks[0] + picks[1], tokens, preferred_element_type=jnp.float32)
+    send_scaled = 0.0
     for k in range(TOP):
         scaled = (combine[k][:, None] * cotangent_wide).astype(jnp.bfloat16)
-        shifted = (buffer_row == target[None, :, k] + capacity).astype(jnp.bfloat16)
-        send = send + jnp.dot(shifted, scaled, preferred_element_type=jnp.float32)
-    send = send.astype(jnp.bfloat16).reshape(experts_all, 2, capacity, width)
-    got = lax.all_to_all(send, "expert", split_axis=0, concat_axis=0, tiled=True)
-    got = got.reshape(n_expert, local_experts, 2, capacity, width)
-    got = jnp.transpose(got, (2, 1, 0, 3, 4)).reshape(2, local_experts, n_expert * capacity, width)
+        send_scaled = send_scaled + jnp.dot(picks[k], scaled, preferred_element_type=jnp.float32)
+    send = jnp.stack([send_tokens, send_scaled]).astype(jnp.bfloat16)
+    send = send.reshape(2, experts_all, capacity, width)
+    got = lax.all_to_all(send, "expert", split_axis=1, concat_axis=1, tiled=True)
+    got = got.reshape(2, n_expert, local_experts, capacity, width)
+    got = jnp.swapaxes(got, 1, 2).reshape(2, local_experts, n_expert * capacity, width)
     input_slots, cotangent_slots = got[0], got[1]
     gate, upper, sigmoid_gate, activated, hidden = recompute(input_slots, w_in, hidden_width)
     grad_hidden = jnp.einsum(

time: 175 us -> 178 us (1.017)
  local copies, waits for them, and re-layouts: 17.4 us -> 19.7 us
    unnamed x16 -> x14, local copies, waits for them, and re-layouts: 0.48 us -> 2.75 us
    dot_general x3, matrix products: 6.31 us -> 4.47 us  [the longest x2 2.65 us: per_device(): jnp.dot(picks[k], scaled, preferred_element_type=jnp.float32)]
where the time goes in v8:
time: 178 us; the launch traced here: 177 us
  blocking collectives  55.5 us (31%)
  waiting for transfers between devices  43.1 us (24%)
  matrix products  25.1 us (14%)
  local copies, waits for them, and re-layouts  19.7 us (11%)
  between operations  14.2 us (8%)
  other arithmetic  13.4 us (8%)
  starting transfers between devices  6.28 us (4%)
    all_to_all x1, blocking collectives, per_device(): lax.all_to_all(send, 'expert', split_axis=1, concat_axis=1, tiled=True)  55.5 us
    all_to_all x1, waiting for transfers between devices, per_device(): lax.all_to_all(returned, 'expert', split_axis=1, concat_axis=0, tiled=True)  25.2 us
    reduce_scatter x1, waiting for transfers between devices, per_device(): summed = lax.psum_scatter(parts, 'dp', scatter_dimension=1, tiled=True)  17.9 us
    dot_general x1, matrix products, per_device(): jnp.einsum('ksf,kdf->ksd', grad_pair, w_in, preferred_element_type=jnp.fl...  7.18 us
    all_to_all x1, starting transfers between devices, per_device(): lax.all_to_all(returned, 'expert', split_axis=1, concat_axis=0, tiled=True)  6.24 us
    gather x1, local copies, waits for them, and re-layouts, per_device(): arrived.reshape(-1, width)[destination].reshape(token_count, TOP, width)  5.52 us
    reduce_sum x1, other arithmetic, per_device(): input_grad = jnp.sum(rows.astype(jnp.float32), axis=1).astype(jnp.bfloat16)  4.59 us
    concatenate x1, other arithmetic, per_device(): jnp.concatenate([part_in, packed], axis=2)  4.05 us
  transfers between devices with their start and end apart: 2, of which 2 were waited for; matrix products, arithmetic and copies ran while one was open for 14% of the time, Pallas kernels for 0%

profile of v8, /device:TPU:4, one launch (start us, length us, event | category | flops | bytes accessed | tf_op | source)
XLA Modules:
  0.0 177.2 jit_solution(635537059419935940)
XLA Ops:
  7.2 0.9 multiply_add_fusion
  8.1 0.8 broadcast_subtract_fusion
  8.9 1.8 %convolution_convert_fusion.2 = bf16[1024,1024]{1,0:T(8,128)(2,1)S(1)} fusion(bf16[256,1024]{1,0:T(8,128)(2,1)} %param.7, s32[256]{0:T(256)S(1)} %bitcast.47, s32[256]{0:T(256)S(1)} %bitcast.49), kind=kOutput, calls=%fused_computation.19 | convolution fusion | flops 540016640 | bytes 2623488 | tf_op jit(solution)/shard_map/dot_general | solution.py:37
  10.7 1.8 %fusion.10 = f32[1024,1024]{1,0:T(8,128)S(1)} fusion(bf16[256,1024]{1,0:T(8,128)(2,1)} %param.8, f32[256]{0:T(256)S(1)} %bitcast.53, s32[256]{0:T(256)S(1)} %bitcast.50), kind=kOutput, calls=%fused_computation.27 | convolution fusion | flops 537919488 | bytes 4720640 | tf_op jit(solution)/shard_map/dot_general | solution.py:41
  12.6 0.8 add_convert_fusion
  13.4 0.4 pad_maximum_fusion
  13.8 55.5 %all_to_all.20 = bf16[2,32,32,1024]{3,2,0,1:T(8,128)(2,1)S(1)} all-to-all(bf16[2,32,32,1024]{3,2,0,1:T(8,128)(2,1)S(1)} %pad_maximum_fusion), channel_id=1, replica_groups=mesh['dp'=16,'expert'=16] {'expert'}, dimensions={1} | all-to-all | bytes 8388608 | tf_op jit(solution)/shard_map/all_to_all | solution.py:44
  69.3 0.8 copy.30
  70.1 0.6 fusion.27
  70.7 0.8 slice-done
  71.4 0.9 slice-done.1
  72.3 1.8 %fusion.3 = f32[2,512,768]{2,1,0:T(8,128)S(1)} fusion(bf16[2,512,1024]{2,1,0:T(8,128)(2,1)S(1)} %bitcast.42, bf16[2,1024,1536]{2,1,0:T(8,128)(2,1)S(1)} %bitcast.55), kind=kOutput, calls=%fused_computation.14 | convolution fusion | flops 1610612736 | bytes 8388608 | tf_op jit(solution)/shard_map/ksd,kdf->ksf/dot_general | solution.py:13
  74.2 1.9 %fusion.31 = f32[2,512,768]{2,1,0:T(8,128)S(1)} fusion(bf16[2,512,1024]{2,1,0:T(8,128)(2,1)S(1)} %bitcast.45, bf16[2,768,1024]{2,1,0:T(8,128)(2,1)S(1)} %copy-done), kind=kOutput, calls=%fused_computation.50 | convolution fusion | flops 1610612736 | bytes 8388608 | tf_op jit(solution)/shard_map/ksd,kfd->ksf/dot_general | solution.py:49
  76.1 3.9 %multiply_convert_fusion.2 = (bf16[2,512,768]{2,1,0:T(8,128)(2,1)S(1)}, bf16[2,512,768]{2,1,0:T(8,128)(2,1)}, f32[2,512,768]{2,1,0:T(8,128)S(1)}) fusion(f32[2,512,768]{2,1,0:T(8,128)S(1)} %fusion.31, f32[2,512,768]{2,1,0:T(8,128)S(1)} %fusion.3, bf16[2,512,1024]{2,1,0:T(8,128)(2,1)S(1)} %bitcast.43, bf16[2,1024,1536]{2,1,0:T(8,128)(2,1)S(1)} %bitcast.55), kind=kOutput, calls=%fused_computation.9 | convolution fusion | flops 1620836352 | bytes 17825792 | tf_op jit(solution)/shard_map/ksd,kdf->ksf/dot_general | solution.py:10
  80.0 2.1 %convolution_convert_fusion.1 = bf16[2,768,1024]{2,1,0:T(8,128)(2,1)S(1)} fusion(bf16[2,512,1024]{2,1,0:T(8,128)(2,1)S(1)} %bitcast.46, f32[2,512,768]{2,1,0:T(8,128)S(1)} %fusion.3, f32[2,512,768]{2,1,0:T(8,128)S(1)} %get-tuple-element.15), kind=kOutput, calls=%fused_computation.16 | convolution fusion | flops 1616904192 | bytes 11534336 | tf_op jit(solution)/shard_map/ksf,ksd->kfd/dot_general | solution.py:52
  82.2 0.2 slice.72
  82.4 1.1 copy-done.4
  83.4 3.7 %convolution_convert_fusion = bf16[2,1024,1536]{2,1,0:T(8,128)(2,1)S(1)} fusion(bf16[2,512,1024]{2,1,0:T(8,128)(2,1)S(1)} %bitcast.44, bf16[2,512,768]{2,1,0:T(8,128)(2,1)S(1)} %copy-done.4, bf16[2,512,768]{2,1,0:T(8,128)(2,1)S(1)} %get-tuple-element.5), kind=kOutput, calls=%fused_computation.2 | convolution fusion | flops 3230662656 | bytes 11534336 | tf_op jit(solution)/shard_map/ksd,ksf->kdf/dot_general | solution.py:58
  87.2 4.1 %maximum_maximum_fusion = bf16[2,16,96,1536]{3,2,1,0:T(8,128)(2,1)} fusion(bf16[2,16,16,512]{3,2,1,0:T(8,128)(2,1)S(1)} %get-tuple-element.10, bf16[2,16,16,512]{3,2,1,0:T(8,128)(2,1)S(1)} %get-tuple-element.9, bf16[2,16,32,1024]{3,2,1,0:T(8,128)(2,1)S(1)} %slice.72, bf16[2,16,64,1536]{3,2,1,0:T(8,128)(2,1)S(1)} %bitcast.39), kind=kLoop, calls=%fused_computation.1 | loop fusion | flops 37748736 | bytes 18874368 | tf_op jit(solution)/shard_map/concatenate | solution.py:74
  91.3 7.2 %fusion.6 = bf16[2,512,1024]{2,1,0:T(8,128)(2,1)S(1)} fusion(bf16[2,1024,1536]{2,1,0:T(8,128)(2,1)} %param.12, bf16[2,512,768]{2,1,0:T(8,128)(2,1)} %get-tuple-element.6, bf16[2,512,768]{2,1,0:T(8,128)(2,1)} %copy-done.3), kind=kOutput, calls=%fused_computation.18 | convolution fusion | flops 3228565504 | bytes 11534336 | tf_op jit(solution)/shard_map/ksf,kdf->ksd/dot_general | solution.py:59
  98.5 3.5 %copy.22 = bf16[2,512,1024]{2,0,1:T(2,128)(2,1)} copy(bf16[2,512,1024]{2,1,0:T(8,128)(2,1)S(1)} %fusion.6) | data formatting | bytes 4194304 | tf_op jit(solution)/shard_map/convert_element_type | solution.py:61
  101.9 6.2 %all-to-all-start.1 = ((bf16[2,512,1024]{2,0,1:T(2,128)(2,1)}), bf16[2,512,1024]{2,0,1:T(2,128)(2,1)S(1)}, u32[]{:S(2)}, u32[]{:S(2)}) async-start(bf16[2,512,1024]{2,0,1:T(2,128)(2,1)} %copy.22), calls=%async_computation.1 | async-start | bytes 4194304 | tf_op jit(solution)/shard_map/all_to_all | solution.py:62
  108.5 25.2 %all-to-all-done.1 = bf16[2,512,1024]{2,0,1:T(2,128)(2,1)S(1)} async-done(((bf16[2,512,1024]{2,0,1:T(2,128)(2,1)}), bf16[2,512,1024]{2,0,1:T(2,128)(2,1)S(1)}, u32[]{:S(2)}, u32[]{:S(2)}) %all-to-all-start.1) | async-done | bytes 2097184 | tf_op jit(solution)/shard_map/all_to_all | solution.py:62
  133.7 2.0 %copy.23 = bf16[2,16,32,1024]{3,2,0,1:T(8,128)(2,1)} copy(bf16[2,16,32,1024]{3,0,2,1:T(2,128)(2,1)S(1)} %bitcast.36) | data formatting | bytes 4194304 | tf_op jit(solution)/shard_map/all_to_all | solution.py:62
  135.7 5.5 %gather_fusion = bf16[512,1024]{1,0:T(8,128)(2,1)} fusion(bf16[1024,1024]{1,0:T(8,128)(2,1)} %bitcast.32, s32[1024]{0:T(1024)S(1)} %pad_clamp_fusion), kind=kCustom, calls=%fused_computation | custom fusion | bytes 2099200 | tf_op jit(solution)/shard_map/gather | solution.py:63
  141.2 2.3 %reshape.73 = bf16[256,2,1024]{2,1,0:T(2,128)(2,1)} reshape(bf16[512,1024]{1,0:T(8,128)(2,1)} %gather_fusion) | data formatting | bytes 2097152 | tf_op jit(solution)/shard_map/reshape | solution.py:63
  143.5 4.6 %reduce_sum.12 = bf16[256,1024]{1,0:T(8,128)(2,1)} reduce(bf16[256,2,1024]{2,1,0:T(2,128)(2,1)} %reshape.73, bf16[]{:T(256)} %constant.4.clone.1), dimensions={1}, to_apply=%region_0.0 | reduce | flops 262144 | bytes 1572866 | tf_op jit(solution)/shard_map/reduce_sum | solution.py:64
  148.1 17.9 %reduce-scatter.2.cloned.1.call-done = bf16[2,96,1536]{2,1,0:T(8,128)(2,1)} async-done(((bf16[2,1536,1536]{2,1,0:T(8,128)(2,1)}), bf16[2,96,1536]{2,1,0:T(8,128)(2,1)}) %reduce-scatter.2.cloned.1.call-update) | async-done | bytes 589840 | tf_op jit(solution)/shard_map/reduce_scatter | solution.py:75
  165.9 0.8 fusion.29
  166.7 0.9 slice.76
  167.6 0.8 maximum_convert_fusion
  168.4 2.0 %slice_convert_fusion = f32[2,64,1536]{2,1,0:T(8,128)} fusion(bf16[2,96,1536]{2,1,0:T(8,128)(2,1)} %reduce-scatter.2.cloned.1.call-done), kind=kLoop, calls=%fused_computation.36 | loop fusion | flops 196608 | bytes 1179648 | tf_op jit(solution)/shard_map/convert_element_type | solution.py:76
  (20 shorter events, 0.5 us)
Async XLA Ops:
  7.2 67.0 %copy-start = (bf16[2,768,1024]{2,1,0:T(8,128)(2,1)S(1)}, bf16[2,768,1024]{2,1,0:T(8,128)(2,1)}, u32[]{:S(2)}) copy-start(bf16[2,768,1024]{2,1,0:T(8,128)(2,1)} %param.13) | copy-start | bytes 9437188
  7.2 158.8 %reduce-scatter.2.cloned.1.call-start = ((), (), s32[]{:S(2)}) async-start(), calls=%async_computation.3 | async-start | bytes 10027008 | tf_op jit(solution)/shard_map/reduce_scatter | solution.py:75
  8.9 3.7 %copy-start.2 = (bf16[256,1024]{1,0:T(8,128)(2,1)S(1)}, bf16[256,1024]{1,0:T(8,128)(2,1)}, u32[]{:S(2)}) copy-start(bf16[256,1024]{1,0:T(8,128)(2,1)} %param.8) | copy-start | bytes 1572868
  69.3 2.2 %slice-start = ((s8[6291456]{0:T(1024)(128)(4,1)}), s8[4194304]{0:T(1024)(128)(4,1)S(1)}, s32[]{:S(2)}) async-start(s8[6291456]{0:T(1024)(128)(4,1)} %bitcast.54), calls=%async_computation.4 | async-start | bytes 8388608
  70.1 2.3 %slice-start.1 = ((s8[6291456]{0:T(1024)(128)(4,1)}), s8[2097152]{0:T(1024)(128)(4,1)S(1)}, s32[]{:S(2)}) async-start(s8[6291456]{0:T(1024)(128)(4,1)} %bitcast.54), calls=%async_computation.5 | async-start | bytes 4194304
  80.0 2.4 %copy-start.3 = (bf16[2,512,768]{2,1,0:T(8,128)(2,1)}, bf16[2,512,768]{2,1,0:T(8,128)(2,1)S(1)}, u32[]{:S(2)}) copy-start(bf16[2,512,768]{2,1,0:T(8,128)(2,1)S(1)} %get-tuple-element.5) | copy-start | bytes 4718596
  82.0 1.4 copy-start.4
  101.9 31.8 %all-to-all-start.1 = ((bf16[2,512,1024]{2,0,1:T(2,128)(2,1)}), bf16[2,512,1024]{2,0,1:T(2,128)(2,1)S(1)}, u32[]{:S(2)}, u32[]{:S(2)}) async-start(bf16[2,512,1024]{2,0,1:T(2,128)(2,1)} %copy.22), calls=%async_computation.1 | async-start | bytes 4194304 | tf_op jit(solution)/shard_map/all_to_all | solution.py:62
  135.7 34.7 %copy-start.1 = (bf16[2,768,1024]{2,1,0:T(8,128)(2,1)S(1)}, bf16[2,768,1024]{2,1,0:T(8,128)(2,1)}, u32[]{:S(2)}) copy-start(bf16[2,768,1024]{2,1,0:T(8,128)(2,1)} %param.13) | copy-start | bytes 9437188
Sparse Core Ops, SparseCore 0:
  91.4 74.5 reduce-scatter.1

commit v9 on v7

--- a/solution.py
+++ b/solution.py
@@ -9,10 +9,10 @@
 def recompute(input_slots, w_in, hidden_width):
     gate = jnp.einsum(
         "ksd,kdf->ksf", input_slots, w_in[:, :, :hidden_width], preferred_element_type=jnp.float32
-    )
+    ).astype(jnp.bfloat16).astype(jnp.float32)
     upper = jnp.einsum(
         "ksd,kdf->ksf", input_slots, w_in[:, :, hidden_width:], preferred_element_type=jnp.float32
-    )
+    ).astype(jnp.bfloat16).astype(jnp.float32)
     sigmoid_gate = jax.nn.sigmoid(gate)
     activated = gate * sigmoid_gate
     hidden = (activated * upper).astype(jnp.bfloat16)

time: 175 us -> 176 us (level)
  no operation moved by 1% of the time
where the time goes in v9:
time: 176 us
  blocking collectives  55.5 us (32%)
  waiting for transfers between devices  43 us (24%)
  matrix products  25.8 us (15%)
  local copies, waits for them, and re-layouts  18.8 us (11%)
  between operations  14.3 us (8%)
  other arithmetic  12.2 us (7%)
  starting transfers between devices  6.27 us (4%)
    all_to_all x1, blocking collectives, per_device(): lax.all_to_all(send, 'expert', split_axis=0, concat_axis=0, tiled=True)  55.5 us
    all_to_all x1, waiting for transfers between devices, per_device(): lax.all_to_all(returned, 'expert', split_axis=1, concat_axis=0, tiled=True)  25.2 us
    reduce_scatter x1, waiting for transfers between devices, per_device(): summed = lax.psum_scatter(parts, 'dp', scatter_dimension=1, tiled=True)  17.8 us
    dot_general x1, matrix products, per_device(): jnp.einsum('ksf,kdf->ksd', grad_pair, w_in, preferred_element_type=jnp.fl...  7.19 us
    all_to_all x1, starting transfers between devices, per_device(): lax.all_to_all(returned, 'expert', split_axis=1, concat_axis=0, tiled=True)  6.23 us
    gather x1, local copies, waits for them, and re-layouts, per_device(): arrived.reshape(-1, width)[destination].reshape(token_count, TOP, width)  5.53 us
    reduce_sum x1, other arithmetic, per_device(): input_grad = jnp.sum(rows.astype(jnp.float32), axis=1).astype(jnp.bfloat16)  4.59 us
    concatenate x1, other arithmetic, per_device(): jnp.concatenate([part_in, packed], axis=2)  4.03 us
  transfers between devices with their start and end apart: 2, of which 2 were waited for; matrix products, arithmetic and copies ran while one was open for 14% of the time, Pallas kernels for 0%

profile of v9, /device:TPU:4, one launch (start us, length us, event | category | flops | bytes accessed | tf_op | source)
XLA Modules:
  0.0 175.8 jit_solution(10531892363133639638)
XLA Ops:
  7.2 0.0 reduce-scatter.2.cloned.1.call-start
  7.2 0.9 multiply_add_fusion
  8.1 2.4 %fusion.27 = f32[2048,1024]{1,0:T(8,128)S(1)} fusion(bf16[256,1024]{1,0:T(8,128)(2,1)} %param.7, s32[256]{0:T(256)S(1)} %bitcast.44, s32[256]{0:T(256)S(1)} %bitcast.42), kind=kOutput, calls=%fused_computation.41 | convolution fusion | flops 1077936128 | bytes 8914944 | tf_op jit(solution)/shard_map/dot_general | solution.py:40
  10.5 1.3 fusion.14
  11.9 2.6 %add_convert_fusion = bf16[2048,1024]{1,0:T(8,128)(2,1)S(1)} fusion(f32[2048,1024]{1,0:T(8,128)S(1)} %fusion.27, f32[2048,1024]{1,0:T(8,128)S(1)} %fusion.14, s32[256]{0:T(256)S(1)} %broadcast_add_fusion, bf16[256,1024]{1,0:T(8,128)(2,1)} %param.8, f32[256]{0:T(256)S(1)} %bitcast.46), kind=kOutput, calls=%fused_computation.2 | convolution fusion | flops 1081344000 | bytes 21497856 | tf_op jit(solution)/shard_map/dot_general | solution.py:44
  14.5 55.5 %all_to_all.20 = bf16[32,2,32,1024]{3,2,1,0:T(8,128)(2,1)S(1)} all-to-all(bf16[32,2,32,1024]{3,2,1,0:T(8,128)(2,1)S(1)} %bitcast.31), channel_id=1, replica_groups=mesh['dp'=16,'expert'=16] {'expert'}, dimensions={0} | all-to-all | bytes 8388608 | tf_op jit(solution)/shard_map/all_to_all | solution.py:46
  70.0 0.8 copy.28
  70.8 0.8 fusion.41
  71.6 1.5 slice-done.1
  73.1 1.8 %fusion.17 = bf16[2,512,768]{2,1,0:T(8,128)(2,1)S(1)} fusion(bf16[2,512,1024]{2,1,0:T(8,128)(2,1)S(1)} %bitcast.36, bf16[2,1024,1536]{2,1,0:T(8,128)(2,1)S(1)} %bitcast.49), kind=kOutput, calls=%fused_computation.34 | convolution fusion | flops 1611399168 | bytes 6815744 | tf_op jit(solution)/shard_map/ksd,kdf->ksf/dot_general | solution.py:13
  74.9 1.8 %fusion.20 = bf16[2,512,768]{2,1,0:T(8,128)(2,1)S(1)} fusion(bf16[2,512,1024]{2,1,0:T(8,128)(2,1)S(1)} %bitcast.37, bf16[2,1024,1536]{2,1,0:T(8,128)(2,1)S(1)} %bitcast.49), kind=kOutput, calls=%fused_computation.35 | convolution fusion | flops 1611399168 | bytes 6815744 | tf_op jit(solution)/shard_map/ksd,kdf->ksf/dot_general | solution.py:10
  76.7 2.1 %convolution_convert_fusion.1 = bf16[2,768,1024]{2,1,0:T(8,128)(2,1)S(1)} fusion(bf16[2,512,1024]{2,1,0:T(8,128)(2,1)S(1)} %bitcast.39, bf16[2,512,768]{2,1,0:T(8,128)(2,1)S(1)} %fusion.17, bf16[2,512,768]{2,1,0:T(8,128)(2,1)S(1)} %fusion.20), kind=kOutput, calls=%fused_computation.24 | convolution fusion | flops 1618477056 | bytes 8388608 | tf_op jit(solution)/shard_map/ksf,ksd->kfd/dot_general | solution.py:54
  78.8 0.1 fusion.42
  78.9 0.2 slice.74
  79.2 2.9 %fusion.2 = (bf16[2,512,768]{2,1,0:T(8,128)(2,1)S(1)}, bf16[2,512,768]{2,1,0:T(8,128)(2,1)S(1)}) fusion(bf16[2,512,768]{2,1,0:T(8,128)(2,1)S(1)} %fusion.17, bf16[2,512,768]{2,1,0:T(8,128)(2,1)S(1)} %fusion.20, bf16[2,512,1024]{2,1,0:T(8,128)(2,1)S(1)} %bitcast.40, bf16[2,768,1024]{2,1,0:T(8,128)(2,1)S(1)} %copy-done), kind=kOutput, calls=%fused_computation.12 | convolution fusion | flops 1622409216 | bytes 11534336 | tf_op jit(solution)/shard_map/ksd,kfd->ksf/dot_general | solution.py:51
  82.1 3.8 %convolution_convert_fusion = bf16[2,1024,1536]{2,1,0:T(8,128)(2,1)S(1)} fusion(bf16[2,512,1024]{2,1,0:T(8,128)(2,1)S(1)} %bitcast.38, bf16[2,512,768]{2,1,0:T(8,128)(2,1)S(1)} %get-tuple-element.6, bf16[2,512,768]{2,1,0:T(8,128)(2,1)S(1)} %get-tuple-element.5), kind=kOutput, calls=%fused_computation.3 | convolution fusion | flops 3230662656 | bytes 11534336 | tf_op jit(solution)/shard_map/ksd,ksf->kdf/dot_general | solution.py:60
  85.9 4.0 %maximum_maximum_fusion = bf16[2,16,96,1536]{3,2,1,0:T(8,128)(2,1)} fusion(bf16[2,16,16,512]{3,2,1,0:T(8,128)(2,1)S(1)} %get-tuple-element.10, bf16[2,16,16,512]{3,2,1,0:T(8,128)(2,1)S(1)} %get-tuple-element.9, bf16[2,16,32,1024]{3,2,1,0:T(8,128)(2,1)S(1)} %slice.74, bf16[2,16,64,1536]{3,2,1,0:T(8,128)(2,1)S(1)} %bitcast.33), kind=kLoop, calls=%fused_computation.1 | loop fusion | flops 37748736 | bytes 18874368 | tf_op jit(solution)/shard_map/concatenate | solution.py:76
  89.9 7.2 %fusion.16 = bf16[2,512,1024]{2,1,0:T(8,128)(2,1)S(1)} fusion(bf16[2,1024,1536]{2,1,0:T(8,128)(2,1)} %param.12, bf16[2,512,768]{2,1,0:T(8,128)(2,1)} %copy-done.5, bf16[2,512,768]{2,1,0:T(8,128)(2,1)} %copy-done.4), kind=kOutput, calls=%fused_computation.33 | convolution fusion | flops 3228565504 | bytes 11534336 | tf_op jit(solution)/shard_map/ksf,kdf->ksd/dot_general | solution.py:61
  97.1 3.5 %copy.20 = bf16[2,512,1024]{2,0,1:T(2,128)(2,1)} copy(bf16[2,512,1024]{2,1,0:T(8,128)(2,1)S(1)} %fusion.16) | data formatting | bytes 4194304 | tf_op jit(solution)/shard_map/convert_element_type | solution.py:63
  100.6 6.2 %all-to-all-start.1 = ((bf16[2,512,1024]{2,0,1:T(2,128)(2,1)}), bf16[2,512,1024]{2,0,1:T(2,128)(2,1)S(1)}, u32[]{:S(2)}, u32[]{:S(2)}) async-start(bf16[2,512,1024]{2,0,1:T(2,128)(2,1)} %copy.20), calls=%async_computation.1 | async-start | bytes 4194304 | tf_op jit(solution)/shard_map/all_to_all | solution.py:64
  106.8 0.1 copy.22
  107.0 0.1 reshape.83
  107.1 25.2 %all-to-all-done.1 = bf16[2,512,1024]{2,0,1:T(2,128)(2,1)S(1)} async-done(((bf16[2,512,1024]{2,0,1:T(2,128)(2,1)}), bf16[2,512,1024]{2,0,1:T(2,128)(2,1)S(1)}, u32[]{:S(2)}, u32[]{:S(2)}) %all-to-all-start.1) | async-done | bytes 2097184 | tf_op jit(solution)/shard_map/all_to_all | solution.py:64
  132.4 2.0 %copy.21 = bf16[2,16,32,1024]{3,2,0,1:T(8,128)(2,1)} copy(bf16[2,16,32,1024]{3,0,2,1:T(2,128)(2,1)S(1)} %bitcast.32) | data formatting | bytes 4194304 | tf_op jit(solution)/shard_map/all_to_all | solution.py:64
  134.4 5.5 %gather_fusion = bf16[512,1024]{1,0:T(8,128)(2,1)} fusion(bf16[1024,1024]{1,0:T(8,128)(2,1)} %bitcast.27, s32[1024]{0:T(1024)S(1)} %pad_clamp_fusion), kind=kCustom, calls=%fused_computation | custom fusion | bytes 2099200 | tf_op jit(solution)/shard_map/gather | solution.py:65
  139.9 2.3 %reshape.84 = bf16[256,2,1024]{2,1,0:T(2,128)(2,1)} reshape(bf16[512,1024]{1,0:T(8,128)(2,1)} %gather_fusion) | data formatting | bytes 2097152 | tf_op jit(solution)/shard_map/reshape | solution.py:65
  142.2 4.6 %reduce_sum.12 = bf16[256,1024]{1,0:T(8,128)(2,1)} reduce(bf16[256,2,1024]{2,1,0:T(2,128)(2,1)} %reshape.84, bf16[]{:T(256)} %constant.4.clone.1), dimensions={1}, to_apply=%region_0.0 | reduce | flops 262144 | bytes 1572866 | tf_op jit(solution)/shard_map/reduce_sum | solution.py:66
  146.8 17.8 %reduce-scatter.2.cloned.1.call-done = bf16[2,96,1536]{2,1,0:T(8,128)(2,1)} async-done(((bf16[2,1536,1536]{2,1,0:T(8,128)(2,1)}), bf16[2,96,1536]{2,1,0:T(8,128)(2,1)}) %reduce-scatter.2.cloned.1.call-update) | async-done | bytes 589840 | tf_op jit(solution)/shard_map/reduce_scatter | solution.py:77
  164.6 0.8 fusion.43
  165.3 0.9 slice.78
  166.3 0.8 maximum_convert_fusion
  167.0 2.0 %slice_convert_fusion = f32[2,64,1536]{2,1,0:T(8,128)} fusion(bf16[2,96,1536]{2,1,0:T(8,128)(2,1)} %reduce-scatter.2.cloned.1.call-done), kind=kLoop, calls=%fused_computation.48 | loop fusion | flops 196608 | bytes 1179648 | tf_op jit(solution)/shard_map/convert_element_type | solution.py:78
  (23 shorter events, 0.1 us)
Async XLA Ops:
  7.2 72.0 %copy-start = (bf16[2,768,1024]{2,1,0:T(8,128)(2,1)S(1)}, bf16[2,768,1024]{2,1,0:T(8,128)(2,1)}, u32[]{:S(2)}) copy-start(bf16[2,768,1024]{2,1,0:T(8,128)(2,1)} %param.13) | copy-start | bytes 9437188
  7.2 157.4 %reduce-scatter.2.cloned.1.call-start = ((), (), s32[]{:S(2)}) async-start(), calls=%async_computation.3 | async-start | bytes 10027008 | tf_op jit(solution)/shard_map/reduce_scatter | solution.py:77
  8.1 2.4 %copy-start.3 = (f32[256,2]{0,1:T(2,128)S(1)}, f32[256,2]{0,1:T(2,128)}, u32[]{:S(2)}) copy-start(f32[256,2]{0,1:T(2,128)} %param.9) | copy-start | bytes 6148
  8.1 2.4 %copy-start.2 = (bf16[256,1024]{1,0:T(8,128)(2,1)S(1)}, bf16[256,1024]{1,0:T(8,128)(2,1)}, u32[]{:S(2)}) copy-start(bf16[256,1024]{1,0:T(8,128)(2,1)} %param.8) | copy-start | bytes 1572868
  70.0 1.6 slice-start
  70.8 2.4 %slice-start.1 = ((s8[6291456]{0:T(1024)(128)(4,1)}), s8[4194304]{0:T(1024)(128)(4,1)S(1)}, s32[]{:S(2)}) async-start(s8[6291456]{0:T(1024)(128)(4,1)} %bitcast.48), calls=%async_computation.5 | async-start | bytes 8388608
  82.1 3.8 %copy-start.4 = (bf16[2,512,768]{2,1,0:T(8,128)(2,1)}, bf16[2,512,768]{2,1,0:T(8,128)(2,1)S(1)}, u32[]{:S(2)}) copy-start(bf16[2,512,768]{2,1,0:T(8,128)(2,1)S(1)} %get-tuple-element.5) | copy-start | bytes 4718596
  82.1 3.8 %copy-start.5 = (bf16[2,512,768]{2,1,0:T(8,128)(2,1)}, bf16[2,512,768]{2,1,0:T(8,128)(2,1)S(1)}, u32[]{:S(2)}) copy-start(bf16[2,512,768]{2,1,0:T(8,128)(2,1)S(1)} %get-tuple-element.6) | copy-start | bytes 4718596
  100.6 31.8 %all-to-all-start.1 = ((bf16[2,512,1024]{2,0,1:T(2,128)(2,1)}), bf16[2,512,1024]{2,0,1:T(2,128)(2,1)S(1)}, u32[]{:S(2)}, u32[]{:S(2)}) async-start(bf16[2,512,1024]{2,0,1:T(2,128)(2,1)} %copy.20), calls=%async_computation.1 | async-start | bytes 4194304 | tf_op jit(solution)/shard_map/all_to_all | solution.py:64
  134.4 34.6 %copy-start.1 = (bf16[2,768,1024]{2,1,0:T(8,128)(2,1)S(1)}, bf16[2,768,1024]{2,1,0:T(8,128)(2,1)}, u32[]{:S(2)}) copy-start(bf16[2,768,1024]{2,1,0:T(8,128)(2,1)} %param.13) | copy-start | bytes 9437188
Sparse Core Ops, SparseCore 0:
  90.1 74.4 reduce-scatter.1

commit v10 on v7

--- a/solution.py
+++ b/solution.py
@@ -1,6 +1,10 @@
+import functools
+
 import jax
 import jax.numpy as jnp
 from jax import lax
+from jax.experimental import pallas as pl
+from jax.experimental.pallas import tpu as pltpu
 from jax.sharding import PartitionSpec as P
 
 TOP = 2
@@ -17,6 +21,43 @@
     activated = gate * sigmoid_gate
     hidden = (activated * upper).astype(jnp.bfloat16)
     return (gate, upper, sigmoid_gate, activated, hidden)
+
+
+def pack_kernel(main, spare, in_ref, down_ref, out_ref, sems):
+    experts, _, in_rows, in_cols = in_ref.shape
+    down_rows, down_cols = down_ref.shape[2], down_ref.shape[3]
+    rest = down_rows - main
+    copies = []
+    for k in range(experts):
+        pairs = [
+            (in_ref.at[k], out_ref.at[k, :, pl.ds(0, in_rows), :]),
+            (down_ref.at[k, :, pl.ds(0, main), :], out_ref.at[k, :, pl.ds(in_rows, main), pl.ds(0, down_cols)]),
+        ]
+        for i, c in enumerate(range(0, down_cols, spare)):
+            pairs.append((
+                down_ref.at[k, :, pl.ds(main, rest), pl.ds(c, spare)],
+                out_ref.at[k, :, pl.ds(in_rows + i * rest, rest), pl.ds(down_cols, spare)],
+            ))
+        for src, dst in pairs:
+            copy = pltpu.make_async_copy(src, dst, sems.at[len(copies)])
+            copy.start()
+            copies.append(copy)
+    for copy in copies:
+        copy.wait()
+
+
+def pack(part_in, part_down, main, spare):
+    experts, n_dp, in_rows, in_cols = part_in.shape
+    n_copies = experts * (2 + part_down.shape[3] // spare)
+    nbytes = 2 * (part_in.size + part_down.size) * part_in.dtype.itemsize
+    return pl.pallas_call(
+        functools.partial(pack_kernel, main, spare),
+        out_shape=jax.ShapeDtypeStruct((experts, n_dp, in_rows + main, in_cols), part_in.dtype),
+        in_specs=[pl.BlockSpec(memory_space=pl.ANY)] * 2,
+        out_specs=pl.BlockSpec(memory_space=pl.ANY),
+        scratch_shapes=[pltpu.SemaphoreType.DMA((n_copies,))],
+        cost_estimate=pl.CostEstimate(flops=0, bytes_accessed=nbytes, transcendentals=0),
+    )(part_in, part_down)
 
 
 def per_device(tokens, cotangent, route_logits, expert_ids, slot_pos, w_in, w_down):
@@ -71,9 +112,7 @@
     spare = in_cols - down_cols
     part_in = term_in.astype(jnp.bfloat16).reshape(local_experts, n_dp, in_rows // n_dp, in_cols)
     part_down = term_down.astype(jnp.bfloat16).reshape(local_experts, n_dp, rows_q, down_cols)
-    pieces = [part_down[:, :, main:, c : c + spare] for c in range(0, down_cols, spare)]
-    packed = jnp.concatenate([part_down[:, :, :main], jnp.concatenate(pieces, axis=2)], axis=3)
-    parts = jnp.concatenate([part_in, packed], axis=2).reshape(local_experts, -1, in_cols)
+    parts = pack(part_in, part_down, main, spare).reshape(local_experts, -1, in_cols)
     summed = lax.psum_scatter(parts, "dp", scatter_dimension=1, tiled=True)
     grad_in = summed[:, : in_rows // n_dp].astype(jnp.float32)
     got_down = summed[:, in_rows // n_dp :]

time: 175 us -> 461 us (2.63)
  Pallas kernels: 0 us -> 287 us
    pallas_call x0 -> x1, Pallas kernels: none -> 287 us  [pack(): pl.pallas_call(functools.partial(pack_kernel, main, spare), out_shape=jax...]
  transfers between devices with their start and end apart: 2 -> 2, of which waited for: 2 -> 2; matrix products, arithmetic and copies ran while one was open for 14% -> 5% of each run, Pallas kernels for 0% -> 0%
where the time goes in v10:
time: 461 us
  Pallas kernels  287 us (62%)
  blocking collectives  55.5 us (12%)
  waiting for transfers between devices  43.2 us (9%)
  matrix products  29.2 us (6%)
  local copies, waits for them, and re-layouts  17.3 us (4%)
  between operations  14.2 us (3%)
  other arithmetic  8.2 us (2%)
  starting transfers between devices  6.27 us (1%)
    pallas_call x1, Pallas kernels, pack(): pl.pallas_call(functools.partial(pack_kernel, main, spare), out_shape=jax...  287 us
    all_to_all x1, blocking collectives, per_device(): lax.all_to_all(send, 'expert', split_axis=0, concat_axis=0, tiled=True)  55.5 us
    all_to_all x1, waiting for transfers between devices, per_device(): lax.all_to_all(returned, 'expert', split_axis=1, concat_axis=0, tiled=True)  25.2 us
    reduce_scatter x1, waiting for transfers between devices, per_device(): summed = lax.psum_scatter(parts, 'dp', scatter_dimension=1, tiled=True)  17.9 us
  transfers between devices with their start and end apart: 2, of which 2 were waited for; matrix products, arithmetic and copies ran while one was open for 5% of the time, Pallas kernels for 0%

profile of v10, /device:TPU:4, one launch (start us, length us, event | category | flops | bytes accessed | tf_op | source)
XLA Modules:
  0.0 460.9 jit_solution(8138557297145818245)
XLA Ops:
  7.2 0.0 copy-start
  7.2 0.0 reduce-scatter.2.cloned.1.call-start
  7.2 0.9 multiply_add_fusion
  8.1 2.4 fusion.13
  10.5 1.3 fusion.7
  11.9 2.6 add_convert_fusion
  14.5 55.5 %all_to_all.20 = bf16[32,2,32,1024]{3,2,1,0:T(8,128)(2,1)S(1)} all-to-all(bf16[32,2,32,1024]{3,2,1,0:T(8,128)(2,1)S(1)} %bitcast.31), channel_id=1, replica_groups=mesh['dp'=16,'expert'=16] {'expert'}, dimensions={0} | all-to-all | bytes 8388608 | tf_op jit(solution)/shard_map/all_to_all | solution.py:87
  70.0 0.8 copy.28
  70.8 0.8 fusion.28
  71.6 1.8 fusion.31
  73.5 0.4 slice-done.1
  73.9 1.8 fusion.3
  75.7 3.0 multiply_convert_fusion.2
  78.7 3.7 convolution_convert_fusion.1
  82.4 5.4 %convolution_convert_fusion = bf16[2,1024,1536]{2,1,0:T(8,128)(2,1)} fusion(bf16[2,512,1024]{2,1,0:T(8,128)(2,1)S(1)} %bitcast.37, bf16[2,512,768]{2,1,0:T(8,128)(2,1)S(1)} %get-tuple-element.6, bf16[2,512,768]{2,1,0:T(8,128)(2,1)S(1)} %get-tuple-element.5), kind=kOutput, calls=%fused_computation.2 | convolution fusion | flops 3230662656 | bytes 11534336 | tf_op jit(solution)/shard_map/ksd,ksf->kdf/dot_general | solution.py:101
  87.8 287.0 %shard_map.94 = bf16[2,16,96,1536]{3,2,1,0:T(8,128)(2,1)} custom-call(bf16[2,16,64,1536]{3,2,1,0:T(8,128)(2,1)} %bitcast.33, bf16[2,16,48,1024]{3,2,1,0:T(8,128)(2,1)} %bitcast.34), custom_call_target="tpu_custom_call" | custom-call | bytes 18874368 | tf_op jit(solution)/shard_map/pallas_call | solution.py:53
  374.8 0.0 reduce-scatter.2.cloned.1.call-update
  374.8 7.2 %fusion.9 = bf16[2,512,1024]{2,1,0:T(8,128)(2,1)S(1)} fusion(bf16[2,1024,1536]{2,1,0:T(8,128)(2,1)} %param.12, bf16[2,512,768]{2,1,0:T(8,128)(2,1)} %copy-done.5, bf16[2,512,768]{2,1,0:T(8,128)(2,1)} %copy-done.4), kind=kOutput, calls=%fused_computation.23 | convolution fusion | flops 3228565504 | bytes 11534336 | tf_op jit(solution)/shard_map/ksf,kdf->ksd/dot_general | solution.py:102
  382.0 3.5 copy.20
  385.5 6.2 %all-to-all-start.1 = ((bf16[2,512,1024]{2,0,1:T(2,128)(2,1)}), bf16[2,512,1024]{2,0,1:T(2,128)(2,1)S(1)}, u32[]{:S(2)}, u32[]{:S(2)}) async-start(bf16[2,512,1024]{2,0,1:T(2,128)(2,1)} %copy.20), calls=%async_computation.1 | async-start | bytes 4194304 | tf_op jit(solution)/shard_map/all_to_all | solution.py:105
  391.7 0.1 copy.22
  391.9 0.1 reshape.83
  392.1 25.2 %all-to-all-done.1 = bf16[2,512,1024]{2,0,1:T(2,128)(2,1)S(1)} async-done(((bf16[2,512,1024]{2,0,1:T(2,128)(2,1)}), bf16[2,512,1024]{2,0,1:T(2,128)(2,1)S(1)}, u32[]{:S(2)}, u32[]{:S(2)}) %all-to-all-start.1) | async-done | bytes 2097184 | tf_op jit(solution)/shard_map/all_to_all | solution.py:105
  417.3 2.0 copy.21
  419.3 5.5 %gather_fusion = bf16[512,1024]{1,0:T(8,128)(2,1)} fusion(bf16[1024,1024]{1,0:T(8,128)(2,1)} %bitcast.27, s32[1024]{0:T(1024)S(1)} %pad_clamp_fusion), kind=kCustom, calls=%fused_computation | custom fusion | bytes 2099200 | tf_op jit(solution)/shard_map/gather | solution.py:106
  424.8 2.3 reshape.84
  427.1 4.6 reduce_sum.12
  431.7 17.9 %reduce-scatter.2.cloned.1.call-done = bf16[2,96,1536]{2,1,0:T(8,128)(2,1)} async-done(((bf16[2,1536,1536]{2,1,0:T(8,128)(2,1)}), bf16[2,96,1536]{2,1,0:T(8,128)(2,1)}) %reduce-scatter.2.cloned.1.call-update) | async-done | bytes 589840 | tf_op jit(solution)/shard_map/reduce_scatter | solution.py:116
  449.6 0.8 fusion.29
  450.4 0.9 slice.63
  451.3 0.8 maximum_convert_fusion
  452.1 2.0 slice_convert_fusion
  (21 shorter events, 0.1 us)
Async XLA Ops:
  7.2 64.4 %copy-start = (bf16[2,768,1024]{2,1,0:T(8,128)(2,1)S(1)}, bf16[2,768,1024]{2,1,0:T(8,128)(2,1)}, u32[]{:S(2)}) copy-start(bf16[2,768,1024]{2,1,0:T(8,128)(2,1)} %param.13) | copy-start | bytes 9437188
  7.2 442.4 %reduce-scatter.2.cloned.1.call-start = ((), (), s32[]{:S(2)}) async-start(), calls=%async_computation.3 | async-start | bytes 10027008 | tf_op jit(solution)/shard_map/reduce_scatter | solution.py:116
  8.1 2.4 copy-start.3
  8.1 2.4 copy-start.2
  70.8 2.7 slice-start
  71.6 2.3 slice-start.1
  78.6 3.7 copy-start.4
  78.7 3.7 copy-start.5
  385.5 31.8 %all-to-all-start.1 = ((bf16[2,512,1024]{2,0,1:T(2,128)(2,1)}), bf16[2,512,1024]{2,0,1:T(2,128)(2,1)S(1)}, u32[]{:S(2)}, u32[]{:S(2)}) async-start(bf16[2,512,1024]{2,0,1:T(2,128)(2,1)} %copy.20), calls=%async_computation.1 | async-start | bytes 4194304 | tf_op jit(solution)/shard_map/all_to_all | solution.py:105
  419.3 34.7 %copy-start.1 = (bf16[2,768,1024]{2,1,0:T(8,128)(2,1)S(1)}, bf16[2,768,1024]{2,1,0:T(8,128)(2,1)}, u32[]{:S(2)}) copy-start(bf16[2,768,1024]{2,1,0:T(8,128)(2,1)} %param.13) | copy-start | bytes 9437188
Sparse Core Ops, SparseCore 0:
  375.0 74.5 reduce-scatter.1

commit v11 on v7

--- a/solution.py
+++ b/solution.py
@@ -37,12 +37,12 @@
     for k in range(TOP):
         picks.append((buffer_row == target[None, :, k]).astype(jnp.bfloat16))
     token_picks = picks[0] + picks[1]
-    send = jnp.dot(token_picks, tokens, preferred_element_type=jnp.float32)
+    send = jnp.dot(token_picks, tokens, preferred_element_type=jnp.bfloat16)
     for k in range(TOP):
         scaled = (combine[k][:, None] * cotangent_wide).astype(jnp.bfloat16)
         shifted = (buffer_row == target[None, :, k] + capacity).astype(jnp.bfloat16)
-        send = send + jnp.dot(shifted, scaled, preferred_element_type=jnp.float32)
-    send = send.astype(jnp.bfloat16).reshape(experts_all, 2, capacity, width)
+        send = send + jnp.dot(shifted, scaled, preferred_element_type=jnp.bfloat16)
+    send = send.reshape(experts_all, 2, capacity, width)
     got = lax.all_to_all(send, "expert", split_axis=0, concat_axis=0, tiled=True)
     got = got.reshape(n_expert, local_experts, 2, capacity, width)
     got = jnp.transpose(got, (2, 1, 0, 3, 4)).reshape(2, local_experts, n_expert * capacity, width)

time: 175 us -> 178 us (1.017)
  local copies, waits for them, and re-layouts: 17.4 us -> 19.6 us
    unnamed x16, local copies, waits for them, and re-layouts: 0.48 us -> 2.93 us
where the time goes in v11:
time: 178 us; the launch traced here: 177 us
  blocking collectives  55.5 us (31%)
  waiting for transfers between devices  43 us (24%)
  matrix products  25.7 us (14%)
  local copies, waits for them, and re-layouts  19.6 us (11%)
  between operations  14.2 us (8%)
  other arithmetic  13 us (7%)
  starting transfers between devices  6.29 us (4%)
    all_to_all x1, blocking collectives, per_device(): lax.all_to_all(send, 'expert', split_axis=0, concat_axis=0, tiled=True)  55.5 us
    all_to_all x1, waiting for transfers between devices, per_device(): lax.all_to_all(returned, 'expert', split_axis=1, concat_axis=0, tiled=True)  25.2 us
    reduce_scatter x1, waiting for transfers between devices, per_device(): summed = lax.psum_scatter(parts, 'dp', scatter_dimension=1, tiled=True)  17.8 us
    dot_general x1, matrix products, per_device(): jnp.einsum('ksf,kdf->ksd', grad_pair, w_in, preferred_element_type=jnp.fl...  7.19 us
    all_to_all x1, starting transfers between devices, per_device(): lax.all_to_all(returned, 'expert', split_axis=1, concat_axis=0, tiled=True)  6.26 us
    gather x1, local copies, waits for them, and re-layouts, per_device(): arrived.reshape(-1, width)[destination].reshape(token_count, TOP, width)  5.53 us
    reduce_sum x1, other arithmetic, per_device(): input_grad = jnp.sum(rows.astype(jnp.float32), axis=1).astype(jnp.bfloat16)  4.59 us
    concatenate x1, other arithmetic, per_device(): jnp.concatenate([part_in, packed], axis=2)  4.05 us
  transfers between devices with their start and end apart: 2, of which 2 were waited for; matrix products, arithmetic and copies ran while one was open for 14% of the time, Pallas kernels for 0%

profile of v11, /device:TPU:4, one launch (start us, length us, event | category | flops | bytes accessed | tf_op | source)
XLA Modules:
  0.0 177.3 jit_solution(11638036405770213298)
XLA Ops:
  7.2 0.9 broadcast_subtract_fusion
  8.1 0.8 multiply_add_fusion
  8.9 2.5 %fusion.7 = bf16[2048,1024]{1,0:T(8,128)(2,1)S(1)} fusion(s32[256]{0:T(256)S(1)} %broadcast_add_fusion.1, bf16[256,1024]{1,0:T(8,128)(2,1)} %param.8, f32[256]{0:T(256)S(1)} %bitcast.47), kind=kOutput, calls=%fused_computation.22 | convolution fusion | flops 1075052544 | bytes 4720640 | tf_op jit(solution)/shard_map/dot_general | solution.py:44
  11.4 1.3 fusion.8
  12.7 1.3 add_add_fusion
  14.1 55.5 %all_to_all.20 = bf16[32,2,32,1024]{3,2,1,0:T(8,128)(2,1)S(1)} all-to-all(bf16[32,2,32,1024]{3,2,1,0:T(8,128)(2,1)S(1)} %bitcast.29), channel_id=1, replica_groups=mesh['dp'=16,'expert'=16] {'expert'}, dimensions={0} | all-to-all | bytes 8388608 | tf_op jit(solution)/shard_map/all_to_all | solution.py:46
  69.6 0.5 copy.28
  70.1 0.6 fusion.28
  70.7 0.5 slice-done
  71.1 1.4 slice-done.1
  72.5 1.8 %fusion.3 = f32[2,512,768]{2,1,0:T(8,128)S(1)} fusion(bf16[2,512,1024]{2,1,0:T(8,128)(2,1)S(1)} %bitcast.36, bf16[2,1024,1536]{2,1,0:T(8,128)(2,1)S(1)} %bitcast.49), kind=kOutput, calls=%fused_computation.13 | convolution fusion | flops 1610612736 | bytes 8388608 | tf_op jit(solution)/shard_map/ksd,kdf->ksf/dot_general | solution.py:13
  74.3 1.9 %fusion.32 = f32[2,512,768]{2,1,0:T(8,128)S(1)} fusion(bf16[2,512,1024]{2,1,0:T(8,128)(2,1)S(1)} %bitcast.39, bf16[2,768,1024]{2,1,0:T(8,128)(2,1)S(1)} %copy-done), kind=kOutput, calls=%fused_computation.54 | convolution fusion | flops 1610612736 | bytes 8388608 | tf_op jit(solution)/shard_map/ksd,kfd->ksf/dot_general | solution.py:51
  76.2 3.9 %multiply_convert_fusion.2 = (bf16[2,512,768]{2,1,0:T(8,128)(2,1)S(1)}, bf16[2,512,768]{2,1,0:T(8,128)(2,1)}, f32[2,512,768]{2,1,0:T(8,128)S(1)}) fusion(f32[2,512,768]{2,1,0:T(8,128)S(1)} %fusion.32, f32[2,512,768]{2,1,0:T(8,128)S(1)} %fusion.3, bf16[2,512,1024]{2,1,0:T(8,128)(2,1)S(1)} %bitcast.37, bf16[2,1024,1536]{2,1,0:T(8,128)(2,1)S(1)} %bitcast.49), kind=kOutput, calls=%fused_computation.8 | convolution fusion | flops 1620836352 | bytes 17825792 | tf_op jit(solution)/shard_map/ksd,kdf->ksf/dot_general | solution.py:10
  80.1 2.1 %convolution_convert_fusion.1 = bf16[2,768,1024]{2,1,0:T(8,128)(2,1)S(1)} fusion(bf16[2,512,1024]{2,1,0:T(8,128)(2,1)S(1)} %bitcast.40, f32[2,512,768]{2,1,0:T(8,128)S(1)} %fusion.3, f32[2,512,768]{2,1,0:T(8,128)S(1)} %get-tuple-element.17), kind=kOutput, calls=%fused_computation.15 | convolution fusion | flops 1616904192 | bytes 11534336 | tf_op jit(solution)/shard_map/ksf,ksd->kfd/dot_general | solution.py:54
  82.3 0.2 slice.74
  82.5 1.1 copy-done.5
  83.6 3.7 %convolution_convert_fusion = bf16[2,1024,1536]{2,1,0:T(8,128)(2,1)S(1)} fusion(bf16[2,512,1024]{2,1,0:T(8,128)(2,1)S(1)} %bitcast.38, bf16[2,512,768]{2,1,0:T(8,128)(2,1)S(1)} %copy-done.5, bf16[2,512,768]{2,1,0:T(8,128)(2,1)S(1)} %get-tuple-element.5), kind=kOutput, calls=%fused_computation.2 | convolution fusion | flops 3230662656 | bytes 11534336 | tf_op jit(solution)/shard_map/ksd,ksf->kdf/dot_general | solution.py:60
  87.4 4.1 %maximum_maximum_fusion = bf16[2,16,96,1536]{3,2,1,0:T(8,128)(2,1)} fusion(bf16[2,16,16,512]{3,2,1,0:T(8,128)(2,1)S(1)} %get-tuple-element.10, bf16[2,16,16,512]{3,2,1,0:T(8,128)(2,1)S(1)} %get-tuple-element.9, bf16[2,16,32,1024]{3,2,1,0:T(8,128)(2,1)S(1)} %slice.74, bf16[2,16,64,1536]{3,2,1,0:T(8,128)(2,1)S(1)} %bitcast.33), kind=kLoop, calls=%fused_computation.1 | loop fusion | flops 37748736 | bytes 18874368 | tf_op jit(solution)/shard_map/concatenate | solution.py:76
  91.4 7.2 %fusion.10 = bf16[2,512,1024]{2,1,0:T(8,128)(2,1)S(1)} fusion(bf16[2,1024,1536]{2,1,0:T(8,128)(2,1)} %param.12, bf16[2,512,768]{2,1,0:T(8,128)(2,1)} %get-tuple-element.6, bf16[2,512,768]{2,1,0:T(8,128)(2,1)} %copy-done.4), kind=kOutput, calls=%fused_computation.25 | convolution fusion | flops 3228565504 | bytes 11534336 | tf_op jit(solution)/shard_map/ksf,kdf->ksd/dot_general | solution.py:61
  98.6 3.5 %copy.20 = bf16[2,512,1024]{2,0,1:T(2,128)(2,1)} copy(bf16[2,512,1024]{2,1,0:T(8,128)(2,1)S(1)} %fusion.10) | data formatting | bytes 4194304 | tf_op jit(solution)/shard_map/convert_element_type | solution.py:63
  102.1 6.3 %all-to-all-start.1 = ((bf16[2,512,1024]{2,0,1:T(2,128)(2,1)}), bf16[2,512,1024]{2,0,1:T(2,128)(2,1)S(1)}, u32[]{:S(2)}, u32[]{:S(2)}) async-start(bf16[2,512,1024]{2,0,1:T(2,128)(2,1)} %copy.20), calls=%async_computation.1 | async-start | bytes 4194304 | tf_op jit(solution)/shard_map/all_to_all | solution.py:64
  108.5 0.1 reshape.83
  108.7 25.2 %all-to-all-done.1 = bf16[2,512,1024]{2,0,1:T(2,128)(2,1)S(1)} async-done(((bf16[2,512,1024]{2,0,1:T(2,128)(2,1)}), bf16[2,512,1024]{2,0,1:T(2,128)(2,1)S(1)}, u32[]{:S(2)}, u32[]{:S(2)}) %all-to-all-start.1) | async-done | bytes 2097184 | tf_op jit(solution)/shard_map/all_to_all | solution.py:64
  133.9 2.0 %copy.21 = bf16[2,16,32,1024]{3,2,0,1:T(8,128)(2,1)} copy(bf16[2,16,32,1024]{3,0,2,1:T(2,128)(2,1)S(1)} %bitcast.32) | data formatting | bytes 4194304 | tf_op jit(solution)/shard_map/all_to_all | solution.py:64
  135.9 5.5 %gather_fusion = bf16[512,1024]{1,0:T(8,128)(2,1)} fusion(bf16[1024,1024]{1,0:T(8,128)(2,1)} %bitcast.27, s32[1024]{0:T(1024)S(1)} %pad_clamp_fusion), kind=kCustom, calls=%fused_computation | custom fusion | bytes 2099200 | tf_op jit(solution)/shard_map/gather | solution.py:65
  141.4 2.3 %reshape.84 = bf16[256,2,1024]{2,1,0:T(2,128)(2,1)} reshape(bf16[512,1024]{1,0:T(8,128)(2,1)} %gather_fusion) | data formatting | bytes 2097152 | tf_op jit(solution)/shard_map/reshape | solution.py:65
  143.7 4.6 %reduce_sum.12 = bf16[256,1024]{1,0:T(8,128)(2,1)} reduce(bf16[256,2,1024]{2,1,0:T(2,128)(2,1)} %reshape.84, bf16[]{:T(256)} %constant.4.clone.1), dimensions={1}, to_apply=%region_0.0 | reduce | flops 262144 | bytes 1572866 | tf_op jit(solution)/shard_map/reduce_sum | solution.py:66
  148.3 17.8 %reduce-scatter.2.cloned.1.call-done = bf16[2,96,1536]{2,1,0:T(8,128)(2,1)} async-done(((bf16[2,1536,1536]{2,1,0:T(8,128)(2,1)}), bf16[2,96,1536]{2,1,0:T(8,128)(2,1)}) %reduce-scatter.2.cloned.1.call-update) | async-done | bytes 589840 | tf_op jit(solution)/shard_map/reduce_scatter | solution.py:77
  166.1 0.8 fusion.30
  166.8 0.9 slice.78
  167.8 0.8 maximum_convert_fusion
  168.5 2.0 %slice_convert_fusion = f32[2,64,1536]{2,1,0:T(8,128)} fusion(bf16[2,96,1536]{2,1,0:T(8,128)(2,1)} %reduce-scatter.2.cloned.1.call-done), kind=kLoop, calls=%fused_computation.37 | loop fusion | flops 196608 | bytes 1179648 | tf_op jit(solution)/shard_map/convert_element_type | solution.py:78
  (23 shorter events, 0.4 us)
Async XLA Ops:
  7.2 67.2 %copy-start = (bf16[2,768,1024]{2,1,0:T(8,128)(2,1)S(1)}, bf16[2,768,1024]{2,1,0:T(8,128)(2,1)}, u32[]{:S(2)}) copy-start(bf16[2,768,1024]{2,1,0:T(8,128)(2,1)} %param.13) | copy-start | bytes 9437188
  7.2 158.9 %reduce-scatter.2.cloned.1.call-start = ((), (), s32[]{:S(2)}) async-start(), calls=%async_computation.3 | async-start | bytes 10027008 | tf_op jit(solution)/shard_map/reduce_scatter | solution.py:77
  8.9 2.5 %copy-start.2 = (bf16[256,1024]{1,0:T(8,128)(2,1)S(1)}, bf16[256,1024]{1,0:T(8,128)(2,1)}, u32[]{:S(2)}) copy-start(bf16[256,1024]{1,0:T(8,128)(2,1)} %param.8) | copy-start | bytes 1572868
  11.4 1.4 copy-start.3
  69.5 1.6 slice-start
  70.1 2.4 %slice-start.1 = ((s8[6291456]{0:T(1024)(128)(4,1)}), s8[4194304]{0:T(1024)(128)(4,1)S(1)}, s32[]{:S(2)}) async-start(s8[6291456]{0:T(1024)(128)(4,1)} %bitcast.48), calls=%async_computation.5 | async-start | bytes 8388608
  80.1 2.4 %copy-start.4 = (bf16[2,512,768]{2,1,0:T(8,128)(2,1)}, bf16[2,512,768]{2,1,0:T(8,128)(2,1)S(1)}, u32[]{:S(2)}) copy-start(bf16[2,512,768]{2,1,0:T(8,128)(2,1)S(1)} %get-tuple-element.5) | copy-start | bytes 4718596
  82.2 1.4 copy-start.5
  102.1 31.8 %all-to-all-start.1 = ((bf16[2,512,1024]{2,0,1:T(2,128)(2,1)}), bf16[2,512,1024]{2,0,1:T(2,128)(2,1)S(1)}, u32[]{:S(2)}, u32[]{:S(2)}) async-start(bf16[2,512,1024]{2,0,1:T(2,128)(2,1)} %copy.20), calls=%async_computation.1 | async-start | bytes 4194304 | tf_op jit(solution)/shard_map/all_to_all | solution.py:64
  135.9 34.6 %copy-start.1 = (bf16[2,768,1024]{2,1,0:T(8,128)(2,1)S(1)}, bf16[2,768,1024]{2,1,0:T(8,128)(2,1)}, u32[]{:S(2)}) copy-start(bf16[2,768,1024]{2,1,0:T(8,128)(2,1)} %param.13) | copy-start | bytes 9437188
Sparse Core Ops, SparseCore 0:
  91.6 74.4 reduce-scatter.1
